TPU v7x, 32 devices: a whole 2x2x4 slice. The times are simulated.
32 devices in a mesh: sub: 8 (over y, x, core), in: 4 (over z).
Axes of the slice: x: 2, y: 2, z: 4, core: 2. Of those that a mesh axis runs over, the one named last changes fastest.
Arguments:
- body_load: float32 [4, 32, 32, 1024], P(None, 'in', None, 'sub'), may hold values from -6 to 6
- materials: int32 [32, 32, 1024], P('in', None, 'sub'), may hold values from 0 to 7
- material_tables: float32 [8, 4, 4], replicated
- corner_index: int32 [256], P(('sub', 'in')), may hold values from 0 to 1023
- coarse_inverse: float32 [256, 256], P(('sub', 'in')), as said below
Outputs:
- interior_solution: float32 [4, 32, 32, 1024], P(None, 'in', None, 'sub')
- interface_sum: float32 [8, 4, 32, 32], P('sub', None, 'in')
Inputs may be any that keep to these rules, and one draw needn't show every extreme that they name: coarse_inverse is symmetric.
All inputs are finite; a program needn't handle non-finite values.
Results may differ from a plain program's by a relative error of at most 0.0003.
Values sent between devices are 32-bit elements; how exact they have to be, the bound alone decides.
No kernel may reach another device: no remote copies, remote signals or barrier semaphores. Data moves between devices by JAX's collectives and lax.ppermute only.
A program may use at most 64 MiB of HBM per device.

v0:
```python
import jax
import jax.numpy as jnp
from jax import lax
from jax.sharding import PartitionSpec as P

NMAT = 8
ITERS = 3


def extended(cells, sides, width):
    for axis, dim in sides:
        count = lax.axis_size(axis)
        ends = count - 1
        head = lax.slice_in_dim(cells, 0, width, axis=dim)
        tail = lax.slice_in_dim(cells, cells.shape[dim] - width, cells.shape[dim], axis=dim)
        cells = jnp.concatenate(
            [
                lax.ppermute(tail, axis, [(i, (i + 1) % count) for i in range(ends)]),
                cells,
                lax.ppermute(head, axis, [((i + 1) % count, i) for i in range(ends)]),
            ],
            axis=dim,
        )
    return cells


def passed_along(x, axis, by):
    length = lax.axis_size(axis)
    return lax.ppermute(x, axis, [(i, (i + by) % length) for i in range(length)])


def node_tables(material, tables):
    total = jnp.zeros((tables.shape[1], tables.shape[2]) + material.shape, jnp.float32)
    for material_kind in range(NMAT):
        chosen = (material == material_kind).astype(jnp.float32)
        total = total + chosen[None, None] * tables[material_kind][:, :, None, None, None]
    return total


def stencil(padded, center, gains):
    padded = jnp.pad(padded, ((0, 0), (0, 0), (1, 1), (1, 1)))
    beside = padded[:, 2:, 1:-1, 1:-1] + padded[:, :-2, 1:-1, 1:-1]
    beside = beside + padded[:, 1:-1, 2:, 1:-1] + padded[:, 1:-1, :-2, 1:-1]
    beside = beside + padded[:, 1:-1, 1:-1, 2:] + padded[:, 1:-1, 1:-1, :-2]
    coupled = jnp.sum(gains * center[None], axis=1)
    return 6.0 * center + coupled - beside


def two_products(residual, applied):
    return lax.psum((jnp.sum(residual * residual), jnp.sum(residual * applied)), "in")


def on_device(body_load, materials, material_tables, corner_index, coarse_inverse):
    gains_own = node_tables(materials, material_tables)

    def apply_operator(values):
        padded = extended(values, (("in", 1),), 1)
        return stencil(padded, values, gains_own)

    solution = jnp.zeros_like(body_load)
    residual = body_load
    applied = apply_operator(residual)
    norm_now, product = two_products(residual, applied)
    step_size = norm_now / product
    direction, applied_dir = (residual, applied)
    for repeat in range(ITERS):
        solution = solution + step_size * direction
        residual = residual - step_size * applied_dir
        if repeat + 1 < ITERS:
            applied = apply_operator(residual)
            norm_next, product = two_products(residual, applied)
            beta_ratio = norm_next / norm_now
            step_size = norm_next / (product - beta_ratio * norm_next / step_size)
            direction = residual + beta_ratio * direction
            applied_dir = applied + beta_ratio * applied_dir
            norm_now = norm_next
    right_face = residual[..., -1]
    left_face = residual[..., 0]
    from_next = passed_along(left_face, "sub", -1)
    summed = (right_face + from_next).reshape(-1)
    coarse_local = jnp.take(summed, corner_index)
    gathered = lax.all_gather(coarse_local, ("sub", "in"), axis=0, tiled=True)
    coarse_solution = jnp.dot(coarse_inverse, gathered, precision=lax.Precision.HIGHEST)
    corrected = summed.at[corner_index].add(coarse_solution)
    interface_sum = corrected.reshape((1,) + right_face.shape)
    return (solution, interface_sum)


def solution(mesh):
    return jax.shard_map(
        on_device,
        mesh=mesh,
        in_specs=(
            P(None, "in", None, "sub"),
            P("in", None, "sub"),
            P(),
            P(("sub", "in")),
            P(("sub", "in"), None),
        ),
        out_specs=(P(None, "in", None, "sub"), P("sub", None, "in", None)),
        check_vma=False,
    )
```

profile of v0, /device:TPU:0, one launch (start us, length us, event | category | flops | bytes accessed | tf_op | source)
XLA Modules:
  0.0 123.6 jit_solution(13328454466165316334)
XLA Ops:
  0.6 0.0 copy-start
  0.7 0.9 fusion.15
  1.6 1.3 %collective-permute-start = (f32[4,1,32,128]{3,2,1,0:T(8,128)S(1)}, f32[4,1,32,128]{3,2,1,0:T(8,128)S(1)}, u32[]{:S(2)}, u32[]{:S(2)}) collective-permute-start(f32[4,1,32,128]{3,2,1,0:T(8,128)S(1)} %get-tuple-element.38), channel_id=1, source_target_pairs={{1,0},{2,1},{3,2},{5,4},{6,5},{7,6},{9,8},{10,9},{11,10},{13,12},{... | collective-permute-start | bytes 196616 | tf_op jit(solution)/shard_map/ppermute | solution.py:20
  2.9 0.0 copy-start.10
  2.9 5.6 %collective-permute-start.1 = (f32[4,1,32,128]{3,2,1,0:T(8,128)S(1)}, f32[4,1,32,128]{3,2,1,0:T(8,128)S(1)}, u32[]{:S(2)}, u32[]{:S(2)}) collective-permute-start(f32[4,1,32,128]{3,2,1,0:T(8,128)S(1)} %get-tuple-element.37), channel_id=1, source_target_pairs={{0,1},{1,2},{2,3},{4,5},{5,6},{6,7},{8,9},{9,10},{10,11},{12,13},{... | collective-permute-start | bytes 196616 | tf_op jit(solution)/shard_map/ppermute | solution.py:18
  8.5 1.0 compare_convert_fusion.7
  9.5 0.0 copy-start.2
  9.6 1.2 slice_reduce_fusion.9
  10.8 0.0 copy-start.7
  10.8 1.4 %multiply_reduce_fusion.2 = f32[4,8,32,128]{3,2,1,0:T(8,128)S(1)} fusion(f32[4,8,32,128]{3,2,1,0:T(8,128)S(1)} %copy-done.1, f32[4,4]{1,0:T(4,128)S(1)} %get-tuple-element.20, f32[8,32,128]{2,1,0:T(8,128)S(1)} %get-tuple-element.45, f32[4,4]{1,0:T(4,128)S(1)} %get-tuple-element.21, f32[8,32,128]{2,1,0:T(8,128)S(1)} %get-tuple-element.46, ...), kind=kLoop, calls=%fused_computation.8 | loop fusion | flops 8781824 | bytes 2097664 | tf_op jit(solution)/shard_map/reduce_sum | solution.py:45
  12.2 0.5 compare_select_fusion
  12.7 0.0 collective-permute-done
  12.7 0.0 collective-permute-done.1
  12.7 0.5 select_maximum_fusion.4
  13.2 1.2 multiply_reduce_fusion.7
  14.4 11.5 %all-reduce.6 = (f32[]{:T(128)}, f32[]{:T(128)}) all-reduce(f32[]{:T(128)} %get-tuple-element.13, f32[]{:T(128)} %get-tuple-element.12), channel_id=1, replica_groups=mesh['sub'=8,'in'=4] {'in'}, use_global_device_ids=true, to_apply=%region_1.2 | all-reduce | flops 2 | bytes 16 | tf_op jit(solution)/shard_map/psum | solution.py:50
  27.3 0.1 multiply_subtract_fusion.2
  27.4 1.3 %collective-permute-start.2 = (f32[4,1,32,128]{3,2,1,0:T(8,128)S(1)}, f32[4,1,32,128]{3,2,1,0:T(8,128)S(1)}, u32[]{:S(2)}, u32[]{:S(2)}) collective-permute-start(f32[4,1,32,128]{3,2,1,0:T(8,128)S(1)} %get-tuple-element.36), channel_id=1, source_target_pairs={{1,0},{2,1},{3,2},{5,4},{6,5},{7,6},{9,8},{10,9},{11,10},{13,12},{... | collective-permute-start | bytes 196616 | tf_op jit(solution)/shard_map/ppermute | solution.py:20
  28.7 4.5 %collective-permute-start.3 = (f32[4,1,32,128]{3,2,1,0:T(8,128)S(1)}, f32[4,1,32,128]{3,2,1,0:T(8,128)S(1)}, u32[]{:S(2)}, u32[]{:S(2)}) collective-permute-start(f32[4,1,32,128]{3,2,1,0:T(8,128)S(1)} %get-tuple-element.35), channel_id=1, source_target_pairs={{0,1},{1,2},{2,3},{4,5},{5,6},{6,7},{8,9},{9,10},{10,11},{12,13},{... | collective-permute-start | bytes 196616 | tf_op jit(solution)/shard_map/ppermute | solution.py:18
  33.2 0.0 copy-done.2
  33.3 0.0 copy-done.3
  33.3 0.0 copy-done.4
  33.3 1.3 %multiply_reduce_fusion.1 = f32[4,8,32,128]{3,2,1,0:T(8,128)S(1)} fusion(f32[4,8,32,128]{3,2,1,0:T(8,128)S(1)} %multiply_subtract_fusion.2, f32[4,4]{1,0:T(4,128)S(1)} %get-tuple-element.20, f32[8,32,128]{2,1,0:T(8,128)S(1)} %get-tuple-element.45, f32[4,4]{1,0:T(4,128)S(1)} %get-tuple-element.21, f32[8,32,128]{2,1,0:T(8,128)S(1)} %get-tuple-element.46, ...), kind=kLoop, calls=%fused_computation.7 | loop fusion | flops 8781824 | bytes 2097664 | tf_op jit(solution)/shard_map/reduce_sum | solution.py:45
  34.7 0.0 collective-permute-done.2
  34.7 0.5 collective-permute-done.3
  35.1 0.5 select_maximum_fusion.2
  35.6 1.2 multiply_reduce_fusion.5
  36.8 11.4 %all-reduce.5 = (f32[]{:T(128)}, f32[]{:T(128)}) all-reduce(f32[]{:T(128)} %get-tuple-element.11, f32[]{:T(128)} %get-tuple-element.10), channel_id=1, replica_groups=mesh['sub'=8,'in'=4] {'in'}, use_global_device_ids=true, to_apply=%region_6.7 | all-reduce | flops 2 | bytes 16 | tf_op jit(solution)/shard_map/psum | solution.py:50
  52.6 0.2 multiply_subtract_fusion.1
  52.8 1.3 %collective-permute-start.4 = (f32[4,1,32,128]{3,2,1,0:T(8,128)S(1)}, f32[4,1,32,128]{3,2,1,0:T(8,128)S(1)}, u32[]{:S(2)}, u32[]{:S(2)}) collective-permute-start(f32[4,1,32,128]{3,2,1,0:T(8,128)S(1)} %get-tuple-element.34), channel_id=1, source_target_pairs={{1,0},{2,1},{3,2},{5,4},{6,5},{7,6},{9,8},{10,9},{11,10},{13,12},{... | collective-permute-start | bytes 196616 | tf_op jit(solution)/shard_map/ppermute | solution.py:20
  54.1 4.5 %collective-permute-start.5 = (f32[4,1,32,128]{3,2,1,0:T(8,128)S(1)}, f32[4,1,32,128]{3,2,1,0:T(8,128)S(1)}, u32[]{:S(2)}, u32[]{:S(2)}) collective-permute-start(f32[4,1,32,128]{3,2,1,0:T(8,128)S(1)} %get-tuple-element.33), channel_id=1, source_target_pairs={{0,1},{1,2},{2,3},{4,5},{5,6},{6,7},{8,9},{9,10},{10,11},{12,13},{... | collective-permute-start | bytes 196616 | tf_op jit(solution)/shard_map/ppermute | solution.py:18
  58.7 2.4 %multiply_reduce_fusion = f32[4,8,32,128]{3,2,1,0:T(8,128)S(1)} fusion(f32[4,8,32,128]{3,2,1,0:T(8,128)S(1)} %multiply_subtract_fusion.1, f32[4,4]{1,0:T(4,128)} %copy-done.7, f32[8,32,128]{2,1,0:T(8,128)S(1)} %get-tuple-element.45, f32[4,4]{1,0:T(4,128)} %copy-done.8, f32[8,32,128]{2,1,0:T(8,128)} %copy-done.2, f32[4,4]{1,0:T(4,128)S(1)} %get-tuple-element.15, ...), kind=kLoop, calls=%fused_computation.6 | loop fusion | flops 8781824 | bytes 2097664 | tf_op jit(solution)/shard_map/reduce_sum | solution.py:45
  61.0 0.0 collective-permute-done.4
  61.0 0.0 collective-permute-done.5
  61.1 0.5 select_maximum_fusion
  61.6 1.9 %multiply_reduce_fusion.3 = (f32[]{:T(128)}, f32[]{:T(128)}, f32[4,8,32,128]{3,2,1,0:T(8,128)}) fusion(f32[4,8,32,128]{3,2,1,0:T(8,128)S(1)} %multiply_subtract_fusion.1, f32[4,10,34,130]{3,2,1,0:T(8,128)S(1)} %select_maximum_fusion, f32[4,1,32,128]{3,2,1,0:T(8,128)S(1)} %collective-permute-done.5, f32[4,1,32,128]{3,2,1,0:T(8,128)S(1)} %collective-permute-done.4, ...), kind=kLoop, calls=%fused_computation.48 | loop fusion | flops 1835006 | bytes 3801096 | tf_op jit(solution)/shard_map/reduce_sum | solution.py:50
  63.5 10.9 %all-reduce.4 = (f32[]{:T(128)}, f32[]{:T(128)}) all-reduce(f32[]{:T(128)} %get-tuple-element.9, f32[]{:T(128)} %get-tuple-element.8), channel_id=1, replica_groups=mesh['sub'=8,'in'=4] {'in'}, use_global_device_ids=true, to_apply=%region_11.12 | all-reduce | flops 2 | bytes 16 | tf_op jit(solution)/shard_map/psum | solution.py:50
  78.3 2.2 %multiply_subtract_fusion = (f32[4,8,32,128]{3,2,1,0:T(8,128)S(1)}, f32[4,8,32,128]{3,2,1,0:T(8,128)}) fusion(f32[4,8,32,128]{3,2,1,0:T(8,128)S(1)} %multiply_subtract_fusion.1, f32[4,8,32,128]{3,2,1,0:T(8,128)} %get-tuple-element.28, f32[]{:T(128)S(6)} %div.25, f32[]{:T(128)S(6)} %div.27, f32[4,8,32,128]{3,2,1,0:T(8,128)S(1)} %get-tuple-element.29, ...), kind=kLoop, calls=%fused_computation.46 | loop fusion | flops 1966080 | bytes 4194324 | tf_op jit(solution)/shard_map/sub | solution.py:68
  80.6 0.5 slice_reduce_fusion
  81.1 0.1 collective-permute-start.6
  81.1 1.4 %collective-permute-done.6 = f32[4,8,32]{2,1,0:T(8,128)S(1)} collective-permute-done((f32[4,8,32]{2,1,0:T(8,128)S(1)}, f32[4,8,32]{2,1,0:T(8,128)S(1)}, u32[]{:S(2)}, u32[]{:S(2)}) %collective-permute-start.6) | collective-permute-done | bytes 4128 | tf_op jit(solution)/shard_map/ppermute | solution.py:29
  82.6 0.1 reshape.34
  82.6 0.6 gather_fusion
  83.3 0.1 fusion.9
  83.4 38.8 %all-reduce.3 = f32[256]{0:T(256)S(1)} all-reduce(f32[256]{0:T(256)S(1)} %fusion.9), channel_id=1, replica_groups=mesh['sub'=8,'in'=4] {'sub','in'}, use_global_device_ids=true, to_apply=%add.3 | all-reduce | flops 256 | bytes 2048
  122.2 0.1 convolution_bitcast_fusion
  122.3 0.6 scatter_fusion
  123.0 0.7 reshape.35
  (22 shorter events, 0.1 us)
Async XLA Ops:
  0.6 121.6 %copy-start = (f32[8,256]{1,0:T(8,128)S(1)}, f32[8,256]{1,0:T(8,128)}, u32[]{:S(2)}) copy-start(f32[8,256]{1,0:T(8,128)} %param.9) | copy-start | bytes 24580
  0.6 10.2 %copy-start.1 = (f32[4,8,32,128]{3,2,1,0:T(8,128)S(1)}, f32[4,8,32,128]{3,2,1,0:T(8,128)}, u32[]{:S(2)}) copy-start(f32[4,8,32,128]{3,2,1,0:T(8,128)} %param.5) | copy-start | bytes 1572868
  1.6 11.1 %collective-permute-start = (f32[4,1,32,128]{3,2,1,0:T(8,128)S(1)}, f32[4,1,32,128]{3,2,1,0:T(8,128)S(1)}, u32[]{:S(2)}, u32[]{:S(2)}) collective-permute-start(f32[4,1,32,128]{3,2,1,0:T(8,128)S(1)} %get-tuple-element.38), channel_id=1, source_target_pairs={{1,0},{2,1},{3,2},{5,4},{6,5},{7,6},{9,8},{10,9},{11,10},{13,12},{... | collective-permute-start | bytes 196616 | tf_op jit(solution)/shard_map/ppermute | solution.py:20
  2.9 9.3 %copy-start.10 = (s32[8]{0:T(128)S(1)}, s32[8]{0:T(128)}, u32[]{:S(2)}) copy-start(s32[8]{0:T(128)} %param.8) | copy-start | bytes 100
  2.9 9.8 %collective-permute-start.1 = (f32[4,1,32,128]{3,2,1,0:T(8,128)S(1)}, f32[4,1,32,128]{3,2,1,0:T(8,128)S(1)}, u32[]{:S(2)}, u32[]{:S(2)}) collective-permute-start(f32[4,1,32,128]{3,2,1,0:T(8,128)S(1)} %get-tuple-element.37), channel_id=1, source_target_pairs={{0,1},{1,2},{2,3},{4,5},{5,6},{6,7},{8,9},{9,10},{10,11},{12,13},{... | collective-permute-start | bytes 196616 | tf_op jit(solution)/shard_map/ppermute | solution.py:18
  9.5 23.7 %copy-start.2 = (f32[8,32,128]{2,1,0:T(8,128)}, f32[8,32,128]{2,1,0:T(8,128)S(1)}, u32[]{:S(2)}) copy-start(f32[8,32,128]{2,1,0:T(8,128)S(1)} %get-tuple-element.46) | copy-start | bytes 393220
  10.7 22.5 %copy-start.3 = (f32[4,4]{1,0:T(4,128)}, f32[4,4]{1,0:T(4,128)S(1)}, u32[]{:S(2)}) copy-start(f32[4,4]{1,0:T(4,128)S(1)} %get-tuple-element.16) | copy-start | bytes 196
  10.8 22.5 %copy-start.4 = (f32[4,4]{1,0:T(4,128)}, f32[4,4]{1,0:T(4,128)S(1)}, u32[]{:S(2)}) copy-start(f32[4,4]{1,0:T(4,128)S(1)} %get-tuple-element.17) | copy-start | bytes 196
  10.8 22.5 %copy-start.5 = (f32[4,4]{1,0:T(4,128)}, f32[4,4]{1,0:T(4,128)S(1)}, u32[]{:S(2)}) copy-start(f32[4,4]{1,0:T(4,128)S(1)} %get-tuple-element.18) | copy-start | bytes 196
  10.8 22.5 %copy-start.6 = (f32[4,4]{1,0:T(4,128)}, f32[4,4]{1,0:T(4,128)S(1)}, u32[]{:S(2)}) copy-start(f32[4,4]{1,0:T(4,128)S(1)} %get-tuple-element.19) | copy-start | bytes 196
  10.8 22.5 %copy-start.7 = (f32[4,4]{1,0:T(4,128)}, f32[4,4]{1,0:T(4,128)S(1)}, u32[]{:S(2)}) copy-start(f32[4,4]{1,0:T(4,128)S(1)} %get-tuple-element.20) | copy-start | bytes 196
  10.8 22.5 %copy-start.8 = (f32[4,4]{1,0:T(4,128)}, f32[4,4]{1,0:T(4,128)S(1)}, u32[]{:S(2)}) copy-start(f32[4,4]{1,0:T(4,128)S(1)} %get-tuple-element.21) | copy-start | bytes 196
  27.4 7.3 %collective-permute-start.2 = (f32[4,1,32,128]{3,2,1,0:T(8,128)S(1)}, f32[4,1,32,128]{3,2,1,0:T(8,128)S(1)}, u32[]{:S(2)}, u32[]{:S(2)}) collective-permute-start(f32[4,1,32,128]{3,2,1,0:T(8,128)S(1)} %get-tuple-element.36), channel_id=1, source_target_pairs={{1,0},{2,1},{3,2},{5,4},{6,5},{7,6},{9,8},{10,9},{11,10},{13,12},{... | collective-permute-start | bytes 196616 | tf_op jit(solution)/shard_map/ppermute | solution.py:20
  28.7 6.4 %collective-permute-start.3 = (f32[4,1,32,128]{3,2,1,0:T(8,128)S(1)}, f32[4,1,32,128]{3,2,1,0:T(8,128)S(1)}, u32[]{:S(2)}, u32[]{:S(2)}) collective-permute-start(f32[4,1,32,128]{3,2,1,0:T(8,128)S(1)} %get-tuple-element.35), channel_id=1, source_target_pairs={{0,1},{1,2},{2,3},{4,5},{5,6},{6,7},{8,9},{9,10},{10,11},{12,13},{... | collective-permute-start | bytes 196616 | tf_op jit(solution)/shard_map/ppermute | solution.py:18
  52.8 8.2 %collective-permute-start.4 = (f32[4,1,32,128]{3,2,1,0:T(8,128)S(1)}, f32[4,1,32,128]{3,2,1,0:T(8,128)S(1)}, u32[]{:S(2)}, u32[]{:S(2)}) collective-permute-start(f32[4,1,32,128]{3,2,1,0:T(8,128)S(1)} %get-tuple-element.34), channel_id=1, source_target_pairs={{1,0},{2,1},{3,2},{5,4},{6,5},{7,6},{9,8},{10,9},{11,10},{13,12},{... | collective-permute-start | bytes 196616 | tf_op jit(solution)/shard_map/ppermute | solution.py:20
  54.1 7.0 %collective-permute-start.5 = (f32[4,1,32,128]{3,2,1,0:T(8,128)S(1)}, f32[4,1,32,128]{3,2,1,0:T(8,128)S(1)}, u32[]{:S(2)}, u32[]{:S(2)}) collective-permute-start(f32[4,1,32,128]{3,2,1,0:T(8,128)S(1)} %get-tuple-element.33), channel_id=1, source_target_pairs={{0,1},{1,2},{2,3},{4,5},{5,6},{6,7},{8,9},{9,10},{10,11},{12,13},{... | collective-permute-start | bytes 196616 | tf_op jit(solution)/shard_map/ppermute | solution.py:18
  78.3 2.8 %copy-start.9 = (s32[8]{0:T(128)S(1)}, s32[8]{0:T(128)}, u32[]{:S(2)}) copy-start(s32[8]{0:T(128)} %compare_select_fusion) | copy-start | bytes 100
  80.5 2.7 %copy-start.11 = (s32[8]{0:T(128)S(1)}, s32[8]{0:T(128)}, u32[]{:S(2)}) copy-start(s32[8]{0:T(128)} %param.8) | copy-start | bytes 100
  81.1 1.5 %collective-permute-start.6 = (f32[4,8,32]{2,1,0:T(8,128)S(1)}, f32[4,8,32]{2,1,0:T(8,128)S(1)}, u32[]{:S(2)}, u32[]{:S(2)}) collective-permute-start(f32[4,8,32]{2,1,0:T(8,128)S(1)} %get-tuple-element.6), channel_id=1, source_target_pairs={{0,28},{4,0},{8,4},{12,8},{16,12},{20,16},{24,20},{28,24},{1,29},{... | collective-permute-start | bytes 12296 | tf_op jit(solution)/shard_map/ppermute | solution.py:29
where the time goes:
time: 124 us
  blocking collectives  72.7 us (59%)
  starting transfers between devices  18.6 us (15%)
  other arithmetic  15.7 us (13%)
  between operations  10.6 us (9%)
  local copies, waits for them, and re-layouts  4.09 us (3%)
  waiting for transfers between devices  1.88 us (2%)
    unnamed x1, blocking collectives  38.8 us
    psum x3, blocking collectives, two_products(): lax.psum((jnp.sum(residual * residual), jnp.sum(residual * applied)), 'in')  33.8 us
    ppermute x3, starting transfers between devices, extended(): lax.ppermute(tail, axis, [(i, (i + 1) % count) for i in range(ends)])  14.7 us
    reduce_sum x3, other arithmetic, stencil(): coupled = jnp.sum(gains * center[None], axis=1)  5.07 us
    reduce_sum x3, other arithmetic, two_products(): jnp.sum(residual * applied)  4.33 us
    ppermute x3, starting transfers between devices, extended(): lax.ppermute(head, axis, [((i + 1) % count, i) for i in range(ends)])  3.88 us
  transfers between devices with their start and end apart: 7, of which 2 were waited for; matrix products, arithmetic and copies ran while one was open for 6% of the time, Pallas kernels for 0%

commit v1 on v0

v1 whole, which is shorter than its diff:
```python
import functools

import jax
import jax.numpy as jnp
from jax import lax
from jax.experimental import pallas as pl
from jax.experimental.pallas import tpu as pltpu
from jax.sharding import PartitionSpec as P

ITERS = 3
LANES = 128
MAT_DEPTH = ITERS - 1
PAIRS = [(i, j) for i in range(ITERS) for j in range(i, ITERS + 1)]
GRAM_LANE = 64
VMEM = pl.BlockSpec(memory_space=pltpu.VMEM)
SMEM = pl.BlockSpec(memory_space=pltpu.SMEM)
HBM = pl.BlockSpec(memory_space=pl.ANY)


def spectrum(table, comp, kinds):
    rows = lax.broadcasted_iota(jnp.int32, table.shape, 0)
    live = lax.broadcasted_iota(jnp.int32, table.shape, 1) < kinds
    diagonal = live & (lax.rem(rows, comp + 1) == 0)
    table = jnp.where(live, table, 0.0)
    mean = jnp.sum(jnp.where(diagonal, table, 0.0)) / (comp * kinds)
    centred = jnp.where(diagonal, table - mean, table)
    size = jnp.abs(centred)
    widest = 0.0
    for c in range(comp):
        widest = jnp.maximum(widest, jnp.max(jnp.sum(size[comp * c : comp * (c + 1)], axis=0, keepdims=True)))
    scale = 6.0 + widest
    return mean, scale, centred


def pack_kernel(body, mats, a_out, b_out, kinds, sems):
    comp, depth = body.shape[0], body.shape[1]
    odd = lax.rem(lax.axis_index("in"), 2)
    copies = []
    for slot, (out, low) in enumerate(((a_out, odd), (b_out, 1 - odd))):
        first = (1 - low) * (depth - ITERS)
        for c in range(comp):
            copies.append(pltpu.make_async_copy(
                body.at[c, pl.ds(first, ITERS)], out.at[pl.ds(ITERS * c, ITERS)], sems.at[slot, c]))
        first = (1 - low) * (depth - MAT_DEPTH)
        copies.append(pltpu.make_async_copy(
            mats.at[pl.ds(first, MAT_DEPTH)], kinds.at[slot], sems.at[slot, comp]))
    for copy in copies:
        copy.start()
    for copy in copies:
        copy.wait()
    for slot, out in enumerate((a_out, b_out)):
        out[pl.ds(ITERS * comp, MAT_DEPTH)] = kinds[slot].astype(jnp.float32)


def basis_kernel(kinds, body, mats, halo_a, halo_b, table, corners, corners_before,
                 v1, v2, left_out, right_out, message,
                 v0, gains, packed):
    comp, depth, py, px = body.shape
    ext = depth + 2 * ITERS
    place = lax.axis_index("in")
    last = lax.axis_size("in") - 1
    odd = lax.rem(place, 2) == 1

    mean, scale, centred = spectrum(table[...], comp, kinds)
    inverse = 1.0 / scale
    scaled = centred * inverse

    lane = lax.broadcasted_iota(jnp.int32, (py, px), 1)
    row = lax.broadcasted_iota(jnp.int32, (py, px), 0)
    first_x, last_x = lane == 0, lane == px - 1
    first_y, last_y = row == 0, row == py - 1

    for c in range(comp):
        for t in range(ITERS):
            a = halo_a[ITERS * c + t]
            b = halo_b[ITERS * c + t]
            v0[c, t] = jnp.where(odd, a, b)
            v0[c, ITERS + depth + t] = jnp.where(odd, b, a)

    def own(z, carry):
        for c in range(comp):
            v0[c, ITERS + z] = body[c, z]
        return carry
    lax.fori_loop(0, depth, own, 0)

    def neighbours(source, c, at, value):
        total = source[c, at - 1] + source[c, at + 1]
        total += jnp.where(first_x, 0.0, pltpu.roll(value, 1, 1)) + jnp.where(last_x, 0.0, pltpu.roll(value, px - 1, 1))
        total += jnp.where(first_y, 0.0, pltpu.roll(value, 1, 0)) + jnp.where(last_y, 0.0, pltpu.roll(value, py - 1, 0))
        return total

    def applied(source, at, gain):
        values = [source[c, at] for c in range(comp)]
        results = []
        for c in range(comp):
            total = gain(c, 0) * values[0]
            for d in range(1, comp):
                total += gain(c, d) * values[d]
            results.append(total - inverse * neighbours(source, c, at, values[c]))
        return values, results

    def look_up(kind, at):
        for c in range(comp):
            for d in range(comp):
                line = jnp.broadcast_to(scaled[comp * c + d : comp * c + d + 1], (py, px))
                gains[comp * c + d, at] = jnp.take_along_axis(line, kind, axis=1)

    for t in range(MAT_DEPTH):
        a = halo_a[ITERS * comp + t]
        b = halo_b[ITERS * comp + t]
        look_up(jnp.where(odd, a, b).astype(jnp.int32), 1 + t)
        look_up(jnp.where(odd, b, a).astype(jnp.int32), ITERS + depth + t)

    def own_gains(z, carry):
        look_up(mats[z], ITERS + z)
        return carry
    lax.fori_loop(0, depth, own_gains, 0)

    def first_level(at, carry):
        _, results = applied(v0, at, lambda c, d: gains[comp * c + d, at])
        for c in range(comp):
            v1[c, at] = results[c]
        return carry
    lax.fori_loop(1, ext - 1, first_level, 0)

    def clear(ref, lows, highs):
        @pl.when(place == 0)
        def _():
            for c in range(comp):
                for t in lows:
                    ref[c, t] = jnp.zeros((py, px), jnp.float32)

        @pl.when(place == last)
        def _():
            for c in range(comp):
                for t in highs:
                    ref[c, t] = jnp.zeros((py, px), jnp.float32)

    clear(v1, (1, 2), (ext - 3, ext - 2))

    def second_level(at, carry):
        _, results = applied(v1, at, lambda c, d: gains[comp * c + d, at])
        for c in range(comp):
            v2[c, at] = results[c]
        return carry
    lax.fori_loop(2, ext - 2, second_level, 0)
    clear(v2, (2,), (ext - 3,))

    def fold(value):
        total = value[0:8]
        for t in range(1, py // 8):
            total += value[8 * t : 8 * (t + 1)]
        return total

    def third_level(z, sums):
        at = ITERS + z
        thirds, fourths = applied(v2, at, lambda c, d: gains[comp * c + d, at])
        sums = list(sums)
        for c in range(comp):
            basis = [v0[c, at], v1[c, at], thirds[c], fourths[c]]
            for g, (i, j) in enumerate(PAIRS):
                sums[g] = sums[g] + fold(basis[i] * basis[j])
            block = basis[0]
            for k in range(1, ITERS + 1):
                block = jnp.where((lane == 2 * k) | (lane == 2 * k - 1), pltpu.roll(basis[k], 2 * k, 1), block)
            packed[z, pl.ds(py * c, py)] = block
        return tuple(sums)
    zero = jnp.zeros((8, px), jnp.float32)
    sums = lax.fori_loop(0, depth, third_level, tuple(zero for _ in PAIRS))

    for z in range(depth):
        turned = packed[z].T
        for k in range(ITERS + 1):
            left_out[k, pl.ds(z, 1)] = turned[2 * k : 2 * k + 1]
            at = (2 * k - 1) % px
            right_out[k, pl.ds(z, 1)] = turned[at : at + 1]

    spots = lax.broadcasted_iota(jnp.int32, (1, px), 1)
    line = jnp.zeros((1, px), jnp.float32)
    even = lax.rem(spots, 2) == 0
    slab = depth * py

    def corner_row(index):
        c = index // slab
        z = (index - c * slab) // py
        y = index - c * slab - z * py
        return packed[z, pl.ds(c * py + y, 1)]

    count = corners.shape[0]
    for j in range(count):
        mine = pltpu.roll(corner_row(corners[j]), 8 * j + 1, 1)
        before = pltpu.roll(corner_row(corners_before[j]), 8 * j + 1, 1)
        line = jnp.where(spots // 8 == j, jnp.where(even, mine, before), line)
    for g in range(len(PAIRS)):
        line = jnp.where(spots == GRAM_LANE + g, jnp.sum(sums[g]), line)
    message[...] = jnp.broadcast_to(line, message.shape)


def coefficients(gram, mean, scale):
    centre = 6.0 + mean

    def inner(u, w):
        total = None
        for i, a in enumerate(u):
            part = None
            for j, b in enumerate(w):
                term = gram[(min(i, j), max(i, j))] * b
                part = term if part is None else part + term
            part = a * part
            total = part if total is None else total + part
        return total

    one = jnp.ones_like(gram[(0, 0)])
    residual, direction, found = [one], [one], []
    norm = gram[(0, 0)]
    for repeat in range(ITERS):
        size = len(direction)
        image = [centre * direction[0]]
        for j in range(1, size):
            image.append(centre * direction[j] + scale * direction[j - 1])
        image.append(scale * direction[size - 1])
        step = norm / inner(direction, image)
        found = [
            (found[j] if j < len(found) else 0.0) + step * direction[j] for j in range(size)
        ]
        residual = [
            (residual[j] if j < size else 0.0) - step * image[j] for j in range(size + 1)
        ]
        if repeat + 1 < ITERS:
            fresh = inner(residual, residual)
            ratio = fresh / norm
            direction = [
                residual[j] + (ratio * direction[j] if j < size else 0.0) for j in range(size + 1)
            ]
            norm = fresh
    return found, residual


def final_kernel(kinds, messages, body, v1, v2, right, left_next, table, coarse, corners,
                 solution_out, interface_out, book):
    comp, depth, py, px = body.shape
    devices = messages.shape[0]
    n_in = lax.axis_size("in")
    me = lax.axis_index("sub") * n_in + lax.axis_index("in")
    following = lax.rem(me + n_in, devices)
    mean, scale, _ = spectrum(table[...], comp, kinds)

    got = messages[...]
    lane = lax.broadcasted_iota(jnp.int32, got.shape, 1)
    row = lax.broadcasted_iota(jnp.int32, got.shape, 0)
    groups = got.reshape(devices // n_in, n_in, px) if n_in % 8 == 0 else None
    if groups is not None:
        summed = jnp.broadcast_to(jnp.sum(groups, axis=1, keepdims=True), groups.shape).reshape(got.shape)
    else:
        summed = got
        reach = 1
        while reach < n_in:
            partner = jnp.where(
                lax.rem(row // reach, 2) == 0,
                pltpu.roll(summed, devices - reach, 0),
                pltpu.roll(summed, reach, 0))
            summed = summed + partner
            reach *= 2
    gram = {}
    for g, pair in enumerate(PAIRS):
        gram[pair] = summed[:, GRAM_LANE + g : GRAM_LANE + g + 1]
    found, residual = coefficients(gram, mean, scale)

    kind = lax.rem(lane, 8) // 2
    spread = jnp.zeros_like(got)
    sheet = jnp.zeros_like(got)
    for k in range(ITERS + 1):
        spread = jnp.where(kind == k, residual[k], spread)
        sheet = jnp.where(lane == k, residual[k], sheet)
    for k in range(ITERS):
        sheet = jnp.where(lane == ITERS + 1 + k, found[k], sheet)
    book[...] = sheet
    product = got * spread
    product = jnp.where(lax.rem(lane, 2) == 0, product, pltpu.roll(product, devices - n_in, 0))
    for reach in (1, 2, 4):
        product = product + pltpu.roll(product, px - reach, 1)
    count = corners.shape[0]
    spots = jnp.minimum(lane * 8, px - 1)
    product = jnp.take_along_axis(product, spots, axis=1)[:, :count]

    mine = book[pl.ds(me, 1)]
    other = book[pl.ds(following, 1)]

    face = None
    for k in range(ITERS + 1):
        part = mine[:, k : k + 1] * right[k] + other[:, k : k + 1] * left_next[k]
        face = part if face is None else face + part

    zs = lax.broadcasted_iota(jnp.int32, face.shape, 0)
    ls = lax.broadcasted_iota(jnp.int32, face.shape, 1)
    slab = depth * py
    add = jnp.zeros_like(face)
    for j in range(count):
        value = jnp.sum(coarse[j] * product)
        index = corners[j]
        c = index // slab
        z = (index - c * slab) // py
        y = index - c * slab - z * py
        add = add + jnp.where((zs == z) & (ls == c * py + y), value, 0.0)
    face = face + add
    for c in range(comp):
        interface_out[0, c] = face[:, py * c : py * (c + 1)]

    def combine(z, carry):
        at = ITERS + z
        for c in range(comp):
            total = jnp.broadcast_to(mine[:, 4:5], (py, px)) * body[c, z]
            total += jnp.broadcast_to(mine[:, 5:6], (py, px)) * v1[c, at]
            total += jnp.broadcast_to(mine[:, 6:7], (py, px)) * v2[c, at]
            solution_out[c, z] = total
        return carry
    lax.fori_loop(0, depth, combine, 0)


def on_device(body_load, materials, material_tables, corner_index, coarse_inverse):
    comp, depth, py, px = body_load.shape
    kinds = material_tables.shape[0]
    n_in, n_sub = lax.axis_size("in"), lax.axis_size("sub")
    devices = n_in * n_sub
    count = corner_index.shape[0]
    ext = depth + 2 * ITERS
    f32 = jnp.float32
    shape = jax.ShapeDtypeStruct
    halo = shape((ITERS * comp + MAT_DEPTH, py, px), f32)

    table = jnp.pad(material_tables.transpose(1, 2, 0).reshape(comp * comp, kinds), ((0, 0), (0, LANES - kinds)))
    coarse = coarse_inverse.reshape(count, devices, count)

    send_a, send_b = pl.pallas_call(
        pack_kernel,
        out_shape=(halo, halo),
        in_specs=[HBM, HBM],
        out_specs=(VMEM, VMEM),
        scratch_shapes=[
            pltpu.VMEM((2, MAT_DEPTH, py, px), jnp.int32),
            pltpu.SemaphoreType.DMA((2, comp + 1)),
        ],
        name="pack",
    )(body_load, materials)

    def swaps(start):
        pairs = [(i, i + 1) for i in range(start, n_in - 1, 2)]
        return pairs + [(j, i) for i, j in pairs]

    halo_a = lax.ppermute(send_a, "in", swaps(0))
    halo_b = lax.ppermute(send_b, "in", swaps(1))
    corners_before = lax.ppermute(corner_index, "sub", [(i, (i + 1) % n_sub) for i in range(n_sub)])

    extended = shape((comp, ext, py, px), f32)
    faces = shape((ITERS + 1, depth, comp * py), f32)
    v1, v2, left, right, message = pl.pallas_call(
        functools.partial(basis_kernel, kinds),
        out_shape=(extended, extended, faces, faces, shape((devices, LANES), f32)),
        in_specs=[VMEM, VMEM, VMEM, VMEM, VMEM, SMEM, SMEM],
        out_specs=(VMEM,) * 5,
        scratch_shapes=[
            pltpu.VMEM((comp, ext, py, px), f32),
            pltpu.VMEM((comp * comp, ext, py, px), f32),
            pltpu.VMEM((depth, comp * py, px), f32),
        ],
        name="basis",
    )(body_load, materials, halo_a, halo_b, table, corner_index, corners_before)

    left_next = lax.ppermute(left, "sub", [((i + 1) % n_sub, i) for i in range(n_sub)])
    messages = lax.all_to_all(message, ("sub", "in"), 0, 0, tiled=True)

    return pl.pallas_call(
        functools.partial(final_kernel, kinds),
        out_shape=(shape(body_load.shape, f32), shape((1, comp, depth, py), f32)),
        in_specs=[VMEM] * 8 + [SMEM],
        out_specs=(VMEM, VMEM),
        scratch_shapes=[pltpu.VMEM((devices, LANES), f32)],
        name="final",
    )(messages, body_load, v1, v2, right, left_next, table, coarse, corner_index)


def solution(mesh):
    return jax.shard_map(
        on_device,
        mesh=mesh,
        in_specs=(
            P(None, "in", None, "sub"),
            P("in", None, "sub"),
            P(),
            P(("sub", "in")),
            P(("sub", "in"), None),
        ),
        out_specs=(P(None, "in", None, "sub"), P("sub", None, "in", None)),
        check_vma=False,
    )
```

time: 124 us -> 43.3 us (0.35)
  blocking collectives: 72.7 us -> 0 us
  Pallas kernels: 0 us -> 16.7 us
  other arithmetic: 15.7 us -> 0 us
  between operations: 10.6 us -> 0.72 us
  waiting for transfers between devices: 1.88 us -> 8.43 us
  starting transfers between devices: 18.6 us -> 13.8 us
    unnamed x1 -> x0, blocking collectives: 38.8 us -> none
    psum x3 -> x0, blocking collectives: 33.8 us -> none  [two_products(): lax.psum((jnp.sum(residual * residual), jnp.sum(residual * applied)), 'in')]
    pallas_call x0 -> x3, Pallas kernels: none -> 16.7 us  [the longest x1 9.6 us: on_device(): pl.pallas_call(functools.partial(basis_kernel, kinds), out_shape=(extende...]
    ppermute x7 -> x4, starting transfers between devices: 18.6 us -> 6.28 us  [the longest x1 3.12 us: on_device(): halo_a = lax.ppermute(send_a, 'in', swaps(0))]
    reduce_sum x6 -> x0, other arithmetic: 9.4 us -> none  [the longest x3 5.07 us: stencil(): coupled = jnp.sum(gains * center[None], axis=1)]
    all_to_all x0 -> x1, starting transfers between devices: none -> 7.49 us  [on_device(): messages = lax.all_to_all(message, ('sub', 'in'), 0, 0, tiled=True)]
    all_to_all x0 -> x1, waiting for transfers between devices: none -> 3.29 us  [on_device(): messages = lax.all_to_all(message, ('sub', 'in'), 0, 0, tiled=True)]
    ppermute x7 -> x4, waiting for transfers between devices: 1.88 us -> 5.14 us  [the longest x1 3.28 us: on_device(): lax.ppermute(corner_index, 'sub', [(i, (i + 1) % n_sub) for i in range(n_...]
  transfers between devices with their start and end apart: 7 -> 5, of which waited for: 2 -> 4; matrix products, arithmetic and copies ran while one was open for 6% -> 3% of each run, Pallas kernels for 0% -> 0%
where the time goes in v1:
time: 43.3 us; the launch traced here: 43 us
  Pallas kernels  16.7 us (39%)
  starting transfers between devices  13.8 us (32%)
  waiting for transfers between devices  8.43 us (19%)
  local copies, waits for them, and re-layouts  3.36 us (8%)
  between operations  0.72 us (2%)
    pallas_call x1, Pallas kernels, on_device(): pl.pallas_call(functools.partial(basis_kernel, kinds), out_shape=(extende...  9.6 us
    all_to_all x1, starting transfers between devices, on_device(): messages = lax.all_to_all(message, ('sub', 'in'), 0, 0, tiled=True)  7.49 us
    pallas_call x1, Pallas kernels, on_device(): pl.pallas_call(functools.partial(final_kernel, kinds), out_shape=(shape(b...  5.29 us
    all_to_all x1, waiting for transfers between devices, on_device(): messages = lax.all_to_all(message, ('sub', 'in'), 0, 0, tiled=True)  3.29 us
    ppermute x1, waiting for transfers between devices, on_device(): lax.ppermute(corner_index, 'sub', [(i, (i + 1) % n_sub) for i in range(n_...  3.28 us
    ppermute x1, starting transfers between devices, on_device(): halo_a = lax.ppermute(send_a, 'in', swaps(0))  3.12 us
    ppermute x1, starting transfers between devices, on_device(): lax.ppermute(left, 'sub', [((i + 1) % n_sub, i) for i in range(n_sub)])  2.44 us
    unnamed x18, local copies, waits for them, and re-layouts  2 us
  transfers between devices with their start and end apart: 5, of which 4 were waited for; matrix products, arithmetic and copies ran while one was open for 3% of the time, Pallas kernels for 0%

profile of v1, /device:TPU:0, one launch (start us, length us, event | category | flops | bytes accessed | tf_op | source)
XLA Modules:
  0.0 43.0 jit_solution(13928415862813872972)
XLA Ops:
  0.6 0.0 copy-start.5
  0.6 1.9 %pack.1 = (f32[14,32,128]{2,1,0:T(8,128)}, f32[14,32,128]{2,1,0:T(8,128)}) custom-call(f32[4,8,32,128]{3,2,1,0:T(8,128)} %body.5, s32[8,32,128]{2,1,0:T(8,128)} %mats.3), custom_call_target="tpu_custom_call" | custom-call | tf_op jit(solution)/shard_map/pack/pallas_call | solution.py:334
  2.5 0.0 copy-start.6
  2.5 3.1 %collective-permute-start = (f32[14,32,128]{2,1,0:T(8,128)}, f32[14,32,128]{2,1,0:T(8,128)S(1)}, u32[]{:S(2)}, u32[]{:S(2)}) collective-permute-start(f32[14,32,128]{2,1,0:T(8,128)} %get-tuple-element.9), channel_id=1, source_target_pairs={{0,1},{2,3},{1,0},{3,2},{4,5},{6,7},{5,4},{7,6},{8,9},{10,11},{9,8... | collective-permute-start | bytes 688136 | tf_op jit(solution)/shard_map/ppermute | solution.py:350
  5.6 0.7 %collective-permute-start.1 = (f32[14,32,128]{2,1,0:T(8,128)}, f32[14,32,128]{2,1,0:T(8,128)S(1)}, u32[]{:S(2)}, u32[]{:S(2)}) collective-permute-start(f32[14,32,128]{2,1,0:T(8,128)} %get-tuple-element.10), channel_id=1, source_target_pairs={{1,2},{2,1},{5,6},{6,5},{9,10},{10,9},{13,14},{14,13},{17,18},{18,... | collective-permute-start | bytes 688136 | tf_op jit(solution)/shard_map/ppermute | solution.py:351
  6.3 0.0 copy-done.6
  6.3 0.1 collective-permute-start.2
  6.4 0.0 copy-done.5
  6.4 0.6 %pad.4.table = f32[16,128]{1,0:T(8,128)} pad(f32[16,8]{1,0:T(8,128)S(1)} %bitcast.9, f32[]{:T(128)} %constant.2.clone.1), padding=0_0x0_120 | pad | bytes 8708 | tf_op jit(solution)/shard_map/jit(_pad)/pad | solution.py:331
  7.0 3.3 %collective-permute-done.2.corners_before = s32[8]{0:T(128)S(1)} collective-permute-done((s32[8]{0:T(128)S(1)}, s32[8]{0:T(128)S(1)}, u32[]{:S(2)}, u32[]{:S(2)}) %collective-permute-start.2) | collective-permute-done | bytes 64 | tf_op jit(solution)/shard_map/ppermute | solution.py:352
  10.3 0.0 copy-start.7
  10.3 1.2 %collective-permute-done.halo_a = f32[14,32,128]{2,1,0:T(8,128)S(1)} collective-permute-done((f32[14,32,128]{2,1,0:T(8,128)}, f32[14,32,128]{2,1,0:T(8,128)S(1)}, u32[]{:S(2)}, u32[]{:S(2)}) %collective-permute-start) | collective-permute-done | bytes 229408 | tf_op jit(solution)/shard_map/ppermute | solution.py:350
  11.4 0.0 copy-start
  11.4 0.0 collective-permute-done.1.halo_b
  11.4 0.0 copy-done.7
  11.5 0.7 %copy-done = f32[14,32,128]{2,1,0:T(8,128)} copy-done((f32[14,32,128]{2,1,0:T(8,128)}, f32[14,32,128]{2,1,0:T(8,128)S(1)}, u32[]{:S(2)}) %copy-start) | copy-done | bytes 229400
  12.1 0.0 copy-start.1
  12.1 0.7 %copy-done.1 = f32[14,32,128]{2,1,0:T(8,128)} copy-done((f32[14,32,128]{2,1,0:T(8,128)}, f32[14,32,128]{2,1,0:T(8,128)S(1)}, u32[]{:S(2)}) %copy-start.1) | copy-done | bytes 229400
  12.8 9.6 %basis.1 = (f32[4,14,32,128]{3,2,1,0:T(8,128)}, f32[4,14,32,128]{3,2,1,0:T(8,128)}, f32[4,8,128]{2,1,0:T(8,128)}, f32[4,8,128]{2,1,0:T(8,128)}, f32[32,128]{1,0:T(8,128)}) custom-call(f32[4,8,32,128]{3,2,1,0:T(8,128)} %body.5, s32[8,32,128]{2,1,0:T(8,128)} %mats.3, f32[14,32,128]{2,1,0:T(8,128)} %copy-done, f32[14,32,128]{2,1,0:T(8,128)} %copy-done.1, ...), custom_call_target="tpu_custom_call" | custom-call | tf_op jit(solution)/shard_map/basis/pallas_call | solution.py:356
  22.4 0.0 copy-start.8
  22.4 0.0 copy-start.4
  22.4 7.5 %all-to-all-start = ((f32[32,1,128]{2,1,0:T(1,128)}), f32[32,1,128]{2,1,0:T(1,128)S(1)}, u32[]{:S(2)}, u32[]{:S(2)}) async-start(f32[32,1,128]{2,1,0:T(1,128)} %bitcast.8), calls=%async_computation | async-start | bytes 32768 | tf_op jit(solution)/shard_map/all_to_all | solution.py:370
  29.9 0.0 copy-done.8
  30.0 2.4 %collective-permute-start.3 = (f32[4,8,128]{2,1,0:T(8,128)S(1)}, f32[4,8,128]{2,1,0:T(8,128)S(1)}, u32[]{:S(2)}, u32[]{:S(2)}) collective-permute-start(f32[4,8,128]{2,1,0:T(8,128)S(1)} %copy-done.8), channel_id=1, source_target_pairs={{4,0},{8,4},{12,8},{16,12},{20,16},{24,20},{28,24},{0,28},{5,1},{9... | collective-permute-start | bytes 49160 | tf_op jit(solution)/shard_map/ppermute | solution.py:369
  32.4 0.0 copy-done.4
  32.4 0.8 %reshape.13.coarse = f32[8,32,8]{2,1,0:T(8,128)} reshape(f32[8,256]{1,0:T(8,128)S(1)} %copy-done.4) | data formatting | bytes 16384 | tf_op jit(solution)/shard_map/reshape | solution.py:332
  33.2 0.7 %collective-permute-done.3.left_next = f32[4,8,128]{2,1,0:T(8,128)S(1)} collective-permute-done((f32[4,8,128]{2,1,0:T(8,128)S(1)}, f32[4,8,128]{2,1,0:T(8,128)S(1)}, u32[]{:S(2)}, u32[]{:S(2)}) %collective-permute-start.3) | collective-permute-done | bytes 16416 | tf_op jit(solution)/shard_map/ppermute | solution.py:369
  33.8 0.0 copy-start.3
  33.8 3.3 %all-to-all-done = f32[32,1,128]{2,1,0:T(1,128)S(1)} async-done(((f32[32,1,128]{2,1,0:T(1,128)}), f32[32,1,128]{2,1,0:T(1,128)S(1)}, u32[]{:S(2)}, u32[]{:S(2)}) %all-to-all-start) | async-done | bytes 16416 | tf_op jit(solution)/shard_map/all_to_all | solution.py:370
  37.1 0.0 copy-start.2
  37.1 0.0 copy-done.3
  37.1 0.6 %copy-done.2 = f32[32,1,128]{2,1,0:T(1,128)} copy-done((f32[32,1,128]{2,1,0:T(1,128)}, f32[32,1,128]{2,1,0:T(1,128)S(1)}, u32[]{:S(2)}) %copy-start.2) | copy-done | bytes 16408
  37.7 5.3 %final.1 = (f32[4,8,32,128]{3,2,1,0:T(8,128)}, f32[1,4,8,32]{3,2,1,0:T(8,128)}) custom-call(f32[32,128]{1,0:T(8,128)} %bitcast.7, f32[4,8,32,128]{3,2,1,0:T(8,128)} %body.5, f32[4,14,32,128]{3,2,1,0:T(8,128)} %get-tuple-element.12.v1, f32[4,14,32,128]{3,2,1,0:T(8,128)} %get-tuple-element.13.v2, f32[4,8,128]{2,1,0:T(8,128)} %get-tuple-element.14.right, ...), custom_call_target="tpu_custom_call" | custom-call | tf_op jit(solution)/shard_map/final/pallas_call | solution.py:372
Async XLA Ops:
  0.6 5.8 %copy-start.5 = (f32[8,4,4]{0,2,1:T(4,128)S(1)}, f32[8,4,4]{0,2,1:T(4,128)}, u32[]{:S(2)}) copy-start(f32[8,4,4]{0,2,1:T(4,128)} %param.7) | copy-start | bytes 1540
  2.5 3.8 %copy-start.6 = (s32[8]{0:T(128)S(1)}, s32[8]{0:T(128)}, u32[]{:S(2)}) copy-start(s32[8]{0:T(128)} %corners.3) | copy-start | bytes 100
  2.5 8.9 %collective-permute-start = (f32[14,32,128]{2,1,0:T(8,128)}, f32[14,32,128]{2,1,0:T(8,128)S(1)}, u32[]{:S(2)}, u32[]{:S(2)}) collective-permute-start(f32[14,32,128]{2,1,0:T(8,128)} %get-tuple-element.9), channel_id=1, source_target_pairs={{0,1},{2,3},{1,0},{3,2},{4,5},{6,7},{5,4},{7,6},{8,9},{10,11},{9,8... | collective-permute-start | bytes 688136 | tf_op jit(solution)/shard_map/ppermute | solution.py:350
  5.6 5.8 %collective-permute-start.1 = (f32[14,32,128]{2,1,0:T(8,128)}, f32[14,32,128]{2,1,0:T(8,128)S(1)}, u32[]{:S(2)}, u32[]{:S(2)}) collective-permute-start(f32[14,32,128]{2,1,0:T(8,128)} %get-tuple-element.10), channel_id=1, source_target_pairs={{1,2},{2,1},{5,6},{6,5},{9,10},{10,9},{13,14},{14,13},{17,18},{18,... | collective-permute-start | bytes 688136 | tf_op jit(solution)/shard_map/ppermute | solution.py:351
  6.3 3.9 %collective-permute-start.2 = (s32[8]{0:T(128)S(1)}, s32[8]{0:T(128)S(1)}, u32[]{:S(2)}, u32[]{:S(2)}) collective-permute-start(s32[8]{0:T(128)S(1)} %copy-done.6), channel_id=1, source_target_pairs={{0,4},{4,8},{8,12},{12,16},{16,20},{20,24},{24,28},{28,0},{1,5},{5... | collective-permute-start | bytes 104 | tf_op jit(solution)/shard_map/ppermute | solution.py:352
  10.3 1.2 %copy-start.7 = (s32[8]{0:T(128)}, s32[8]{0:T(128)S(1)}, u32[]{:S(2)}) copy-start(s32[8]{0:T(128)S(1)} %collective-permute-done.2.corners_before) | copy-start | bytes 100
  11.4 0.7 %copy-start = (f32[14,32,128]{2,1,0:T(8,128)}, f32[14,32,128]{2,1,0:T(8,128)S(1)}, u32[]{:S(2)}) copy-start(f32[14,32,128]{2,1,0:T(8,128)S(1)} %collective-permute-done.halo_a) | copy-start | bytes 688132
  12.1 0.7 %copy-start.1 = (f32[14,32,128]{2,1,0:T(8,128)}, f32[14,32,128]{2,1,0:T(8,128)S(1)}, u32[]{:S(2)}) copy-start(f32[14,32,128]{2,1,0:T(8,128)S(1)} %collective-permute-done.1.halo_b) | copy-start | bytes 688132
  22.4 7.5 %copy-start.8 = (f32[4,8,128]{2,1,0:T(8,128)S(1)}, f32[4,8,128]{2,1,0:T(8,128)}, u32[]{:S(2)}) copy-start(f32[4,8,128]{2,1,0:T(8,128)} %get-tuple-element.15) | copy-start | bytes 49156
  22.4 10.0 %copy-start.4 = (f32[8,256]{1,0:T(8,128)S(1)}, f32[8,256]{1,0:T(8,128)}, u32[]{:S(2)}) copy-start(f32[8,256]{1,0:T(8,128)} %param.9) | copy-start | bytes 24580
  22.4 14.7 %all-to-all-start = ((f32[32,1,128]{2,1,0:T(1,128)}), f32[32,1,128]{2,1,0:T(1,128)S(1)}, u32[]{:S(2)}, u32[]{:S(2)}) async-start(f32[32,1,128]{2,1,0:T(1,128)} %bitcast.8), calls=%async_computation | async-start | bytes 32768 | tf_op jit(solution)/shard_map/all_to_all | solution.py:370
  30.0 3.9 %collective-permute-start.3 = (f32[4,8,128]{2,1,0:T(8,128)S(1)}, f32[4,8,128]{2,1,0:T(8,128)S(1)}, u32[]{:S(2)}, u32[]{:S(2)}) collective-permute-start(f32[4,8,128]{2,1,0:T(8,128)S(1)} %copy-done.8), channel_id=1, source_target_pairs={{4,0},{8,4},{12,8},{16,12},{20,16},{24,20},{28,24},{0,28},{5,1},{9... | collective-permute-start | bytes 49160 | tf_op jit(solution)/shard_map/ppermute | solution.py:369
  33.8 3.3 %copy-start.3 = (f32[4,8,128]{2,1,0:T(8,128)}, f32[4,8,128]{2,1,0:T(8,128)S(1)}, u32[]{:S(2)}) copy-start(f32[4,8,128]{2,1,0:T(8,128)S(1)} %collective-permute-done.3.left_next) | copy-start | bytes 49156
  37.1 0.6 %copy-start.2 = (f32[32,1,128]{2,1,0:T(1,128)}, f32[32,1,128]{2,1,0:T(1,128)S(1)}, u32[]{:S(2)}) copy-start(f32[32,1,128]{2,1,0:T(1,128)S(1)} %all-to-all-done) | copy-start | bytes 49156

commit v2 on v0

v2 whole, which is shorter than its diff:
```python
import functools

import jax
import jax.numpy as jnp
from jax import lax
from jax.experimental import pallas as pl
from jax.experimental.pallas import tpu as pltpu
from jax.sharding import PartitionSpec as P

ITERS = 3
LANES = 128
MAT_DEPTH = ITERS - 1
PAIRS = [(i, j) for i in range(ITERS) for j in range(i, ITERS + 1)]
GRAM_LANE = 64
VMEM = pl.BlockSpec(memory_space=pltpu.VMEM)
SMEM = pl.BlockSpec(memory_space=pltpu.SMEM)
HBM = pl.BlockSpec(memory_space=pl.ANY)


def spectrum(table, comp):
    kinds = table.shape[1]
    rows = lax.broadcasted_iota(jnp.int32, table.shape, 0)
    diagonal = lax.rem(rows, comp + 1) == 0
    picked = jnp.where(diagonal, table, 0.0)
    mean = jnp.sum(jnp.sum(picked, axis=0, keepdims=True), axis=1, keepdims=True) / (comp * kinds)
    centred = jnp.where(diagonal, table - mean, table)
    size = jnp.abs(centred)
    widest = jnp.zeros((1, kinds), jnp.float32)
    for c in range(comp):
        widest = jnp.maximum(widest, jnp.sum(size[comp * c : comp * (c + 1)], axis=0, keepdims=True))
    scale = 6.0 + jnp.max(widest, axis=1, keepdims=True)
    return mean, scale, centred


def split(index, size):
    if size & (size - 1):
        return lax.div(index, size), lax.rem(index, size)
    return lax.shift_right_logical(index, size.bit_length() - 1), index & (size - 1)


def pack_kernel(body, mats, table, a_out, b_out, body_out, mats_out, table_out, kinds, sems, whole):
    comp, depth = body.shape[0], body.shape[1]
    odd = lax.rem(lax.axis_index("in"), 2)
    copies = []
    for slot, (out, low) in enumerate(((a_out, odd), (b_out, 1 - odd))):
        first = (1 - low) * (depth - MAT_DEPTH)
        copies.append(pltpu.make_async_copy(
            mats.at[pl.ds(first, MAT_DEPTH)], kinds.at[slot], sems.at[slot, comp]))
        first = (1 - low) * (depth - ITERS)
        for c in range(comp):
            copies.append(pltpu.make_async_copy(
                body.at[c, pl.ds(first, ITERS)], out.at[pl.ds(ITERS * c, ITERS)], sems.at[slot, c]))
    copies.append(pltpu.make_async_copy(table, table_out, whole.at[0]))
    copies.append(pltpu.make_async_copy(mats, mats_out, whole.at[1]))
    copies.append(pltpu.make_async_copy(body, body_out, whole.at[2]))
    for copy in copies:
        copy.start()
    for copy in copies:
        copy.wait()
    for slot, out in enumerate((a_out, b_out)):
        out[pl.ds(ITERS * comp, MAT_DEPTH)] = kinds[slot].astype(jnp.float32)


class Slab:
    def __init__(self, comp, py, px):
        self.comp, self.px, self.parts = comp, px, py // 8
        lane = lax.broadcasted_iota(jnp.int32, (8, px), 1)
        row = lax.broadcasted_iota(jnp.int32, (8, px), 0)
        self.lane = lane
        self.first_x, self.last_x = lane == 0, lane == px - 1
        self.first_y, self.last_y = row == 0, row == 7

    def natural(self, ref, *at):
        return [ref[(*at, pl.ds(r, 8, stride=self.parts))] for r in range(self.parts)]

    def load(self, ref, *at):
        return [ref[(*at, pl.ds(8 * r, 8))] for r in range(self.parts)]

    def store(self, ref, values, *at):
        for r in range(self.parts):
            ref[(*at, pl.ds(8 * r, 8))] = values[r]

    def neighbours(self, below, above, value):
        parts, px = self.parts, self.px
        totals = []
        for r in range(parts):
            total = below[r] + above[r]
            total += jnp.where(self.first_x, 0.0, pltpu.roll(value[r], 1, 1))
            total += jnp.where(self.last_x, 0.0, pltpu.roll(value[r], px - 1, 1))
            total += value[r - 1] if r else jnp.where(self.first_y, 0.0, pltpu.roll(value[parts - 1], 1, 0))
            total += value[r + 1] if r + 1 < parts else jnp.where(self.last_y, 0.0, pltpu.roll(value[0], 7, 0))
            totals.append(total)
        return totals

    def applied(self, source, at, gains, gains_at, inverse, alive=None):
        comp, parts = self.comp, self.parts
        values = [self.load(source, c, at) for c in range(comp)]
        for c in range(comp):
            around = self.neighbours(self.load(source, c, at - 1), self.load(source, c, at + 1), values[c])
            out = []
            for r in range(parts):
                total = None
                for d in range(comp):
                    term = gains[comp * c + d, gains_at, pl.ds(8 * r, 8)] * values[d][r]
                    total = term if total is None else total + term
                total = total - inverse * around[r]
                out.append(total if alive is None else alive * total)
            yield c, values[c], out

    def products(self, total, left, right):
        for r in range(self.parts):
            total = total + left[r] * right[r]
        return total

    def look_up(self, kinds, tab, gains, at, count):
        bits = [[(kind & (1 << b)) != 0 for kind in kinds] for b in range((count - 1).bit_length())]
        entries = self.comp * self.comp
        for e in range(entries):
            lines = [tab[pl.ds(k * entries + e, 8, stride=0)] for k in range(count)]
            out = []
            for r in range(self.parts):
                level = lines
                for bit in bits:
                    level = [
                        jnp.where(bit[r], level[k + 1], level[k]) if k + 1 < len(level) else level[k]
                        for k in range(0, len(level), 2)
                    ]
                out.append(level[0])
            self.store(gains, out, e, at)

    def pack(self, packed, z, c, basis):
        rows = self.parts * 8
        for r in range(self.parts):
            block = basis[0][r]
            for k in range(1, len(basis)):
                here = (self.lane == 2 * k) | (self.lane == 2 * k - 1)
                block = jnp.where(here, pltpu.roll(basis[k][r], 2 * k, 1), block)
            packed[z, pl.ds(rows * c + 8 * r, 8)] = block


def levels(slab, v0, v1, v2, gains, packed, inverse):
    def first(z, sums):
        g01, g11 = sums
        for c, v, w in slab.applied(v0, z + 3, gains, z + 2, inverse):
            slab.store(v1, w, c, z + 2)
            g01, g11 = slab.products(g01, v, w), slab.products(g11, w, w)
        return g01, g11

    def second(z, sums):
        g02, g12, g22 = sums
        for c, v, w in slab.applied(v1, z + 2, gains, z + 2, inverse):
            slab.store(v2, w, c, z + 1)
            u = slab.load(v0, c, z + 3)
            g02, g12, g22 = slab.products(g02, u, w), slab.products(g12, v, w), slab.products(g22, w, w)
        return g02, g12, g22

    def third(z, sums):
        g03, g13, g23 = sums
        for c, v, w in slab.applied(v2, z + 1, gains, z + 2, inverse):
            t, u = slab.load(v0, c, z + 3), slab.load(v1, c, z + 2)
            slab.pack(packed, z, c, (t, u, v, w))
            g03, g13, g23 = slab.products(g03, t, w), slab.products(g13, u, w), slab.products(g23, v, w)
        return g03, g13, g23

    return first, second, third


def interior_kernel(body, mats, table, v0, v1, v2, gains, packed, gram, tab):
    comp, depth, py, px = body.shape
    kinds = table.shape[1]
    entries = comp * comp
    slab = Slab(comp, py, px)
    mean, scale, centred = spectrum(table[...], comp)
    inverse = jnp.broadcast_to(1.0 / scale, (8, px))
    scaled = centred / scale
    for k in range(kinds):
        tab[pl.ds(k * entries, entries)] = jnp.broadcast_to(scaled[:, k : k + 1], (entries, px))
    for t, value in enumerate((inverse, mean, scale)):
        tab[pl.ds(kinds * entries + 8 * t, 8)] = jnp.broadcast_to(value, (8, px))
    zero = jnp.zeros((8, px), jnp.float32)

    def own(z, g00):
        for c in range(comp):
            value = slab.natural(body, c, z)
            slab.store(v0, value, c, ITERS + z)
            g00 = slab.products(g00, value, value)
        slab.look_up(slab.natural(mats, z), tab, gains, MAT_DEPTH + z, kinds)
        return g00
    g00 = lax.fori_loop(0, depth, own, zero)

    first, second, third = levels(slab, v0, v1, v2, gains, packed, inverse)
    g01, g11 = lax.fori_loop(1, depth - 1, first, (zero,) * 2)
    g02, g12, g22 = lax.fori_loop(2, depth - 2, second, (zero,) * 3)
    g03, g13, g23 = lax.fori_loop(3, depth - 3, third, (zero,) * 3)
    for g, value in enumerate((g00, g01, g02, g03, g11, g12, g13, g22, g23)):
        gram[g] = value


def edge_kernel(kinds, halo_a, halo_b, tab, corners_hbm, before_hbm, v0_in, v1_in, v2_in, gains_in, packed_in, gram_in,
                v0, v1, v2, gains, packed, message, corners, before, sems):
    comp, py, px = v0.shape[0], v0.shape[2], v0.shape[3]
    depth = packed.shape[0]
    fetch = (
        pltpu.make_async_copy(corners_hbm, corners, sems.at[0]),
        pltpu.make_async_copy(before_hbm, before, sems.at[1]),
    )
    for copy in fetch:
        copy.start()
    slab = Slab(comp, py, px)
    parts = slab.parts
    place = lax.axis_index("in")
    odd = lax.rem(place, 2) == 1
    inverse = tab[pl.ds(kinds * comp * comp, 8)]
    alive = (
        (place > 0).astype(jnp.float32),
        (place < lax.axis_size("in") - 1).astype(jnp.float32),
    )

    for t in range(ITERS):
        for c in range(comp):
            a = slab.natural(halo_a, ITERS * c + t)
            b = slab.natural(halo_b, ITERS * c + t)
            slab.store(v0, [jnp.where(odd, x, y) for x, y in zip(a, b)], c, t)
            slab.store(v0, [jnp.where(odd, y, x) for x, y in zip(a, b)], c, ITERS + depth + t)

    def halo_gains(t, carry):
        a = slab.natural(halo_a, ITERS * comp + t)
        b = slab.natural(halo_b, ITERS * comp + t)
        low = [jnp.where(odd, x, y).astype(jnp.int32) for x, y in zip(a, b)]
        high = [jnp.where(odd, y, x).astype(jnp.int32) for x, y in zip(a, b)]
        slab.look_up(low, tab, gains, t, kinds)
        slab.look_up(high, tab, gains, MAT_DEPTH + depth + t, kinds)
        return carry
    lax.fori_loop(0, MAT_DEPTH, halo_gains, 0)

    g00, g01, g02, g03, g11, g12, g13, g22, g23 = [gram_in[g] for g in range(len(PAIRS))]
    first, second, third = levels(slab, v0, v1, v2, gains, packed, inverse)

    def first_halo(i, carry):
        for side, z in enumerate((i - 2, depth + i)):
            for c, _, w in slab.applied(v0, z + 3, gains, z + 2, inverse, alive[side]):
                slab.store(v1, w, c, z + 2)
        return carry
    lax.fori_loop(0, 2, first_halo, 0)
    g01, g11 = lax.fori_loop(0, 2, lambda i, sums: first(i * (depth - 1), sums), (g01, g11))
    for side, z in enumerate((-1, depth)):
        for c, _, w in slab.applied(v1, z + 2, gains, z + 2, inverse, alive[side]):
            slab.store(v2, w, c, z + 1)
    g02, g12, g22 = lax.fori_loop(
        0, 2, lambda i, sums: second(depth - 2 + i, second(i, sums)), (g02, g12, g22))
    g03, g13, g23 = lax.fori_loop(
        0, 3, lambda i, sums: third(depth - 3 + i, third(i, sums)), (g03, g13, g23))

    spots = lax.broadcasted_iota(jnp.int32, (1, px), 1)
    line = jnp.zeros((1, px), jnp.float32)
    even = lax.rem(spots, 2) == 0
    for g, value in enumerate((g00, g01, g02, g03, g11, g12, g13, g22, g23)):
        total = jnp.sum(jnp.sum(value, axis=0, keepdims=True), axis=1, keepdims=True)
        line = jnp.where(spots == GRAM_LANE + g, total, line)

    for copy in fetch:
        copy.wait()

    def corner_row(index):
        c, rest = split(index, depth * py)
        z, y = split(rest, py)
        t, r = split(y, parts)
        return packed[z, pl.ds(c * py + r * 8 + t, 1)]

    for j in range(corners.shape[0]):
        mine = corner_row(corners[j])
        other = corner_row(before[j])
        odd_lanes = pltpu.roll(jnp.where(even, other, mine), 8 * j + 1, 1)
        line = jnp.where(spots // 8 == j, odd_lanes, line)
    message[...] = jnp.broadcast_to(line, message.shape)


def faces_kernel(packed, left, right):
    depth, _, px = packed.shape
    for z in range(depth):
        turned = packed[z].T
        for k in range(ITERS + 1):
            at = (2 * k - 1) % px
            left[k, pl.ds(z, 1)] = turned[2 * k : 2 * k + 1]
            right[k, pl.ds(z, 1)] = turned[at : at + 1]


def coefficients(gram, mean, scale):
    centre = 6.0 + mean

    def inner(u, w):
        total = None
        for i, a in enumerate(u):
            part = None
            for j, b in enumerate(w):
                term = gram[(min(i, j), max(i, j))] * b
                part = term if part is None else part + term
            part = a * part
            total = part if total is None else total + part
        return total

    one = jnp.ones_like(gram[(0, 0)])
    residual, direction, found = [one], [one], []
    norm = gram[(0, 0)]
    for repeat in range(ITERS):
        size = len(direction)
        image = [centre * direction[0]]
        for j in range(1, size):
            image.append(centre * direction[j] + scale * direction[j - 1])
        image.append(scale * direction[size - 1])
        step = norm / inner(direction, image)
        found = [
            (found[j] if j < len(found) else 0.0) + step * direction[j] for j in range(size)
        ]
        residual = [
            (residual[j] if j < size else 0.0) - step * image[j] for j in range(size + 1)
        ]
        if repeat + 1 < ITERS:
            fresh = inner(residual, residual)
            ratio = fresh / norm
            direction = [
                residual[j] + (ratio * direction[j] if j < size else 0.0) for j in range(size + 1)
            ]
            norm = fresh
    return found, residual


def final_kernel(kinds, messages, v0, v1, v2, right, left_next, tab, coarse, corners,
                 solution_hbm, interface_out, found_book, solution_out, sems):
    comp, py, px = v0.shape[0], v0.shape[2], v0.shape[3]
    depth = right.shape[1]
    n_in, n_sub = lax.axis_size("in"), lax.axis_size("sub")
    sub = lax.axis_index("sub")
    following = lax.rem(sub + 1, n_sub)
    slab = Slab(comp, py, px)
    base = kinds * comp * comp
    mean, scale = tab[pl.ds(base + 8, 1)][:, :1], tab[pl.ds(base + 16, 1)][:, :1]

    got = [messages[pl.ds(i, n_sub, stride=n_in)] for i in range(n_in)]
    summed = got[0]
    for i in range(1, n_in):
        summed = summed + got[i]
    gram = {}
    for g, pair in enumerate(PAIRS):
        gram[pair] = summed[:, GRAM_LANE + g : GRAM_LANE + g + 1]
    found, residual = coefficients(gram, mean, scale)

    lane = lax.broadcasted_iota(jnp.int32, summed.shape, 1)
    kind = lax.rem(lane, 8) // 2
    spread = jnp.zeros_like(summed)
    sheet = jnp.zeros_like(summed)
    for k in range(ITERS + 1):
        spread = jnp.where(kind == k, residual[k], spread)
        sheet = jnp.where(lane == k, residual[k], sheet)
    for k in range(ITERS):
        sheet = jnp.where(lane == ITERS + 1 + k, found[k], sheet)
    found_book[...] = sheet
    mine = found_book[pl.ds(sub, 1)]
    other = found_book[pl.ds(following, 1)]

    weights = [jnp.broadcast_to(mine[:, ITERS + 1 + k : ITERS + 2 + k], (8, px)) for k in range(ITERS)]
    copies = [
        pltpu.make_async_copy(solution_out.at[:, z], solution_hbm.at[:, z], sems.at[z]) for z in range(depth)
    ]
    for z in range(depth):
        for c in range(comp):
            fields = slab.load(v0, c, z + 3), slab.load(v1, c, z + 2), slab.load(v2, c, z + 1)
            for r in range(slab.parts):
                total = weights[0] * fields[0][r] + weights[1] * fields[1][r] + weights[2] * fields[2][r]
                solution_out[c, z, pl.ds(r, 8, stride=slab.parts)] = total
        copies[z].start()

    count = corners.shape[1]
    spots = jnp.minimum(lane * 8, px - 1)
    values = []
    for i in range(n_in):
        product = got[i] * spread
        product = jnp.where(lax.rem(lane, 2) == 0, product, pltpu.roll(product, n_sub - 1, 0))
        for reach in (1, 2, 4):
            product = product + pltpu.roll(product, px - reach, 1)
        values.append(jnp.take_along_axis(product, spots, axis=1, mode="promise_in_bounds")[:, :count])

    face = None
    for k in range(ITERS + 1):
        part = mine[:, k : k + 1] * right[k] + other[:, k : k + 1] * left_next[k]
        face = part if face is None else face + part

    zs = lax.broadcasted_iota(jnp.int32, face.shape, 0)
    ls = lax.broadcasted_iota(jnp.int32, face.shape, 1)
    y = lax.rem(ls, py)
    face = jnp.take_along_axis(
        face, ls - y + lax.rem(y, slab.parts) * 8 + y // slab.parts, axis=1, mode="promise_in_bounds")
    flat = (ls // py) * (depth * py) + zs * py + y
    picks = corners[...]
    for j in range(count):
        total = None
        for i in range(n_in):
            part = coarse[j, i] * values[i]
            total = part if total is None else total + part
        value = jnp.sum(jnp.sum(total, axis=0, keepdims=True), axis=1, keepdims=True)
        face = face + jnp.where(flat == picks[:, j : j + 1], value, 0.0)
    for c in range(comp):
        interface_out[0, c] = face[:, py * c : py * (c + 1)]
    for copy in copies:
        copy.wait()


def params(mib):
    return pltpu.CompilerParams(vmem_limit_bytes=mib * 2**20)


def on_device(body_load, materials, material_tables, corner_index, coarse_inverse):
    comp, depth, py, px = body_load.shape
    kinds = material_tables.shape[0]
    n_in, n_sub = lax.axis_size("in"), lax.axis_size("sub")
    devices = n_in * n_sub
    count = corner_index.shape[0]
    f32 = jnp.float32
    shape = jax.ShapeDtypeStruct
    halo = shape((ITERS * comp + MAT_DEPTH, py, px), f32)

    table = material_tables.transpose(1, 2, 0).reshape(comp * comp, kinds)
    coarse = coarse_inverse.reshape(count, n_sub, n_in, count).transpose(0, 2, 1, 3)

    def hbm(x):
        return pltpu.with_memory_space_constraint(x, pltpu.HBM)

    send_a, send_b, body, mats, table = pl.pallas_call(
        pack_kernel,
        out_shape=(halo, halo, shape(body_load.shape, f32), shape(materials.shape, jnp.int32), shape(table.shape, f32)),
        in_specs=[HBM] * 3,
        out_specs=(VMEM,) * 5,
        scratch_shapes=[
            pltpu.VMEM((2, MAT_DEPTH, py, px), jnp.int32),
            pltpu.SemaphoreType.DMA((2, comp + 1)),
            pltpu.SemaphoreType.DMA((3,)),
        ],
        compiler_params=params(4),
        name="pack",
    )(hbm(body_load), hbm(materials), hbm(table))

    def swaps(start):
        pairs = [(i, i + 1) for i in range(start, n_in - 1, 2)]
        return pairs + [(j, i) for i, j in pairs]

    halo_a = lax.ppermute(send_a, "in", swaps(0))
    halo_b = lax.ppermute(send_b, "in", swaps(1))
    before = lax.ppermute(corner_index, "sub", [(i, (i + 1) % n_sub) for i in range(n_sub)])

    fields = (
        shape((comp, depth + 2 * ITERS, py, px), f32),
        shape((comp, depth + 2 * ITERS - 2, py, px), f32),
        shape((comp, depth + 2 * ITERS - 4, py, px), f32),
        shape((comp * comp, depth + 2 * MAT_DEPTH, py, px), f32),
        shape((depth, comp * py, px), f32),
    )
    *inner, tab = pl.pallas_call(
        interior_kernel,
        out_shape=(*fields, shape((len(PAIRS), 8, px), f32), shape((kinds * comp * comp + 24, px), f32)),
        in_specs=[VMEM] * 3,
        out_specs=(VMEM,) * 7,
        compiler_params=params(4),
        name="interior",
    )(body, mats, table)

    v0, v1, v2, _, packed, message = pl.pallas_call(
        functools.partial(edge_kernel, kinds),
        out_shape=(*fields, shape((devices, LANES), f32)),
        in_specs=[VMEM] * 3 + [HBM] * 2 + [VMEM] * 6,
        out_specs=(VMEM,) * 6,
        input_output_aliases={5: 0, 6: 1, 7: 2, 8: 3, 9: 4},
        scratch_shapes=[
            pltpu.SMEM((count,), jnp.int32),
            pltpu.SMEM((count,), jnp.int32),
            pltpu.SemaphoreType.DMA((2,)),
        ],
        compiler_params=params(4),
        name="edge",
    )(halo_a, halo_b, tab, hbm(corner_index), before, *inner)

    messages = lax.all_to_all(message, ("sub", "in"), 0, 0, tiled=True)
    faces = shape((ITERS + 1, depth, comp * py), f32)
    left, right = pl.pallas_call(
        faces_kernel,
        out_shape=(faces, faces),
        in_specs=[VMEM],
        out_specs=(VMEM, VMEM),
        compiler_params=params(4),
        name="faces",
    )(packed)
    left_next = lax.ppermute(left, "sub", [((i + 1) % n_sub, i) for i in range(n_sub)])

    return pl.pallas_call(
        functools.partial(final_kernel, kinds),
        out_shape=(shape(body_load.shape, f32), shape((1, comp, depth, py), f32)),
        in_specs=[VMEM] * 9,
        out_specs=(HBM, VMEM),
        scratch_shapes=[
            pltpu.VMEM((n_sub, LANES), f32),
            pltpu.VMEM(body_load.shape, f32),
            pltpu.SemaphoreType.DMA((depth,)),
        ],
        compiler_params=params(16),
        name="final",
    )(messages, v0, v1, v2, right, left_next, tab, coarse, corner_index.reshape(1, count))


def solution(mesh):
    return jax.shard_map(
        on_device,
        mesh=mesh,
        in_specs=(
            P(None, "in", None, "sub"),
            P("in", None, "sub"),
            P(),
            P(("sub", "in")),
            P(("sub", "in"), None),
        ),
        out_specs=(P(None, "in", None, "sub"), P("sub", None, "in", None)),
        check_vma=False,
    )
```

time: 124 us -> 32.4 us (0.26)
  blocking collectives: 72.7 us -> 0 us
  other arithmetic: 15.7 us -> 0 us
  Pallas kernels: 0 us -> 10.1 us
  between operations: 10.6 us -> 0.71 us
  waiting for transfers between devices: 1.88 us -> 6.74 us
  starting transfers between devices: 18.6 us -> 14.5 us
  local copies, waits for them, and re-layouts: 4.09 us -> 0.21 us
    unnamed x1 -> x0, blocking collectives: 38.8 us -> none
    psum x3 -> x0, blocking collectives: 33.8 us -> none  [two_products(): lax.psum((jnp.sum(residual * residual), jnp.sum(residual * applied)), 'in')]
    ppermute x7 -> x4, starting transfers between devices: 18.6 us -> 6.28 us  [the longest x1 3.12 us: on_device(): halo_a = lax.ppermute(send_a, 'in', swaps(0))]
    pallas_call x0 -> x5, Pallas kernels: none -> 10.1 us  [the longest x1 3.16 us: on_device(): pl.pallas_call(functools.partial(edge_kernel, kinds), out_shape=(*fields,...]
    reduce_sum x6 -> x0, other arithmetic: 9.4 us -> none  [the longest x3 5.07 us: stencil(): coupled = jnp.sum(gains * center[None], axis=1)]
    all_to_all x0 -> x1, starting transfers between devices: none -> 8.18 us  [on_device(): messages = lax.all_to_all(message, ('sub', 'in'), 0, 0, tiled=True)]
    all_to_all x0 -> x1, waiting for transfers between devices: none -> 3.04 us  [on_device(): messages = lax.all_to_all(message, ('sub', 'in'), 0, 0, tiled=True)]
    slice x5 -> x0, local copies, waits for them, and re-layouts: 2.65 us -> none  [the longest x1 1.19 us: node_tables(): tables[material_kind][:, :, None, None, None]]
  transfers between devices with their start and end apart: 7 -> 5, of which waited for: 2 -> 4; matrix products, arithmetic and copies ran while one was open for 6% -> 1% of each run, Pallas kernels for 0% -> 8%
where the time goes in v2:
time: 32.4 us; the launch traced here: 32.3 us
  starting transfers between devices  14.5 us (45%)
  Pallas kernels  10.1 us (31%)
  waiting for transfers between devices  6.74 us (21%)
  between operations  0.71 us (2%)
    all_to_all x1, starting transfers between devices, on_device(): messages = lax.all_to_all(message, ('sub', 'in'), 0, 0, tiled=True)  8.18 us
    pallas_call x1, Pallas kernels, on_device(): pl.pallas_call(functools.partial(edge_kernel, kinds), out_shape=(*fields,...  3.16 us
    ppermute x1, starting transfers between devices, on_device(): halo_a = lax.ppermute(send_a, 'in', swaps(0))  3.12 us
    all_to_all x1, waiting for transfers between devices, on_device(): messages = lax.all_to_all(message, ('sub', 'in'), 0, 0, tiled=True)  3.04 us
    pallas_call x1, Pallas kernels, on_device(): pl.pallas_call(functools.partial(final_kernel, kinds), out_shape=(shape(b...  2.93 us
    ppermute x1, starting transfers between devices, on_device(): lax.ppermute(left, 'sub', [((i + 1) % n_sub, i) for i in range(n_sub)])  2.44 us
    pallas_call x1, Pallas kernels, on_device(): pl.pallas_call(interior_kernel, out_shape=(*fields, shape((len(PAIRS), 8,...  2.38 us
    ppermute x1, waiting for transfers between devices, on_device(): lax.ppermute(corner_index, 'sub', [(i, (i + 1) % n_sub) for i in range(n_...  1.63 us
  transfers between devices with their start and end apart: 5, of which 4 were waited for; matrix products, arithmetic and copies ran while one was open for 1% of the time, Pallas kernels for 8%

profile of v2, /device:TPU:0, one launch (start us, length us, event | category | flops | bytes accessed | tf_op | source)
XLA Modules:
  0.0 32.3 jit_solution(10003867111811131756)
XLA Ops:
  0.6 1.5 %pack.1 = (f32[14,32,128]{2,1,0:T(8,128)S(1)}, f32[14,32,128]{2,1,0:T(8,128)S(1)}, f32[4,8,32,128]{3,2,1,0:T(8,128)S(1)}, s32[8,32,128]{2,1,0:T(8,128)S(1)}, f32[16,8]{1,0:T(8,128)S(1)}) custom-call(f32[4,8,32,128]{3,2,1,0:T(8,128)} %body.1, s32[8,32,128]{2,1,0:T(8,128)} %mats.1, f32[16,8]{1,0:T(8,128)} %bitcast.14), custom_call_target="tpu_custom_call" | custom-call | tf_op jit(solution)/shard_map/pack/pallas_call | solution.py:428
  2.1 3.1 %collective-permute-start = (f32[14,32,128]{2,1,0:T(8,128)S(1)}, f32[14,32,128]{2,1,0:T(8,128)S(1)}, u32[]{:S(2)}, u32[]{:S(2)}) collective-permute-start(f32[14,32,128]{2,1,0:T(8,128)S(1)} %get-tuple-element.21), channel_id=1, source_target_pairs={{0,1},{2,3},{1,0},{3,2},{4,5},{6,7},{5,4},{7,6},{8,9},{10,11},{9,8... | collective-permute-start | bytes 688136 | tf_op jit(solution)/shard_map/ppermute | solution.py:446
  5.2 0.7 %collective-permute-start.1 = (f32[14,32,128]{2,1,0:T(8,128)S(1)}, f32[14,32,128]{2,1,0:T(8,128)S(1)}, u32[]{:S(2)}, u32[]{:S(2)}) collective-permute-start(f32[14,32,128]{2,1,0:T(8,128)S(1)} %get-tuple-element.22), channel_id=1, source_target_pairs={{1,2},{2,1},{5,6},{6,5},{9,10},{10,9},{13,14},{14,13},{17,18},{18,... | collective-permute-start | bytes 688136 | tf_op jit(solution)/shard_map/ppermute | solution.py:447
  5.9 0.1 collective-permute-start.2
  6.0 2.4 %interior.1 = (f32[4,14,32,128]{3,2,1,0:T(8,128)S(1)}, f32[4,12,32,128]{3,2,1,0:T(8,128)S(1)}, f32[4,10,32,128]{3,2,1,0:T(8,128)S(1)}, f32[16,12,32,128]{3,2,1,0...) custom-call(f32[4,8,32,128]{3,2,1,0:T(8,128)S(1)} %get-tuple-element.23.body, ...), custom_call_target="tpu_custom_call" | custom-call | tf_op jit(solution)/shard_map/interior/pallas_call | solution.py:457
  8.4 1.6 %collective-permute-done.2.before_hbm = s32[8]{0:T(128)S(1)} collective-permute-done((s32[8]{0:T(128)}, s32[8]{0:T(128)S(1)}, u32[]{:S(2)}, u32[]{:S(2)}) %collective-permute-start.2) | collective-permute-done | bytes 64 | tf_op jit(solution)/shard_map/ppermute | solution.py:448
  10.0 0.9 %collective-permute-done.halo_a = f32[14,32,128]{2,1,0:T(8,128)S(1)} collective-permute-done((f32[14,32,128]{2,1,0:T(8,128)S(1)}, f32[14,32,128]{2,1,0:T(8,128)S(1)}, u32[]{:S(2)}, u32[]{:S(2)}) %collective-permute-start) | collective-permute-done | bytes 229408 | tf_op jit(solution)/shard_map/ppermute | solution.py:446
  10.8 0.0 collective-permute-done.1.halo_b
  10.8 0.0 copy-start.1
  10.8 0.0 copy-start
  10.8 3.2 %edge.1 = (f32[4,14,32,128]{3,2,1,0:T(8,128)S(1)}, f32[4,12,32,128]{3,2,1,0:T(8,128)S(1)}, f32[4,10,32,128]{3,2,1,0:T(8,128)S(1)}, f32[16,12,32,128]{3,2,1,0:T(8...) custom-call(f32[14,32,128]{2,1,0:T(8,128)S(1)} %collective-permute-d, ...), custom_call_target="tpu_custom_call", output_to_operand_aliasing={{0}: (5, {}), {1}: (6, {}), {2}: (7, {}), {3}: (8, {}), {4}... | custom-call | tf_op jit(solution)/shard_map/edge/pallas_call | solution.py:466
  14.0 8.2 %all-to-all-start = ((f32[32,1,128]{2,1,0:T(1,128)}), f32[32,1,128]{2,1,0:T(1,128)S(1)}, u32[]{:S(2)}, u32[]{:S(2)}) async-start(f32[32,1,128]{2,1,0:T(1,128)} %bitcast.3), calls=%async_computation | async-start | bytes 32768 | tf_op jit(solution)/shard_map/all_to_all | solution.py:481
  22.2 0.2 faces.1
  22.4 2.4 %collective-permute-start.3 = (f32[4,8,128]{2,1,0:T(8,128)S(1)}, f32[4,8,128]{2,1,0:T(8,128)S(1)}, u32[]{:S(2)}, u32[]{:S(2)}) collective-permute-start(f32[4,8,128]{2,1,0:T(8,128)S(1)} %get-tuple-element.39), channel_id=1, source_target_pairs={{4,0},{8,4},{12,8},{16,12},{20,16},{24,20},{28,24},{0,28},{5,1},{9... | collective-permute-start | bytes 49160 | tf_op jit(solution)/shard_map/ppermute | solution.py:491
  24.8 0.0 copy-done.1
  24.8 0.2 reshape.16
  25.1 1.2 %collective-permute-done.3.left_next = f32[4,8,128]{2,1,0:T(8,128)S(1)} collective-permute-done((f32[4,8,128]{2,1,0:T(8,128)S(1)}, f32[4,8,128]{2,1,0:T(8,128)S(1)}, u32[]{:S(2)}, u32[]{:S(2)}) %collective-permute-start.3) | collective-permute-done | bytes 16416 | tf_op jit(solution)/shard_map/ppermute | solution.py:491
  26.3 3.0 %all-to-all-done = f32[32,1,128]{2,1,0:T(1,128)S(1)} async-done(((f32[32,1,128]{2,1,0:T(1,128)}), f32[32,1,128]{2,1,0:T(1,128)S(1)}, u32[]{:S(2)}, u32[]{:S(2)}) %all-to-all-start) | async-done | bytes 16416 | tf_op jit(solution)/shard_map/all_to_all | solution.py:481
  29.3 0.0 copy-done
  29.3 2.9 %final.1 = (f32[4,8,32,128]{3,2,1,0:T(8,128)}, f32[1,4,8,32]{3,2,1,0:T(8,128)}) custom-call(f32[32,128]{1,0:T(8,128)S(1)} %bitcast.12, f32[4,14,32,128]{3,2,1,0:T(8,128)S(1)} %get-tuple-element.34.v0, f32[4,12,32,128]{3,2,1,0:T(8,128)S(1)} %get-tuple-element.35.v1, f32[4,10,32,128]{3,2,1,0:T(8,128)S(1)} %get-tuple-element.36.v2, ...), custom_call_target="tpu_custom_call" | custom-call | tf_op jit(solution)/shard_map/final/pallas_call | solution.py:493
  (1 shorter events, 0.0 us)
Async XLA Ops:
  2.1 8.7 %collective-permute-start = (f32[14,32,128]{2,1,0:T(8,128)S(1)}, f32[14,32,128]{2,1,0:T(8,128)S(1)}, u32[]{:S(2)}, u32[]{:S(2)}) collective-permute-start(f32[14,32,128]{2,1,0:T(8,128)S(1)} %get-tuple-element.21), channel_id=1, source_target_pairs={{0,1},{2,3},{1,0},{3,2},{4,5},{6,7},{5,4},{7,6},{8,9},{10,11},{9,8... | collective-permute-start | bytes 688136 | tf_op jit(solution)/shard_map/ppermute | solution.py:446
  5.2 5.6 %collective-permute-start.1 = (f32[14,32,128]{2,1,0:T(8,128)S(1)}, f32[14,32,128]{2,1,0:T(8,128)S(1)}, u32[]{:S(2)}, u32[]{:S(2)}) collective-permute-start(f32[14,32,128]{2,1,0:T(8,128)S(1)} %get-tuple-element.22), channel_id=1, source_target_pairs={{1,2},{2,1},{5,6},{6,5},{9,10},{10,9},{13,14},{14,13},{17,18},{18,... | collective-permute-start | bytes 688136 | tf_op jit(solution)/shard_map/ppermute | solution.py:447
  5.9 4.1 %collective-permute-start.2 = (s32[8]{0:T(128)}, s32[8]{0:T(128)S(1)}, u32[]{:S(2)}, u32[]{:S(2)}) collective-permute-start(s32[8]{0:T(128)} %corners_hbm.1), channel_id=1, source_target_pairs={{0,4},{4,8},{8,12},{12,16},{16,20},{20,24},{24,28},{28,0},{1,5},{5... | collective-permute-start | bytes 104 | tf_op jit(solution)/shard_map/ppermute | solution.py:448
  10.8 14.0 %copy-start.1 = (f32[8,256]{1,0:T(8,128)S(1)}, f32[8,256]{1,0:T(8,128)}, u32[]{:S(2)}) copy-start(f32[8,256]{1,0:T(8,128)} %param.9) | copy-start | bytes 24580
  10.8 18.5 %copy-start = (s32[8]{0:T(128)S(1)}, s32[8]{0:T(128)}, u32[]{:S(2)}) copy-start(s32[8]{0:T(128)} %corners_hbm.1) | copy-start | bytes 100
  14.0 15.3 %all-to-all-start = ((f32[32,1,128]{2,1,0:T(1,128)}), f32[32,1,128]{2,1,0:T(1,128)S(1)}, u32[]{:S(2)}, u32[]{:S(2)}) async-start(f32[32,1,128]{2,1,0:T(1,128)} %bitcast.3), calls=%async_computation | async-start | bytes 32768 | tf_op jit(solution)/shard_map/all_to_all | solution.py:481
  22.4 3.9 %collective-permute-start.3 = (f32[4,8,128]{2,1,0:T(8,128)S(1)}, f32[4,8,128]{2,1,0:T(8,128)S(1)}, u32[]{:S(2)}, u32[]{:S(2)}) collective-permute-start(f32[4,8,128]{2,1,0:T(8,128)S(1)} %get-tuple-element.39), channel_id=1, source_target_pairs={{4,0},{8,4},{12,8},{16,12},{20,16},{24,20},{28,24},{0,28},{5,1},{9... | collective-permute-start | bytes 49160 | tf_op jit(solution)/shard_map/ppermute | solution.py:491

commit v3 on v2

--- a/solution.py
+++ b/solution.py
@@ -165,7 +165,7 @@
     return first, second, third
 
 
-def interior_kernel(body, mats, table, v0, v1, v2, gains, packed, gram, tab):
+def interior_kernel(body, mats, table, v0, v1, v2, gains, packed, gram, tab, v3):
     comp, depth, py, px = body.shape
     kinds = table.shape[1]
     entries = comp * comp
@@ -178,6 +178,9 @@
     for t, value in enumerate((inverse, mean, scale)):
         tab[pl.ds(kinds * entries + 8 * t, 8)] = jnp.broadcast_to(value, (8, px))
     zero = jnp.zeros((8, px), jnp.float32)
+    for c in range(comp):
+        for at in (ITERS - 1, ITERS + depth):
+            slab.store(v0, [zero] * slab.parts, c, at)
 
     def own(z, g00):
         for c in range(comp):
@@ -188,73 +191,126 @@
         return g00
     g00 = lax.fori_loop(0, depth, own, zero)
 
+    def partial(i, carry):
+        z = i * (depth - 1)
+        for c, _, w in slab.applied(v0, z + 3, gains, z + 2, inverse):
+            slab.store(v1, w, c, z + 2)
+        return carry
+
+    def partial_second(i, carry):
+        z = 1 + i * (depth - 3)
+        for c, _, w in slab.applied(v1, z + 2, gains, z + 2, inverse):
+            slab.store(v2, w, c, z + 1)
+        return carry
+
+    def partial_third(i, carry):
+        z = 2 + i * (depth - 5)
+        for c, _, w in slab.applied(v2, z + 1, gains, z + 2, inverse):
+            slab.store(v3, w, c, i)
+        return carry
+
     first, second, third = levels(slab, v0, v1, v2, gains, packed, inverse)
+    lax.fori_loop(0, 2, partial, 0)
     g01, g11 = lax.fori_loop(1, depth - 1, first, (zero,) * 2)
+    lax.fori_loop(0, 2, partial_second, 0)
     g02, g12, g22 = lax.fori_loop(2, depth - 2, second, (zero,) * 3)
+    lax.fori_loop(0, 2, partial_third, 0)
     g03, g13, g23 = lax.fori_loop(3, depth - 3, third, (zero,) * 3)
     for g, value in enumerate((g00, g01, g02, g03, g11, g12, g13, g22, g23)):
         gram[g] = value
 
 
-def edge_kernel(kinds, halo_a, halo_b, tab, corners_hbm, before_hbm, v0_in, v1_in, v2_in, gains_in, packed_in, gram_in,
-                v0, v1, v2, gains, packed, message, corners, before, sems):
+def one_side(kinds, slot, halo, tab, v3, gram, v0, v1, v2, gains, packed):
     comp, py, px = v0.shape[0], v0.shape[2], v0.shape[3]
     depth = packed.shape[0]
+    slab = Slab(comp, py, px)
+    place = lax.axis_index("in")
+    low = lax.rem(place + 1 + slot, 2) == 0
+    alive = jnp.where(low, place > 0, place < lax.axis_size("in") - 1).astype(jnp.float32)
+    inverse = tab[pl.ds(kinds * comp * comp, 8)]
+
+    def layer(q):
+        return jnp.where(low, q, depth - 1 - q)
+
+    base = jnp.where(low, 0, ITERS + depth)
+    for t in range(ITERS):
+        for c in range(comp):
+            slab.store(v0, slab.natural(halo, ITERS * c + t), c, base + t)
+
+    base_gains = jnp.where(low, 0, MAT_DEPTH + depth)
+
+    def halo_gains(t, carry):
+        kind = [x.astype(jnp.int32) for x in slab.natural(halo, ITERS * comp + t)]
+        slab.look_up(kind, tab, gains, base_gains + t, kinds)
+        return carry
+    lax.fori_loop(0, MAT_DEPTH, halo_gains, 0)
+
+    g00, g01, g02, g03, g11, g12, g13, g22, g23 = [gram[g] for g in range(len(PAIRS))]
+    first, second, third = levels(slab, v0, v1, v2, gains, packed, inverse)
+
+    def first_halo(i, carry):
+        z = layer(i - 2)
+        for c, _, w in slab.applied(v0, z + 3, gains, z + 2, inverse, alive):
+            slab.store(v1, w, c, z + 2)
+        return carry
+    lax.fori_loop(0, 2, first_halo, 0)
+
+    z0, z1, z2, out = layer(0), layer(1), layer(2), layer(-1)
+    side = jnp.where(low, 0, 1)
+
+    def mend(c, sums):
+        g01, g11, g02, g12, g22, g03, g13, g23 = sums
+        term = [inverse * x for x in slab.load(v0, c, out + 3)]
+        w = [a - b for a, b in zip(slab.load(v1, c, z0 + 2), term)]
+        slab.store(v1, w, c, z0 + 2)
+        g01, g11 = slab.products(g01, slab.load(v0, c, z0 + 3), w), slab.products(g11, w, w)
+        term = [inverse * x for x in term]
+        w = [a + b for a, b in zip(slab.load(v2, c, z1 + 1), term)]
+        slab.store(v2, w, c, z1 + 1)
+        g02 = slab.products(g02, slab.load(v0, c, z1 + 3), w)
+        g12 = slab.products(g12, slab.load(v1, c, z1 + 2), w)
+        g22 = slab.products(g22, w, w)
+        term = [inverse * x for x in term]
+        w = [a - b for a, b in zip(slab.load(v3, c, side), term)]
+        t, u, v = slab.load(v0, c, z2 + 3), slab.load(v1, c, z2 + 2), slab.load(v2, c, z2 + 1)
+        slab.pack(packed, z2, c, (t, u, v, w))
+        g03, g13, g23 = slab.products(g03, t, w), slab.products(g13, u, w), slab.products(g23, v, w)
+        return g01, g11, g02, g12, g22, g03, g13, g23
+    sums = (g01, g11, g02, g12, g22, g03, g13, g23)
+    for c in range(comp):
+        sums = mend(c, sums)
+    g01, g11, g02, g12, g22, g03, g13, g23 = sums
+
+    for c, _, w in slab.applied(v1, out + 2, gains, out + 2, inverse, alive):
+        slab.store(v2, w, c, out + 1)
+    g02, g12, g22 = second(z0, (g02, g12, g22))
+    g03, g13, g23 = lax.fori_loop(0, 2, lambda i, sums: third(layer(i), sums), (g03, g13, g23))
+    return g00, g01, g02, g03, g11, g12, g13, g22, g23
+
+
+def near_kernel(kinds, halo, tab, v3, v0_in, v1_in, v2_in, gains_in, packed_in, gram_in,
+                v0, v1, v2, gains, packed, gram):
+    sums = one_side(kinds, 0, halo, tab, v3, gram_in, v0, v1, v2, gains, packed)
+    for g, value in enumerate(sums):
+        gram[g] = value
+
+
+def far_kernel(kinds, halo, tab, v3, corners_hbm, before_hbm, v0_in, v1_in, v2_in, gains_in, packed_in, gram_in,
+               v0, v1, v2, gains, packed, message, corners, before, sems):
     fetch = (
         pltpu.make_async_copy(corners_hbm, corners, sems.at[0]),
         pltpu.make_async_copy(before_hbm, before, sems.at[1]),
     )
     for copy in fetch:
         copy.start()
-    slab = Slab(comp, py, px)
-    parts = slab.parts
-    place = lax.axis_index("in")
-    odd = lax.rem(place, 2) == 1
-    inverse = tab[pl.ds(kinds * comp * comp, 8)]
-    alive = (
-        (place > 0).astype(jnp.float32),
-        (place < lax.axis_size("in") - 1).astype(jnp.float32),
-    )
-
-    for t in range(ITERS):
-        for c in range(comp):
-            a = slab.natural(halo_a, ITERS * c + t)
-            b = slab.natural(halo_b, ITERS * c + t)
-            slab.store(v0, [jnp.where(odd, x, y) for x, y in zip(a, b)], c, t)
-            slab.store(v0, [jnp.where(odd, y, x) for x, y in zip(a, b)], c, ITERS + depth + t)
-
-    def halo_gains(t, carry):
-        a = slab.natural(halo_a, ITERS * comp + t)
-        b = slab.natural(halo_b, ITERS * comp + t)
-        low = [jnp.where(odd, x, y).astype(jnp.int32) for x, y in zip(a, b)]
-        high = [jnp.where(odd, y, x).astype(jnp.int32) for x, y in zip(a, b)]
-        slab.look_up(low, tab, gains, t, kinds)
-        slab.look_up(high, tab, gains, MAT_DEPTH + depth + t, kinds)
-        return carry
-    lax.fori_loop(0, MAT_DEPTH, halo_gains, 0)
-
-    g00, g01, g02, g03, g11, g12, g13, g22, g23 = [gram_in[g] for g in range(len(PAIRS))]
-    first, second, third = levels(slab, v0, v1, v2, gains, packed, inverse)
-
-    def first_halo(i, carry):
-        for side, z in enumerate((i - 2, depth + i)):
-            for c, _, w in slab.applied(v0, z + 3, gains, z + 2, inverse, alive[side]):
-                slab.store(v1, w, c, z + 2)
-        return carry
-    lax.fori_loop(0, 2, first_halo, 0)
-    g01, g11 = lax.fori_loop(0, 2, lambda i, sums: first(i * (depth - 1), sums), (g01, g11))
-    for side, z in enumerate((-1, depth)):
-        for c, _, w in slab.applied(v1, z + 2, gains, z + 2, inverse, alive[side]):
-            slab.store(v2, w, c, z + 1)
-    g02, g12, g22 = lax.fori_loop(
-        0, 2, lambda i, sums: second(depth - 2 + i, second(i, sums)), (g02, g12, g22))
-    g03, g13, g23 = lax.fori_loop(
-        0, 3, lambda i, sums: third(depth - 3 + i, third(i, sums)), (g03, g13, g23))
+    py, px = v0.shape[2], v0.shape[3]
+    depth, parts = packed.shape[0], py // 8
+    sums = one_side(kinds, 1, halo, tab, v3, gram_in, v0, v1, v2, gains, packed)
 
     spots = lax.broadcasted_iota(jnp.int32, (1, px), 1)
     line = jnp.zeros((1, px), jnp.float32)
     even = lax.rem(spots, 2) == 0
-    for g, value in enumerate((g00, g01, g02, g03, g11, g12, g13, g22, g23)):
+    for g, value in enumerate(sums):
         total = jnp.sum(jnp.sum(value, axis=0, keepdims=True), axis=1, keepdims=True)
         line = jnp.where(spots == GRAM_LANE + g, total, line)
 
@@ -270,8 +326,8 @@
     for j in range(corners.shape[0]):
         mine = corner_row(corners[j])
         other = corner_row(before[j])
-        odd_lanes = pltpu.roll(jnp.where(even, other, mine), 8 * j + 1, 1)
-        line = jnp.where(spots // 8 == j, odd_lanes, line)
+        moved = pltpu.roll(jnp.where(even, other, mine), 8 * j + 1, 1)
+        line = jnp.where(spots // 8 == j, moved, line)
     message[...] = jnp.broadcast_to(line, message.shape)
 
 
@@ -285,30 +341,37 @@
             right[k, pl.ds(z, 1)] = turned[at : at + 1]
 
 
-def coefficients(gram, mean, scale):
-    centre = 6.0 + mean
-
-    def inner(u, w):
-        total = None
-        for i, a in enumerate(u):
-            part = None
-            for j, b in enumerate(w):
-                term = gram[(min(i, j), max(i, j))] * b
-                part = term if part is None else part + term
-            part = a * part
-            total = part if total is None else total + part
-        return total
-
-    one = jnp.ones_like(gram[(0, 0)])
+def total_of(terms):
+    while len(terms) > 1:
+        terms = [sum(terms[k : k + 2][1:], terms[k]) for k in range(0, len(terms), 2)]
+    return terms[0]
+
+
+def coefficients(gram, centre, scale):
+    norms, images = {}, {}
+    for i in range(ITERS):
+        for j in range(i, ITERS):
+            forward = centre * gram[(i, j)] + scale * gram[(i, j + 1)]
+            if i == j:
+                norms[(i, j)], images[(i, j)] = gram[(i, j)], forward
+            else:
+                back = centre * gram[(i, j)] + scale * gram[(i + 1, j)]
+                norms[(i, j)], images[(i, j)] = 2.0 * gram[(i, j)], forward + back
+
+    def quadratic(form, u):
+        size = len(u)
+        return total_of([(u[i] * u[j]) * form[(i, j)] for i in range(size) for j in range(i, size)])
+
+    one = jnp.ones_like(centre)
     residual, direction, found = [one], [one], []
     norm = gram[(0, 0)]
     for repeat in range(ITERS):
         size = len(direction)
+        step = norm / (quadratic(images, direction) if repeat else images[(0, 0)])
         image = [centre * direction[0]]
         for j in range(1, size):
             image.append(centre * direction[j] + scale * direction[j - 1])
         image.append(scale * direction[size - 1])
-        step = norm / inner(direction, image)
         found = [
             (found[j] if j < len(found) else 0.0) + step * direction[j] for j in range(size)
         ]
@@ -316,17 +379,17 @@
             (residual[j] if j < size else 0.0) - step * image[j] for j in range(size + 1)
         ]
         if repeat + 1 < ITERS:
-            fresh = inner(residual, residual)
-            ratio = fresh / norm
+            inverse = 1.0 / norm
+            norm = quadratic(norms, residual)
+            ratio = norm * inverse
             direction = [
                 residual[j] + (ratio * direction[j] if j < size else 0.0) for j in range(size + 1)
             ]
-            norm = fresh
     return found, residual
 
 
 def final_kernel(kinds, messages, v0, v1, v2, right, left_next, tab, coarse, corners,
-                 solution_hbm, interface_out, found_book, solution_out, sems):
+                 solution_hbm, interface_hbm, book, solution_out, interface_out, sems):
     comp, py, px = v0.shape[0], v0.shape[2], v0.shape[3]
     depth = right.shape[1]
     n_in, n_sub = lax.axis_size("in"), lax.axis_size("sub")
@@ -334,31 +397,22 @@
     following = lax.rem(sub + 1, n_sub)
     slab = Slab(comp, py, px)
     base = kinds * comp * comp
-    mean, scale = tab[pl.ds(base + 8, 1)][:, :1], tab[pl.ds(base + 16, 1)][:, :1]
 
     got = [messages[pl.ds(i, n_sub, stride=n_in)] for i in range(n_in)]
-    summed = got[0]
-    for i in range(1, n_in):
-        summed = summed + got[i]
+    summed = total_of(got)
+    mean = jnp.broadcast_to(tab[pl.ds(base + 8, 1)], summed.shape)
+    scale = jnp.broadcast_to(tab[pl.ds(base + 16, 1)], summed.shape)
     gram = {}
     for g, pair in enumerate(PAIRS):
-        gram[pair] = summed[:, GRAM_LANE + g : GRAM_LANE + g + 1]
-    found, residual = coefficients(gram, mean, scale)
-
-    lane = lax.broadcasted_iota(jnp.int32, summed.shape, 1)
-    kind = lax.rem(lane, 8) // 2
-    spread = jnp.zeros_like(summed)
-    sheet = jnp.zeros_like(summed)
-    for k in range(ITERS + 1):
-        spread = jnp.where(kind == k, residual[k], spread)
-        sheet = jnp.where(lane == k, residual[k], sheet)
-    for k in range(ITERS):
-        sheet = jnp.where(lane == ITERS + 1 + k, found[k], sheet)
-    found_book[...] = sheet
-    mine = found_book[pl.ds(sub, 1)]
-    other = found_book[pl.ds(following, 1)]
-
-    weights = [jnp.broadcast_to(mine[:, ITERS + 1 + k : ITERS + 2 + k], (8, px)) for k in range(ITERS)]
+        gram[pair] = jnp.broadcast_to(summed[:, GRAM_LANE + g : GRAM_LANE + g + 1], summed.shape)
+    found, residual = coefficients(gram, 6.0 + mean, scale)
+
+    for k, value in enumerate(residual + found):
+        book[k] = value
+    weights = [book[ITERS + 1 + k, pl.ds(sub, 8, stride=0)] for k in range(ITERS)]
+    mine = [book[k, pl.ds(sub, depth, stride=0)] for k in range(ITERS + 1)]
+    other = [book[k, pl.ds(following, depth, stride=0)] for k in range(ITERS + 1)]
+
     copies = [
         pltpu.make_async_copy(solution_out.at[:, z], solution_hbm.at[:, z], sems.at[z]) for z in range(depth)
     ]
@@ -370,6 +424,11 @@
                 solution_out[c, z, pl.ds(r, 8, stride=slab.parts)] = total
         copies[z].start()
 
+    lane = lax.broadcasted_iota(jnp.int32, summed.shape, 1)
+    kind = lax.rem(lane, 8) // 2
+    spread = residual[0]
+    for k in range(1, ITERS + 1):
+        spread = jnp.where(kind == k, residual[k], spread)
     count = corners.shape[1]
     spots = jnp.minimum(lane * 8, px - 1)
     values = []
@@ -382,7 +441,7 @@
 
     face = None
     for k in range(ITERS + 1):
-        part = mine[:, k : k + 1] * right[k] + other[:, k : k + 1] * left_next[k]
+        part = mine[k] * right[k] + other[k] * left_next[k]
         face = part if face is None else face + part
 
     zs = lax.broadcasted_iota(jnp.int32, face.shape, 0)
@@ -401,6 +460,8 @@
         face = face + jnp.where(flat == picks[:, j : j + 1], value, 0.0)
     for c in range(comp):
         interface_out[0, c] = face[:, py * c : py * (c + 1)]
+    copies.append(pltpu.make_async_copy(interface_out, interface_hbm, sems.at[depth]))
+    copies[depth].start()
     for copy in copies:
         copy.wait()
 
@@ -454,29 +515,41 @@
         shape((comp * comp, depth + 2 * MAT_DEPTH, py, px), f32),
         shape((depth, comp * py, px), f32),
     )
-    *inner, tab = pl.pallas_call(
+    fields += (shape((len(PAIRS), 8, px), f32),)
+    *inner, tab, v3 = pl.pallas_call(
         interior_kernel,
-        out_shape=(*fields, shape((len(PAIRS), 8, px), f32), shape((kinds * comp * comp + 24, px), f32)),
+        out_shape=(
+            *fields, shape((kinds * comp * comp + 24, px), f32), shape((comp, 2, py, px), f32)),
         in_specs=[VMEM] * 3,
-        out_specs=(VMEM,) * 7,
+        out_specs=(VMEM,) * 8,
         compiler_params=params(4),
         name="interior",
     )(body, mats, table)
 
+    inner = pl.pallas_call(
+        functools.partial(near_kernel, kinds),
+        out_shape=fields,
+        in_specs=[VMEM] * 9,
+        out_specs=(VMEM,) * 6,
+        input_output_aliases={3 + k: k for k in range(6)},
+        compiler_params=params(4),
+        name="near",
+    )(halo_a, tab, v3, *inner)
+
     v0, v1, v2, _, packed, message = pl.pallas_call(
-        functools.partial(edge_kernel, kinds),
-        out_shape=(*fields, shape((devices, LANES), f32)),
+        functools.partial(far_kernel, kinds),
+        out_shape=(*fields[:5], shape((devices, LANES), f32)),
         in_specs=[VMEM] * 3 + [HBM] * 2 + [VMEM] * 6,
         out_specs=(VMEM,) * 6,
-        input_output_aliases={5: 0, 6: 1, 7: 2, 8: 3, 9: 4},
+        input_output_aliases={5 + k: k for k in range(5)},
         scratch_shapes=[
             pltpu.SMEM((count,), jnp.int32),
             pltpu.SMEM((count,), jnp.int32),
             pltpu.SemaphoreType.DMA((2,)),
         ],
         compiler_params=params(4),
-        name="edge",
-    )(halo_a, halo_b, tab, hbm(corner_index), before, *inner)
+        name="far",
+    )(halo_b, tab, v3, hbm(corner_index), before, *inner)
 
     messages = lax.all_to_all(message, ("sub", "in"), 0, 0, tiled=True)
     faces = shape((ITERS + 1, depth, comp * py), f32)
@@ -494,11 +567,12 @@
         functools.partial(final_kernel, kinds),
         out_shape=(shape(body_load.shape, f32), shape((1, comp, depth, py), f32)),
         in_specs=[VMEM] * 9,
-        out_specs=(HBM, VMEM),
+        out_specs=(HBM, HBM),
         scratch_shapes=[
-            pltpu.VMEM((n_sub, LANES), f32),
+            pltpu.VMEM((2 * ITERS + 1, n_sub, LANES), f32),
             pltpu.VMEM(body_load.shape, f32),
-            pltpu.SemaphoreType.DMA((depth,)),
+            pltpu.VMEM((1, comp, depth, py), f32),
+            pltpu.SemaphoreType.DMA((depth + 1,)),
         ],
         compiler_params=params(16),
         name="final",

time: 32.4 us -> 29.5 us (0.910)
  Pallas kernels: 10.1 us -> 8.84 us
  starting transfers between devices: 14.5 us -> 13.4 us
  waiting for transfers between devices: 6.74 us -> 6.09 us
    ppermute x1, waiting for transfers between devices: 1.63 us -> 0.01 us  [on_device(): lax.ppermute(corner_index, 'sub', [(i, (i + 1) % n_sub) for i in range(n_...]
    pallas_call x1, Pallas kernels: 2.93 us -> 1.31 us  [on_device(): pl.pallas_call(functools.partial(final_kernel, kinds), out_shape=(shape(b...]
    all_to_all x1, starting transfers between devices: 8.18 us -> 7.16 us  [on_device(): messages = lax.all_to_all(message, ('sub', 'in'), 0, 0, tiled=True)]
    ppermute x1, waiting for transfers between devices: 0.85 us -> 1.82 us  [on_device(): halo_a = lax.ppermute(send_a, 'in', swaps(0))]
    pallas_call x2 -> x3, Pallas kernels: 5.54 us -> 5.85 us  [the longest x1 3.03 us: on_device(): pl.pallas_call(interior_kernel, out_shape=(*fields, shape((kinds * comp *...]
  transfers between devices with their start and end apart: 5 -> 5, of which waited for: 4 -> 3; matrix products, arithmetic and copies ran while one was open for 1% -> 1% of each run, Pallas kernels for 8% -> 14%
where the time goes in v3:
time: 29.5 us; the launch traced here: 29.3 us
  starting transfers between devices  13.4 us (45%)
  Pallas kernels  8.84 us (30%)
  waiting for transfers between devices  6.09 us (21%)
  between operations  0.74 us (3%)
    all_to_all x1, starting transfers between devices, on_device(): messages = lax.all_to_all(message, ('sub', 'in'), 0, 0, tiled=True)  7.16 us
    ppermute x1, starting transfers between devices, on_device(): halo_a = lax.ppermute(send_a, 'in', swaps(0))  3.12 us
    all_to_all x1, waiting for transfers between devices, on_device(): messages = lax.all_to_all(message, ('sub', 'in'), 0, 0, tiled=True)  3.04 us
    pallas_call x1, Pallas kernels, on_device(): pl.pallas_call(interior_kernel, out_shape=(*fields, shape((kinds * comp *...  3.03 us
    ppermute x1, starting transfers between devices, on_device(): lax.ppermute(left, 'sub', [((i + 1) % n_sub, i) for i in range(n_sub)])  2.44 us
    pallas_call x1, Pallas kernels, on_device(): pl.pallas_call(functools.partial(far_kernel, kinds), out_shape=(*fields[:...  1.85 us
    ppermute x1, waiting for transfers between devices, on_device(): halo_a = lax.ppermute(send_a, 'in', swaps(0))  1.82 us
    pallas_call x1, Pallas kernels, on_device(): pl.pallas_call(pack_kernel, out_shape=(halo, halo, shape(body_load.shape,...  1.48 us
  transfers between devices with their start and end apart: 5, of which 3 were waited for; matrix products, arithmetic and copies ran while one was open for 1% of the time, Pallas kernels for 14%

profile of v3, /device:TPU:0, one launch (start us, length us, event | category | flops | bytes accessed | tf_op | source)
XLA Modules:
  0.0 29.3 jit_solution(2344253654263157619)
XLA Ops:
  0.6 1.5 %pack.1 = (f32[14,32,128]{2,1,0:T(8,128)S(1)}, f32[14,32,128]{2,1,0:T(8,128)S(1)}, f32[4,8,32,128]{3,2,1,0:T(8,128)S(1)}, s32[8,32,128]{2,1,0:T(8,128)S(1)}, f32[16,8]{1,0:T(8,128)S(1)}) custom-call(f32[4,8,32,128]{3,2,1,0:T(8,128)} %body.1, s32[8,32,128]{2,1,0:T(8,128)} %mats.1, f32[16,8]{1,0:T(8,128)} %bitcast.14), custom_call_target="tpu_custom_call" | custom-call | tf_op jit(solution)/shard_map/pack/pallas_call | solution.py:489
  2.1 3.1 %collective-permute-start.2 = (f32[14,32,128]{2,1,0:T(8,128)S(1)}, f32[14,32,128]{2,1,0:T(8,128)S(1)}, u32[]{:S(2)}, u32[]{:S(2)}) collective-permute-start(f32[14,32,128]{2,1,0:T(8,128)S(1)} %get-tuple-element.34), channel_id=1, source_target_pairs={{0,1},{2,3},{1,0},{3,2},{4,5},{6,7},{5,4},{7,6},{8,9},{10,11},{9,8... | collective-permute-start | bytes 688136 | tf_op jit(solution)/shard_map/ppermute | solution.py:507
  5.2 0.7 %collective-permute-start = (f32[14,32,128]{2,1,0:T(8,128)S(1)}, f32[14,32,128]{2,1,0:T(8,128)S(1)}, u32[]{:S(2)}, u32[]{:S(2)}) collective-permute-start(f32[14,32,128]{2,1,0:T(8,128)S(1)} %get-tuple-element.28), channel_id=1, source_target_pairs={{1,2},{2,1},{5,6},{6,5},{9,10},{10,9},{13,14},{14,13},{17,18},{18,... | collective-permute-start | bytes 688136 | tf_op jit(solution)/shard_map/ppermute | solution.py:508
  5.9 0.1 collective-permute-start.1
  6.0 3.0 %interior.1 = (f32[4,14,32,128]{3,2,1,0:T(8,128)S(1)}, f32[4,12,32,128]{3,2,1,0:T(8,128)S(1)}, f32[4,10,32,128]{3,2,1,0:T(8,128)S(1)}, f32[16,12,32,128]{3,2,1,0...) custom-call(f32[4,8,32,128]{3,2,1,0:T(8,128)S(1)} %get-tuple-element, ...), custom_call_target="tpu_custom_call" | custom-call | tf_op jit(solution)/shard_map/interior/pallas_call | solution.py:519
  9.0 1.8 %collective-permute-done.2.halo = f32[14,32,128]{2,1,0:T(8,128)S(1)} collective-permute-done((f32[14,32,128]{2,1,0:T(8,128)S(1)}, f32[14,32,128]{2,1,0:T(8,128)S(1)}, u32[]{:S(2)}, u32[]{:S(2)}) %collective-permute-start.2) | collective-permute-done | bytes 229408 | tf_op jit(solution)/shard_map/ppermute | solution.py:507
  10.8 1.0 %near.1 = (f32[4,14,32,128]{3,2,1,0:T(8,128)S(1)}, f32[4,12,32,128]{3,2,1,0:T(8,128)S(1)}, f32[4,10,32,128]{3,2,1,0:T(8,128)S(1)}, f32[16,12,32,128]{3,2,1,0:T(8...) custom-call(f32[14,32,128]{2,1,0:T(8,128)S(1)} %collective-permute-d, ...), custom_call_target="tpu_custom_call", output_to_operand_aliasing={{0}: (3, {}), {1}: (4, {}), {2}: (5, {}), {3}: (6, {}), {4}... | custom-call | tf_op jit(solution)/shard_map/near/pallas_call | solution.py:529
  11.8 0.0 collective-permute-done.1.before_hbm
  11.8 0.0 collective-permute-done.halo
  11.8 0.0 copy-start.1
  11.8 0.0 copy-start
  11.9 1.9 %far.1 = (f32[4,14,32,128]{3,2,1,0:T(8,128)S(1)}, f32[4,12,32,128]{3,2,1,0:T(8,128)S(1)}, f32[4,10,32,128]{3,2,1,0:T(8,128)S(1)}, f32[16,12,32,128]{3,2,1,0:T(8,...) custom-call(f32[14,32,128]{2,1,0:T(8,128)S(1)} %collective-permute-d, ...), custom_call_target="tpu_custom_call", output_to_operand_aliasing={{0}: (5, {}), {1}: (6, {}), {2}: (7, {}), {3}: (8, {}), {4}... | custom-call | tf_op jit(solution)/shard_map/far/pallas_call | solution.py:539
  13.7 7.2 %all-to-all-start = ((f32[32,1,128]{2,1,0:T(1,128)}), f32[32,1,128]{2,1,0:T(1,128)S(1)}, u32[]{:S(2)}, u32[]{:S(2)}) async-start(f32[32,1,128]{2,1,0:T(1,128)} %bitcast.3), calls=%async_computation | async-start | bytes 32768 | tf_op jit(solution)/shard_map/all_to_all | solution.py:554
  20.9 0.2 faces.1
  21.1 2.4 %collective-permute-start.3 = (f32[4,8,128]{2,1,0:T(8,128)S(1)}, f32[4,8,128]{2,1,0:T(8,128)S(1)}, u32[]{:S(2)}, u32[]{:S(2)}) collective-permute-start(f32[4,8,128]{2,1,0:T(8,128)S(1)} %get-tuple-element.53), channel_id=1, source_target_pairs={{4,0},{8,4},{12,8},{16,12},{20,16},{24,20},{28,24},{0,28},{5,1},{9... | collective-permute-start | bytes 49160 | tf_op jit(solution)/shard_map/ppermute | solution.py:564
  23.5 0.0 copy-done.1
  23.5 0.2 reshape.16
  23.7 1.2 %collective-permute-done.3.left_next = f32[4,8,128]{2,1,0:T(8,128)S(1)} collective-permute-done((f32[4,8,128]{2,1,0:T(8,128)S(1)}, f32[4,8,128]{2,1,0:T(8,128)S(1)}, u32[]{:S(2)}, u32[]{:S(2)}) %collective-permute-start.3) | collective-permute-done | bytes 16416 | tf_op jit(solution)/shard_map/ppermute | solution.py:564
  25.0 3.0 %all-to-all-done = f32[32,1,128]{2,1,0:T(1,128)S(1)} async-done(((f32[32,1,128]{2,1,0:T(1,128)}), f32[32,1,128]{2,1,0:T(1,128)S(1)}, u32[]{:S(2)}, u32[]{:S(2)}) %all-to-all-start) | async-done | bytes 16416 | tf_op jit(solution)/shard_map/all_to_all | solution.py:554
  28.0 0.0 copy-done
  28.0 1.3 %final.1 = (f32[4,8,32,128]{3,2,1,0:T(8,128)}, f32[1,4,8,32]{3,2,1,0:T(8,128)}) custom-call(f32[32,128]{1,0:T(8,128)S(1)} %bitcast.12, f32[4,14,32,128]{3,2,1,0:T(8,128)S(1)} %get-tuple-element.48.v0, f32[4,12,32,128]{3,2,1,0:T(8,128)S(1)} %get-tuple-element.49.v1, f32[4,10,32,128]{3,2,1,0:T(8,128)S(1)} %get-tuple-element.50.v2, ...), custom_call_target="tpu_custom_call" | custom-call | tf_op jit(solution)/shard_map/final/pallas_call | solution.py:566
  (1 shorter events, 0.0 us)
Async XLA Ops:
  2.1 8.7 %collective-permute-start.2 = (f32[14,32,128]{2,1,0:T(8,128)S(1)}, f32[14,32,128]{2,1,0:T(8,128)S(1)}, u32[]{:S(2)}, u32[]{:S(2)}) collective-permute-start(f32[14,32,128]{2,1,0:T(8,128)S(1)} %get-tuple-element.34), channel_id=1, source_target_pairs={{0,1},{2,3},{1,0},{3,2},{4,5},{6,7},{5,4},{7,6},{8,9},{10,11},{9,8... | collective-permute-start | bytes 688136 | tf_op jit(solution)/shard_map/ppermute | solution.py:507
  5.2 6.6 %collective-permute-start = (f32[14,32,128]{2,1,0:T(8,128)S(1)}, f32[14,32,128]{2,1,0:T(8,128)S(1)}, u32[]{:S(2)}, u32[]{:S(2)}) collective-permute-start(f32[14,32,128]{2,1,0:T(8,128)S(1)} %get-tuple-element.28), channel_id=1, source_target_pairs={{1,2},{2,1},{5,6},{6,5},{9,10},{10,9},{13,14},{14,13},{17,18},{18,... | collective-permute-start | bytes 688136 | tf_op jit(solution)/shard_map/ppermute | solution.py:508
  5.9 5.9 %collective-permute-start.1 = (s32[8]{0:T(128)}, s32[8]{0:T(128)S(1)}, u32[]{:S(2)}, u32[]{:S(2)}) collective-permute-start(s32[8]{0:T(128)} %corners_hbm.1), channel_id=1, source_target_pairs={{0,4},{4,8},{8,12},{12,16},{16,20},{20,24},{24,28},{28,0},{1,5},{5... | collective-permute-start | bytes 104 | tf_op jit(solution)/shard_map/ppermute | solution.py:509
  11.8 11.7 %copy-start.1 = (f32[8,256]{1,0:T(8,128)S(1)}, f32[8,256]{1,0:T(8,128)}, u32[]{:S(2)}) copy-start(f32[8,256]{1,0:T(8,128)} %param.9) | copy-start | bytes 24580
  11.8 16.2 %copy-start = (s32[8]{0:T(128)S(1)}, s32[8]{0:T(128)}, u32[]{:S(2)}) copy-start(s32[8]{0:T(128)} %corners_hbm.1) | copy-start | bytes 100
  13.7 14.3 %all-to-all-start = ((f32[32,1,128]{2,1,0:T(1,128)}), f32[32,1,128]{2,1,0:T(1,128)S(1)}, u32[]{:S(2)}, u32[]{:S(2)}) async-start(f32[32,1,128]{2,1,0:T(1,128)} %bitcast.3), calls=%async_computation | async-start | bytes 32768 | tf_op jit(solution)/shard_map/all_to_all | solution.py:554
  21.1 3.9 %collective-permute-start.3 = (f32[4,8,128]{2,1,0:T(8,128)S(1)}, f32[4,8,128]{2,1,0:T(8,128)S(1)}, u32[]{:S(2)}, u32[]{:S(2)}) collective-permute-start(f32[4,8,128]{2,1,0:T(8,128)S(1)} %get-tuple-element.53), channel_id=1, source_target_pairs={{4,0},{8,4},{12,8},{16,12},{20,16},{24,20},{28,24},{0,28},{5,1},{9... | collective-permute-start | bytes 49160 | tf_op jit(solution)/shard_map/ppermute | solution.py:564

commit v4 on v3

--- a/solution.py
+++ b/solution.py
@@ -38,27 +38,27 @@
     return lax.shift_right_logical(index, size.bit_length() - 1), index & (size - 1)
 
 
-def pack_kernel(body, mats, table, a_out, b_out, body_out, mats_out, table_out, kinds, sems, whole):
+def pack_kernel(body, mats, table, a_out, b_out, middle_out, mats_out, table_out, sems, rest):
     comp, depth = body.shape[0], body.shape[1]
     odd = lax.rem(lax.axis_index("in"), 2)
+    sides = ((a_out, odd), (b_out, 1 - odd))
     copies = []
-    for slot, (out, low) in enumerate(((a_out, odd), (b_out, 1 - odd))):
-        first = (1 - low) * (depth - MAT_DEPTH)
-        copies.append(pltpu.make_async_copy(
-            mats.at[pl.ds(first, MAT_DEPTH)], kinds.at[slot], sems.at[slot, comp]))
+    for slot, (out, low) in enumerate(sides):
         first = (1 - low) * (depth - ITERS)
         for c in range(comp):
             copies.append(pltpu.make_async_copy(
                 body.at[c, pl.ds(first, ITERS)], out.at[pl.ds(ITERS * c, ITERS)], sems.at[slot, c]))
-    copies.append(pltpu.make_async_copy(table, table_out, whole.at[0]))
-    copies.append(pltpu.make_async_copy(mats, mats_out, whole.at[1]))
-    copies.append(pltpu.make_async_copy(body, body_out, whole.at[2]))
+    copies.append(pltpu.make_async_copy(mats, mats_out, rest.at[0]))
+    copies.append(pltpu.make_async_copy(body.at[:, pl.ds(ITERS, depth - 2 * ITERS)], middle_out, rest.at[1]))
+    copies.append(pltpu.make_async_copy(table, table_out, rest.at[2]))
     for copy in copies:
         copy.start()
     for copy in copies:
         copy.wait()
-    for slot, out in enumerate((a_out, b_out)):
-        out[pl.ds(ITERS * comp, MAT_DEPTH)] = kinds[slot].astype(jnp.float32)
+    for out, low in sides:
+        first = (1 - low) * (depth - MAT_DEPTH)
+        for t in range(MAT_DEPTH):
+            out[ITERS * comp + t] = mats_out[first + t].astype(jnp.float32)
 
 
 class Slab:
@@ -128,17 +128,8 @@
                 out.append(level[0])
             self.store(gains, out, e, at)
 
-    def pack(self, packed, z, c, basis):
-        rows = self.parts * 8
-        for r in range(self.parts):
-            block = basis[0][r]
-            for k in range(1, len(basis)):
-                here = (self.lane == 2 * k) | (self.lane == 2 * k - 1)
-                block = jnp.where(here, pltpu.roll(basis[k][r], 2 * k, 1), block)
-            packed[z, pl.ds(rows * c + 8 * r, 8)] = block
-
-
-def levels(slab, v0, v1, v2, gains, packed, inverse):
+
+def levels(slab, v0, v1, v2, v3, gains, inverse):
     def first(z, sums):
         g01, g11 = sums
         for c, v, w in slab.applied(v0, z + 3, gains, z + 2, inverse):
@@ -158,15 +149,17 @@
         g03, g13, g23 = sums
         for c, v, w in slab.applied(v2, z + 1, gains, z + 2, inverse):
             t, u = slab.load(v0, c, z + 3), slab.load(v1, c, z + 2)
-            slab.pack(packed, z, c, (t, u, v, w))
+            slab.store(v3, w, c, z)
             g03, g13, g23 = slab.products(g03, t, w), slab.products(g13, u, w), slab.products(g23, v, w)
         return g03, g13, g23
 
     return first, second, third
 
 
-def interior_kernel(body, mats, table, v0, v1, v2, gains, packed, gram, tab, v3):
-    comp, depth, py, px = body.shape
+def interior_kernel(side_a, side_b, middle, mats, table, v0, v1, v2, v3, gains, gram, tab):
+    comp, _, py, px = middle.shape
+    depth = mats.shape[0]
+    odd = lax.rem(lax.axis_index("in"), 2) == 1
     kinds = table.shape[1]
     entries = comp * comp
     slab = Slab(comp, py, px)
@@ -182,14 +175,25 @@
         for at in (ITERS - 1, ITERS + depth):
             slab.store(v0, [zero] * slab.parts, c, at)
 
-    def own(z, g00):
+    def place(values, z, g00):
         for c in range(comp):
-            value = slab.natural(body, c, z)
-            slab.store(v0, value, c, ITERS + z)
-            g00 = slab.products(g00, value, value)
+            slab.store(v0, values[c], c, ITERS + z)
+            g00 = slab.products(g00, values[c], values[c])
         slab.look_up(slab.natural(mats, z), tab, gains, MAT_DEPTH + z, kinds)
         return g00
-    g00 = lax.fori_loop(0, depth, own, zero)
+
+    def outer(t, g00):
+        a = [slab.natural(side_a, ITERS * c + t) for c in range(comp)]
+        b = [slab.natural(side_b, ITERS * c + t) for c in range(comp)]
+        low = [[jnp.where(odd, x, y) for x, y in zip(a[c], b[c])] for c in range(comp)]
+        g00 = place(low, t, g00)
+        high = [[jnp.where(odd, y, x) for x, y in zip(a[c], b[c])] for c in range(comp)]
+        return place(high, depth - ITERS + t, g00)
+
+    def centre(m, g00):
+        return place([slab.natural(middle, c, m) for c in range(comp)], ITERS + m, g00)
+    g00 = lax.fori_loop(0, ITERS, outer, zero)
+    g00 = lax.fori_loop(0, depth - 2 * ITERS, centre, g00)
 
     def partial(i, carry):
         z = i * (depth - 1)
@@ -206,10 +210,10 @@
     def partial_third(i, carry):
         z = 2 + i * (depth - 5)
         for c, _, w in slab.applied(v2, z + 1, gains, z + 2, inverse):
-            slab.store(v3, w, c, i)
+            slab.store(v3, w, c, z)
         return carry
 
-    first, second, third = levels(slab, v0, v1, v2, gains, packed, inverse)
+    first, second, third = levels(slab, v0, v1, v2, v3, gains, inverse)
     lax.fori_loop(0, 2, partial, 0)
     g01, g11 = lax.fori_loop(1, depth - 1, first, (zero,) * 2)
     lax.fori_loop(0, 2, partial_second, 0)
@@ -220,9 +224,9 @@
         gram[g] = value
 
 
-def one_side(kinds, slot, halo, tab, v3, gram, v0, v1, v2, gains, packed):
+def one_side(kinds, slot, halo, tab, gram, v0, v1, v2, v3, gains):
     comp, py, px = v0.shape[0], v0.shape[2], v0.shape[3]
-    depth = packed.shape[0]
+    depth = v3.shape[1]
     slab = Slab(comp, py, px)
     place = lax.axis_index("in")
     low = lax.rem(place + 1 + slot, 2) == 0
@@ -246,7 +250,7 @@
     lax.fori_loop(0, MAT_DEPTH, halo_gains, 0)
 
     g00, g01, g02, g03, g11, g12, g13, g22, g23 = [gram[g] for g in range(len(PAIRS))]
-    first, second, third = levels(slab, v0, v1, v2, gains, packed, inverse)
+    first, second, third = levels(slab, v0, v1, v2, v3, gains, inverse)
 
     def first_halo(i, carry):
         z = layer(i - 2)
@@ -256,7 +260,6 @@
     lax.fori_loop(0, 2, first_halo, 0)
 
     z0, z1, z2, out = layer(0), layer(1), layer(2), layer(-1)
-    side = jnp.where(low, 0, 1)
 
     def mend(c, sums):
         g01, g11, g02, g12, g22, g03, g13, g23 = sums
@@ -271,9 +274,9 @@
         g12 = slab.products(g12, slab.load(v1, c, z1 + 2), w)
         g22 = slab.products(g22, w, w)
         term = [inverse * x for x in term]
-        w = [a - b for a, b in zip(slab.load(v3, c, side), term)]
+        w = [a - b for a, b in zip(slab.load(v3, c, z2), term)]
+        slab.store(v3, w, c, z2)
         t, u, v = slab.load(v0, c, z2 + 3), slab.load(v1, c, z2 + 2), slab.load(v2, c, z2 + 1)
-        slab.pack(packed, z2, c, (t, u, v, w))
         g03, g13, g23 = slab.products(g03, t, w), slab.products(g13, u, w), slab.products(g23, v, w)
         return g01, g11, g02, g12, g22, g03, g13, g23
     sums = (g01, g11, g02, g12, g22, g03, g13, g23)
@@ -288,15 +291,14 @@
     return g00, g01, g02, g03, g11, g12, g13, g22, g23
 
 
-def near_kernel(kinds, halo, tab, v3, v0_in, v1_in, v2_in, gains_in, packed_in, gram_in,
-                v0, v1, v2, gains, packed, gram):
-    sums = one_side(kinds, 0, halo, tab, v3, gram_in, v0, v1, v2, gains, packed)
+def near_kernel(kinds, halo, tab, v0_in, v1_in, v2_in, v3_in, gains_in, gram_in, v0, v1, v2, v3, gains, gram):
+    sums = one_side(kinds, 0, halo, tab, gram_in, v0, v1, v2, v3, gains)
     for g, value in enumerate(sums):
         gram[g] = value
 
 
-def far_kernel(kinds, halo, tab, v3, corners_hbm, before_hbm, v0_in, v1_in, v2_in, gains_in, packed_in, gram_in,
-               v0, v1, v2, gains, packed, message, corners, before, sems):
+def far_kernel(kinds, halo, tab, corners_hbm, before_hbm, v0_in, v1_in, v2_in, v3_in, gains_in, gram_in,
+               v0, v1, v2, v3, gains, message, corners, before, sems):
     fetch = (
         pltpu.make_async_copy(corners_hbm, corners, sems.at[0]),
         pltpu.make_async_copy(before_hbm, before, sems.at[1]),
@@ -304,12 +306,11 @@
     for copy in fetch:
         copy.start()
     py, px = v0.shape[2], v0.shape[3]
-    depth, parts = packed.shape[0], py // 8
-    sums = one_side(kinds, 1, halo, tab, v3, gram_in, v0, v1, v2, gains, packed)
+    depth, parts = v3.shape[1], py // 8
+    sums = one_side(kinds, 1, halo, tab, gram_in, v0, v1, v2, v3, gains)
 
     spots = lax.broadcasted_iota(jnp.int32, (1, px), 1)
     line = jnp.zeros((1, px), jnp.float32)
-    even = lax.rem(spots, 2) == 0
     for g, value in enumerate(sums):
         total = jnp.sum(jnp.sum(value, axis=0, keepdims=True), axis=1, keepdims=True)
         line = jnp.where(spots == GRAM_LANE + g, total, line)
@@ -317,28 +318,28 @@
     for copy in fetch:
         copy.wait()
 
-    def corner_row(index):
+    def corner_rows(index):
         c, rest = split(index, depth * py)
         z, y = split(rest, py)
         t, r = split(y, parts)
-        return packed[z, pl.ds(c * py + r * 8 + t, 1)]
+        row = pl.ds(r * 8 + t, 1)
+        return [field[c, z + ITERS - k, row] for k, field in enumerate((v0, v1, v2, v3))]
 
     for j in range(corners.shape[0]):
-        mine = corner_row(corners[j])
-        other = corner_row(before[j])
-        moved = pltpu.roll(jnp.where(even, other, mine), 8 * j + 1, 1)
-        line = jnp.where(spots // 8 == j, moved, line)
+        rows = zip(corner_rows(corners[j]), corner_rows(before[j]))
+        for k, (mine, other) in enumerate(rows):
+            moved = pltpu.roll(jnp.where(spots == px - 1, mine, other), 8 * j + 2 * k + 1, 1)
+            line = jnp.where(spots // 2 == 4 * j + k, moved, line)
     message[...] = jnp.broadcast_to(line, message.shape)
 
 
-def faces_kernel(packed, left, right):
-    depth, _, px = packed.shape
+def faces_kernel(v0, v1, v2, v3, left, right):
+    comp, depth, py, px = v3.shape
     for z in range(depth):
-        turned = packed[z].T
-        for k in range(ITERS + 1):
-            at = (2 * k - 1) % px
-            left[k, pl.ds(z, 1)] = turned[2 * k : 2 * k + 1]
-            right[k, pl.ds(z, 1)] = turned[at : at + 1]
+        for k, field in enumerate((v0, v1, v2, v3)):
+            turned = jnp.concatenate([field[c, z + ITERS - k] for c in range(comp)], axis=0).T
+            left[k, pl.ds(z, 1)] = turned[0:1]
+            right[k, pl.ds(z, 1)] = turned[px - 1 : px]
 
 
 def total_of(terms):
@@ -486,14 +487,14 @@
     def hbm(x):
         return pltpu.with_memory_space_constraint(x, pltpu.HBM)
 
-    send_a, send_b, body, mats, table = pl.pallas_call(
+    send_a, send_b, middle, mats, table = pl.pallas_call(
         pack_kernel,
-        out_shape=(halo, halo, shape(body_load.shape, f32), shape(materials.shape, jnp.int32), shape(table.shape, f32)),
+        out_shape=(
+            halo, halo, shape((comp, depth - 2 * ITERS, py, px), f32), shape(materials.shape, jnp.int32), shape(table.shape, f32)),
         in_specs=[HBM] * 3,
         out_specs=(VMEM,) * 5,
         scratch_shapes=[
-            pltpu.VMEM((2, MAT_DEPTH, py, px), jnp.int32),
-            pltpu.SemaphoreType.DMA((2, comp + 1)),
+            pltpu.SemaphoreType.DMA((2, comp)),
             pltpu.SemaphoreType.DMA((3,)),
         ],
         compiler_params=params(4),
@@ -512,36 +513,35 @@
         shape((comp, depth + 2 * ITERS, py, px), f32),
         shape((comp, depth + 2 * ITERS - 2, py, px), f32),
         shape((comp, depth + 2 * ITERS - 4, py, px), f32),
+        shape((comp, depth, py, px), f32),
         shape((comp * comp, depth + 2 * MAT_DEPTH, py, px), f32),
-        shape((depth, comp * py, px), f32),
+        shape((len(PAIRS), 8, px), f32),
     )
-    fields += (shape((len(PAIRS), 8, px), f32),)
-    *inner, tab, v3 = pl.pallas_call(
+    *inner, tab = pl.pallas_call(
         interior_kernel,
-        out_shape=(
-            *fields, shape((kinds * comp * comp + 24, px), f32), shape((comp, 2, py, px), f32)),
-        in_specs=[VMEM] * 3,
-        out_specs=(VMEM,) * 8,
+        out_shape=(*fields, shape((kinds * comp * comp + 24, px), f32)),
+        in_specs=[VMEM] * 5,
+        out_specs=(VMEM,) * 7,
         compiler_params=params(4),
         name="interior",
-    )(body, mats, table)
+    )(send_a, send_b, middle, mats, table)
 
     inner = pl.pallas_call(
         functools.partial(near_kernel, kinds),
         out_shape=fields,
-        in_specs=[VMEM] * 9,
+        in_specs=[VMEM] * 8,
         out_specs=(VMEM,) * 6,
-        input_output_aliases={3 + k: k for k in range(6)},
+        input_output_aliases={2 + k: k for k in range(6)},
         compiler_params=params(4),
         name="near",
-    )(halo_a, tab, v3, *inner)
-
-    v0, v1, v2, _, packed, message = pl.pallas_call(
+    )(halo_a, tab, *inner)
+
+    v0, v1, v2, v3, _, message = pl.pallas_call(
         functools.partial(far_kernel, kinds),
         out_shape=(*fields[:5], shape((devices, LANES), f32)),
-        in_specs=[VMEM] * 3 + [HBM] * 2 + [VMEM] * 6,
+        in_specs=[VMEM] * 2 + [HBM] * 2 + [VMEM] * 6,
         out_specs=(VMEM,) * 6,
-        input_output_aliases={5 + k: k for k in range(5)},
+        input_output_aliases={4 + k: k for k in range(5)},
         scratch_shapes=[
             pltpu.SMEM((count,), jnp.int32),
             pltpu.SMEM((count,), jnp.int32),
@@ -549,18 +549,18 @@
         ],
         compiler_params=params(4),
         name="far",
-    )(halo_b, tab, v3, hbm(corner_index), before, *inner)
+    )(halo_b, tab, hbm(corner_index), before, *inner)
 
     messages = lax.all_to_all(message, ("sub", "in"), 0, 0, tiled=True)
     faces = shape((ITERS + 1, depth, comp * py), f32)
     left, right = pl.pallas_call(
         faces_kernel,
         out_shape=(faces, faces),
-        in_specs=[VMEM],
+        in_specs=[VMEM] * 4,
         out_specs=(VMEM, VMEM),
         compiler_params=params(4),
         name="faces",
-    )(packed)
+    )(v0, v1, v2, v3)
     left_next = lax.ppermute(left, "sub", [((i + 1) % n_sub, i) for i in range(n_sub)])
 
     return pl.pallas_call(

time: 29.5 us -> 29.1 us (0.986)
    all_to_all x1, waiting for transfers between devices: 3.04 us -> 2.63 us  [on_device(): messages = lax.all_to_all(message, ('sub', 'in'), 0, 0, tiled=True)]
  transfers between devices with their start and end apart: 5 -> 5, of which waited for: 3 -> 3; matrix products, arithmetic and copies ran while one was open for 1% -> 1% of each run, Pallas kernels for 14% -> 15%
where the time goes in v4:
time: 29.1 us; the launch traced here: 28.9 us
  starting transfers between devices  13.6 us (47%)
  Pallas kernels  8.55 us (29%)
  waiting for transfers between devices  5.8 us (20%)
  between operations  0.74 us (3%)
    all_to_all x1, starting transfers between devices, on_device(): messages = lax.all_to_all(message, ('sub', 'in'), 0, 0, tiled=True)  7.36 us
    ppermute x1, starting transfers between devices, on_device(): halo_a = lax.ppermute(send_a, 'in', swaps(0))  3.12 us
    pallas_call x1, Pallas kernels, on_device(): pl.pallas_call(interior_kernel, out_shape=(*fields, shape((kinds * comp *...  2.92 us
    all_to_all x1, waiting for transfers between devices, on_device(): messages = lax.all_to_all(message, ('sub', 'in'), 0, 0, tiled=True)  2.63 us
    ppermute x1, starting transfers between devices, on_device(): lax.ppermute(left, 'sub', [((i + 1) % n_sub, i) for i in range(n_sub)])  2.44 us
    ppermute x1, waiting for transfers between devices, on_device(): halo_a = lax.ppermute(send_a, 'in', swaps(0))  1.94 us
    pallas_call x1, Pallas kernels, on_device(): pl.pallas_call(functools.partial(far_kernel, kinds), out_shape=(*fields[:...  1.69 us
    pallas_call x1, Pallas kernels, on_device(): pl.pallas_call(functools.partial(final_kernel, kinds), out_shape=(shape(b...  1.31 us
  transfers between devices with their start and end apart: 5, of which 3 were waited for; matrix products, arithmetic and copies ran while one was open for 1% of the time, Pallas kernels for 15%

profile of v4, /device:TPU:0, one launch (start us, length us, event | category | flops | bytes accessed | tf_op | source)
XLA Modules:
  0.0 28.9 jit_solution(8161314485092050242)
XLA Ops:
  0.6 1.2 %pack.1 = (f32[14,32,128]{2,1,0:T(8,128)S(1)}, f32[14,32,128]{2,1,0:T(8,128)S(1)}, f32[4,2,32,128]{3,2,1,0:T(8,128)S(1)}, s32[8,32,128]{2,1,0:T(8,128)S(1)}, f32[16,8]{1,0:T(8,128)S(1)}) custom-call(f32[4,8,32,128]{3,2,1,0:T(8,128)} %body.1, s32[8,32,128]{2,1,0:T(8,128)} %mats.1, f32[16,8]{1,0:T(8,128)} %bitcast.14), custom_call_target="tpu_custom_call" | custom-call | tf_op jit(solution)/shard_map/pack/pallas_call | solution.py:490
  1.9 3.1 %collective-permute-start.2 = (f32[14,32,128]{2,1,0:T(8,128)S(1)}, f32[14,32,128]{2,1,0:T(8,128)S(1)}, u32[]{:S(2)}, u32[]{:S(2)}) collective-permute-start(f32[14,32,128]{2,1,0:T(8,128)S(1)} %get-tuple-element.28.side_a), channel_id=1, source_target_pairs={{0,1},{2,3},{1,0},{3,2},{4,5},{6,7},{5,4},{7,6},{8,9},{10,11},{9,8... | collective-permute-start | bytes 688136 | tf_op jit(solution)/shard_map/ppermute | solution.py:508
  5.0 0.7 %collective-permute-start = (f32[14,32,128]{2,1,0:T(8,128)S(1)}, f32[14,32,128]{2,1,0:T(8,128)S(1)}, u32[]{:S(2)}, u32[]{:S(2)}) collective-permute-start(f32[14,32,128]{2,1,0:T(8,128)S(1)} %get-tuple-element.27.side_b), channel_id=1, source_target_pairs={{1,2},{2,1},{5,6},{6,5},{9,10},{10,9},{13,14},{14,13},{17,18},{18,... | collective-permute-start | bytes 688136 | tf_op jit(solution)/shard_map/ppermute | solution.py:509
  5.7 0.1 collective-permute-start.1
  5.7 2.9 %interior.1 = (f32[4,14,32,128]{3,2,1,0:T(8,128)S(1)}, f32[4,12,32,128]{3,2,1,0:T(8,128)S(1)}, f32[4,10,32,128]{3,2,1,0:T(8,128)S(1)}, f32[4,8,32,128]{3,2,1,0:T...) custom-call(f32[14,32,128]{2,1,0:T(8,128)S(1)} %get-tuple-element.28.side_a, ...), custom_call_target="tpu_custom_call" | custom-call | tf_op jit(solution)/shard_map/interior/pallas_call | solution.py:520
  8.7 1.9 %collective-permute-done.2.halo = f32[14,32,128]{2,1,0:T(8,128)S(1)} collective-permute-done((f32[14,32,128]{2,1,0:T(8,128)S(1)}, f32[14,32,128]{2,1,0:T(8,128)S(1)}, u32[]{:S(2)}, u32[]{:S(2)}) %collective-permute-start.2) | collective-permute-done | bytes 229408 | tf_op jit(solution)/shard_map/ppermute | solution.py:508
  10.6 0.8 %near.1 = (f32[4,14,32,128]{3,2,1,0:T(8,128)S(1)}, f32[4,12,32,128]{3,2,1,0:T(8,128)S(1)}, f32[4,10,32,128]{3,2,1,0:T(8,128)S(1)}, f32[4,8,32,128]{3,2,1,0:T(8,1...) custom-call(f32[14,32,128]{2,1,0:T(8,128)S(1)} %collective-permute-d, ...), custom_call_target="tpu_custom_call", output_to_operand_aliasing={{0}: (2, {}), {1}: (3, {}), {2}: (4, {}), {3}: (5, {}), {4}... | custom-call | tf_op jit(solution)/shard_map/near/pallas_call | solution.py:529
  11.4 0.0 collective-permute-done.1.before_hbm
  11.4 0.0 collective-permute-done.halo
  11.4 0.0 copy-start.1
  11.4 1.7 %far.1 = (f32[4,14,32,128]{3,2,1,0:T(8,128)S(1)}, f32[4,12,32,128]{3,2,1,0:T(8,128)S(1)}, f32[4,10,32,128]{3,2,1,0:T(8,128)S(1)}, f32[4,8,32,128]{3,2,1,0:T(8,12...) custom-call(f32[14,32,128]{2,1,0:T(8,128)S(1)} %collective-permute-d, ...), custom_call_target="tpu_custom_call", output_to_operand_aliasing={{0}: (4, {}), {1}: (5, {}), {2}: (6, {}), {3}: (7, {}), {4}... | custom-call | tf_op jit(solution)/shard_map/far/pallas_call | solution.py:539
  13.1 0.0 copy-start
  13.1 7.4 %all-to-all-start = ((f32[32,1,128]{2,1,0:T(1,128)}), f32[32,1,128]{2,1,0:T(1,128)S(1)}, u32[]{:S(2)}, u32[]{:S(2)}) async-start(f32[32,1,128]{2,1,0:T(1,128)} %bitcast.3), calls=%async_computation | async-start | bytes 32768 | tf_op jit(solution)/shard_map/all_to_all | solution.py:554
  20.5 0.6 %faces.1 = (f32[4,8,128]{2,1,0:T(8,128)S(1)}, f32[4,8,128]{2,1,0:T(8,128)S(1)}) custom-call(f32[4,14,32,128]{3,2,1,0:T(8,128)S(1)} %get-tuple-element.46.v0, f32[4,12,32,128]{3,2,1,0:T(8,128)S(1)} %get-tuple-element.47.v1, f32[4,10,32,128]{3,2,1,0:T(8,128)S(1)} %get-tuple-element.48.v2, f32[4,8,32,128]{3,2,1,0:T(8,128)S(1)} %get-tuple-element.49.v3), custom_call_target="tpu_custom_call" | custom-call | tf_op jit(solution)/shard_map/faces/pallas_call | solution.py:556
  21.1 2.4 %collective-permute-start.3 = (f32[4,8,128]{2,1,0:T(8,128)S(1)}, f32[4,8,128]{2,1,0:T(8,128)S(1)}, u32[]{:S(2)}, u32[]{:S(2)}) collective-permute-start(f32[4,8,128]{2,1,0:T(8,128)S(1)} %get-tuple-element.51), channel_id=1, source_target_pairs={{4,0},{8,4},{12,8},{16,12},{20,16},{24,20},{28,24},{0,28},{5,1},{9... | collective-permute-start | bytes 49160 | tf_op jit(solution)/shard_map/ppermute | solution.py:564
  23.6 0.0 copy-done.1
  23.6 0.2 reshape.16
  23.8 1.2 %collective-permute-done.3.left_next = f32[4,8,128]{2,1,0:T(8,128)S(1)} collective-permute-done((f32[4,8,128]{2,1,0:T(8,128)S(1)}, f32[4,8,128]{2,1,0:T(8,128)S(1)}, u32[]{:S(2)}, u32[]{:S(2)}) %collective-permute-start.3) | collective-permute-done | bytes 16416 | tf_op jit(solution)/shard_map/ppermute | solution.py:564
  25.0 2.6 %all-to-all-done = f32[32,1,128]{2,1,0:T(1,128)S(1)} async-done(((f32[32,1,128]{2,1,0:T(1,128)}), f32[32,1,128]{2,1,0:T(1,128)S(1)}, u32[]{:S(2)}, u32[]{:S(2)}) %all-to-all-start) | async-done | bytes 16416 | tf_op jit(solution)/shard_map/all_to_all | solution.py:554
  27.6 0.0 copy-done
  27.6 1.3 %final.1 = (f32[4,8,32,128]{3,2,1,0:T(8,128)}, f32[1,4,8,32]{3,2,1,0:T(8,128)}) custom-call(f32[32,128]{1,0:T(8,128)S(1)} %bitcast.12, f32[4,14,32,128]{3,2,1,0:T(8,128)S(1)} %get-tuple-element.46.v0, f32[4,12,32,128]{3,2,1,0:T(8,128)S(1)} %get-tuple-element.47.v1, f32[4,10,32,128]{3,2,1,0:T(8,128)S(1)} %get-tuple-element.48.v2, ...), custom_call_target="tpu_custom_call" | custom-call | tf_op jit(solution)/shard_map/final/pallas_call | solution.py:566
  (1 shorter events, 0.0 us)
Async XLA Ops:
  1.9 8.7 %collective-permute-start.2 = (f32[14,32,128]{2,1,0:T(8,128)S(1)}, f32[14,32,128]{2,1,0:T(8,128)S(1)}, u32[]{:S(2)}, u32[]{:S(2)}) collective-permute-start(f32[14,32,128]{2,1,0:T(8,128)S(1)} %get-tuple-element.28.side_a), channel_id=1, source_target_pairs={{0,1},{2,3},{1,0},{3,2},{4,5},{6,7},{5,4},{7,6},{8,9},{10,11},{9,8... | collective-permute-start | bytes 688136 | tf_op jit(solution)/shard_map/ppermute | solution.py:508
  5.0 6.4 %collective-permute-start = (f32[14,32,128]{2,1,0:T(8,128)S(1)}, f32[14,32,128]{2,1,0:T(8,128)S(1)}, u32[]{:S(2)}, u32[]{:S(2)}) collective-permute-start(f32[14,32,128]{2,1,0:T(8,128)S(1)} %get-tuple-element.27.side_b), channel_id=1, source_target_pairs={{1,2},{2,1},{5,6},{6,5},{9,10},{10,9},{13,14},{14,13},{17,18},{18,... | collective-permute-start | bytes 688136 | tf_op jit(solution)/shard_map/ppermute | solution.py:509
  5.7 5.7 %collective-permute-start.1 = (s32[8]{0:T(128)}, s32[8]{0:T(128)S(1)}, u32[]{:S(2)}, u32[]{:S(2)}) collective-permute-start(s32[8]{0:T(128)} %corners_hbm.1), channel_id=1, source_target_pairs={{0,4},{4,8},{8,12},{12,16},{16,20},{20,24},{24,28},{28,0},{1,5},{5... | collective-permute-start | bytes 104 | tf_op jit(solution)/shard_map/ppermute | solution.py:510
  11.4 12.1 %copy-start.1 = (f32[8,256]{1,0:T(8,128)S(1)}, f32[8,256]{1,0:T(8,128)}, u32[]{:S(2)}) copy-start(f32[8,256]{1,0:T(8,128)} %param.9) | copy-start | bytes 24580
  13.1 14.5 %copy-start = (s32[8]{0:T(128)S(1)}, s32[8]{0:T(128)}, u32[]{:S(2)}) copy-start(s32[8]{0:T(128)} %corners_hbm.1) | copy-start | bytes 100
  13.1 14.5 %all-to-all-start = ((f32[32,1,128]{2,1,0:T(1,128)}), f32[32,1,128]{2,1,0:T(1,128)S(1)}, u32[]{:S(2)}, u32[]{:S(2)}) async-start(f32[32,1,128]{2,1,0:T(1,128)} %bitcast.3), calls=%async_computation | async-start | bytes 32768 | tf_op jit(solution)/shard_map/all_to_all | solution.py:554
  21.1 3.9 %collective-permute-start.3 = (f32[4,8,128]{2,1,0:T(8,128)S(1)}, f32[4,8,128]{2,1,0:T(8,128)S(1)}, u32[]{:S(2)}, u32[]{:S(2)}) collective-permute-start(f32[4,8,128]{2,1,0:T(8,128)S(1)} %get-tuple-element.51), channel_id=1, source_target_pairs={{4,0},{8,4},{12,8},{16,12},{20,16},{24,20},{28,24},{0,28},{5,1},{9... | collective-permute-start | bytes 49160 | tf_op jit(solution)/shard_map/ppermute | solution.py:564

commit v5 on v4

--- a/solution.py
+++ b/solution.py
@@ -40,7 +40,7 @@
 
 def pack_kernel(body, mats, table, a_out, b_out, middle_out, mats_out, table_out, sems, rest):
     comp, depth = body.shape[0], body.shape[1]
-    odd = lax.rem(lax.axis_index("in"), 2)
+    odd = lax.rem(lax.axis_index("in") + 1, 2)
     sides = ((a_out, odd), (b_out, 1 - odd))
     copies = []
     for slot, (out, low) in enumerate(sides):
@@ -159,7 +159,7 @@
 def interior_kernel(side_a, side_b, middle, mats, table, v0, v1, v2, v3, gains, gram, tab):
     comp, _, py, px = middle.shape
     depth = mats.shape[0]
-    odd = lax.rem(lax.axis_index("in"), 2) == 1
+    odd = lax.rem(lax.axis_index("in") + 1, 2) == 1
     kinds = table.shape[1]
     entries = comp * comp
     slab = Slab(comp, py, px)
@@ -229,7 +229,7 @@
     depth = v3.shape[1]
     slab = Slab(comp, py, px)
     place = lax.axis_index("in")
-    low = lax.rem(place + 1 + slot, 2) == 0
+    low = lax.rem(place + slot, 2) == 0
     alive = jnp.where(low, place > 0, place < lax.axis_size("in") - 1).astype(jnp.float32)
     inverse = tab[pl.ds(kinds * comp * comp, 8)]
 
@@ -505,8 +505,8 @@
         pairs = [(i, i + 1) for i in range(start, n_in - 1, 2)]
         return pairs + [(j, i) for i, j in pairs]
 
-    halo_a = lax.ppermute(send_a, "in", swaps(0))
-    halo_b = lax.ppermute(send_b, "in", swaps(1))
+    halo_a = lax.ppermute(send_a, "in", swaps(1))
+    halo_b = lax.ppermute(send_b, "in", swaps(0))
     before = lax.ppermute(corner_index, "sub", [(i, (i + 1) % n_sub) for i in range(n_sub)])
 
     fields = (

time: 29.1 us -> 28.6 us (0.983)
  waiting for transfers between devices: 5.8 us -> 5.45 us
    all_to_all x1, starting transfers between devices: 7.36 us -> 4.45 us  [on_device(): messages = lax.all_to_all(message, ('sub', 'in'), 0, 0, tiled=True)]
    ppermute x2, starting transfers between devices: 3.78 us -> 6.6 us  [the longest x1 5.93 us: on_device(): halo_b = lax.ppermute(send_b, 'in', swaps(0))]
    ppermute x2, waiting for transfers between devices: 1.94 us -> 1.3 us  [the longest x1 1.3 us: on_device(): halo_b = lax.ppermute(send_b, 'in', swaps(0))]
    ppermute x1, waiting for transfers between devices: 0.01 us -> 0.3 us  [on_device(): lax.ppermute(corner_index, 'sub', [(i, (i + 1) % n_sub) for i in range(n_...]
  transfers between devices with their start and end apart: 5 -> 5, of which waited for: 3 -> 4; matrix products, arithmetic and copies ran while one was open for 1% -> 1% of each run, Pallas kernels for 15% -> 15%
where the time goes in v5:
time: 28.6 us; the launch traced here: 28.4 us
  starting transfers between devices  13.5 us (47%)
  Pallas kernels  8.54 us (30%)
  waiting for transfers between devices  5.45 us (19%)
  between operations  0.72 us (3%)
    ppermute x1, starting transfers between devices, on_device(): halo_b = lax.ppermute(send_b, 'in', swaps(0))  5.93 us
    all_to_all x1, starting transfers between devices, on_device(): messages = lax.all_to_all(message, ('sub', 'in'), 0, 0, tiled=True)  4.45 us
    pallas_call x1, Pallas kernels, on_device(): pl.pallas_call(interior_kernel, out_shape=(*fields, shape((kinds * comp *...  2.92 us
    all_to_all x1, waiting for transfers between devices, on_device(): messages = lax.all_to_all(message, ('sub', 'in'), 0, 0, tiled=True)  2.63 us
    ppermute x1, starting transfers between devices, on_device(): lax.ppermute(left, 'sub', [((i + 1) % n_sub, i) for i in range(n_sub)])  2.44 us
    pallas_call x1, Pallas kernels, on_device(): pl.pallas_call(functools.partial(far_kernel, kinds), out_shape=(*fields[:...  1.68 us
    pallas_call x1, Pallas kernels, on_device(): pl.pallas_call(functools.partial(final_kernel, kinds), out_shape=(shape(b...  1.31 us
    ppermute x1, waiting for transfers between devices, on_device(): halo_b = lax.ppermute(send_b, 'in', swaps(0))  1.3 us
  transfers between devices with their start and end apart: 5, of which 4 were waited for; matrix products, arithmetic and copies ran while one was open for 1% of the time, Pallas kernels for 15%

profile of v5, /device:TPU:0, one launch (start us, length us, event | category | flops | bytes accessed | tf_op | source)
XLA Modules:
  0.0 28.4 jit_solution(5304262763489240226)
XLA Ops:
  0.6 1.2 %pack.1 = (f32[14,32,128]{2,1,0:T(8,128)S(1)}, f32[14,32,128]{2,1,0:T(8,128)S(1)}, f32[4,2,32,128]{3,2,1,0:T(8,128)S(1)}, s32[8,32,128]{2,1,0:T(8,128)S(1)}, f32[16,8]{1,0:T(8,128)S(1)}) custom-call(f32[4,8,32,128]{3,2,1,0:T(8,128)} %body.1, s32[8,32,128]{2,1,0:T(8,128)} %mats.1, f32[16,8]{1,0:T(8,128)} %bitcast.14), custom_call_target="tpu_custom_call" | custom-call | tf_op jit(solution)/shard_map/pack/pallas_call | solution.py:490
  1.9 0.7 %collective-permute-start.2 = (f32[14,32,128]{2,1,0:T(8,128)S(1)}, f32[14,32,128]{2,1,0:T(8,128)S(1)}, u32[]{:S(2)}, u32[]{:S(2)}) collective-permute-start(f32[14,32,128]{2,1,0:T(8,128)S(1)} %get-tuple-element.28.side_a), channel_id=1, source_target_pairs={{1,2},{2,1},{5,6},{6,5},{9,10},{10,9},{13,14},{14,13},{17,18},{18,... | collective-permute-start | bytes 688136 | tf_op jit(solution)/shard_map/ppermute | solution.py:508
  2.6 5.9 %collective-permute-start = (f32[14,32,128]{2,1,0:T(8,128)S(1)}, f32[14,32,128]{2,1,0:T(8,128)S(1)}, u32[]{:S(2)}, u32[]{:S(2)}) collective-permute-start(f32[14,32,128]{2,1,0:T(8,128)S(1)} %get-tuple-element.27.side_b), channel_id=1, source_target_pairs={{0,1},{2,3},{1,0},{3,2},{4,5},{6,7},{5,4},{7,6},{8,9},{10,11},{9,8... | collective-permute-start | bytes 688136 | tf_op jit(solution)/shard_map/ppermute | solution.py:509
  8.5 0.0 collective-permute-start.1
  8.5 2.9 %interior.1 = (f32[4,14,32,128]{3,2,1,0:T(8,128)S(1)}, f32[4,12,32,128]{3,2,1,0:T(8,128)S(1)}, f32[4,10,32,128]{3,2,1,0:T(8,128)S(1)}, f32[4,8,32,128]{3,2,1,0:T...) custom-call(f32[14,32,128]{2,1,0:T(8,128)S(1)} %get-tuple-element.28.side_a, ...), custom_call_target="tpu_custom_call" | custom-call | tf_op jit(solution)/shard_map/interior/pallas_call | solution.py:520
  11.4 0.0 collective-permute-done.2.halo
  11.4 0.8 %near.1 = (f32[4,14,32,128]{3,2,1,0:T(8,128)S(1)}, f32[4,12,32,128]{3,2,1,0:T(8,128)S(1)}, f32[4,10,32,128]{3,2,1,0:T(8,128)S(1)}, f32[4,8,32,128]{3,2,1,0:T(8,1...) custom-call(f32[14,32,128]{2,1,0:T(8,128)S(1)} %collective-permute-d, ...), custom_call_target="tpu_custom_call", output_to_operand_aliasing={{0}: (2, {}), {1}: (3, {}), {2}: (4, {}), {3}: (5, {}), {4}... | custom-call | tf_op jit(solution)/shard_map/near/pallas_call | solution.py:529
  12.2 0.3 %collective-permute-done.1.before_hbm = s32[8]{0:T(128)S(1)} collective-permute-done((s32[8]{0:T(128)}, s32[8]{0:T(128)S(1)}, u32[]{:S(2)}, u32[]{:S(2)}) %collective-permute-start.1) | collective-permute-done | bytes 64 | tf_op jit(solution)/shard_map/ppermute | solution.py:510
  12.5 1.3 %collective-permute-done.halo = f32[14,32,128]{2,1,0:T(8,128)S(1)} collective-permute-done((f32[14,32,128]{2,1,0:T(8,128)S(1)}, f32[14,32,128]{2,1,0:T(8,128)S(1)}, u32[]{:S(2)}, u32[]{:S(2)}) %collective-permute-start) | collective-permute-done | bytes 229408 | tf_op jit(solution)/shard_map/ppermute | solution.py:509
  13.8 0.0 copy-start.1
  13.8 1.7 %far.1 = (f32[4,14,32,128]{3,2,1,0:T(8,128)S(1)}, f32[4,12,32,128]{3,2,1,0:T(8,128)S(1)}, f32[4,10,32,128]{3,2,1,0:T(8,128)S(1)}, f32[4,8,32,128]{3,2,1,0:T(8,12...) custom-call(f32[14,32,128]{2,1,0:T(8,128)S(1)} %collective-permute-d, ...), custom_call_target="tpu_custom_call", output_to_operand_aliasing={{0}: (4, {}), {1}: (5, {}), {2}: (6, {}), {3}: (7, {}), {4}... | custom-call | tf_op jit(solution)/shard_map/far/pallas_call | solution.py:539
  15.5 0.0 copy-start
  15.5 4.4 %all-to-all-start = ((f32[32,1,128]{2,1,0:T(1,128)}), f32[32,1,128]{2,1,0:T(1,128)S(1)}, u32[]{:S(2)}, u32[]{:S(2)}) async-start(f32[32,1,128]{2,1,0:T(1,128)} %bitcast.3), calls=%async_computation | async-start | bytes 32768 | tf_op jit(solution)/shard_map/all_to_all | solution.py:554
  20.0 0.6 %faces.1 = (f32[4,8,128]{2,1,0:T(8,128)S(1)}, f32[4,8,128]{2,1,0:T(8,128)S(1)}) custom-call(f32[4,14,32,128]{3,2,1,0:T(8,128)S(1)} %get-tuple-element.46.v0, f32[4,12,32,128]{3,2,1,0:T(8,128)S(1)} %get-tuple-element.47.v1, f32[4,10,32,128]{3,2,1,0:T(8,128)S(1)} %get-tuple-element.48.v2, f32[4,8,32,128]{3,2,1,0:T(8,128)S(1)} %get-tuple-element.49.v3), custom_call_target="tpu_custom_call" | custom-call | tf_op jit(solution)/shard_map/faces/pallas_call | solution.py:556
  20.6 2.4 %collective-permute-start.3 = (f32[4,8,128]{2,1,0:T(8,128)S(1)}, f32[4,8,128]{2,1,0:T(8,128)S(1)}, u32[]{:S(2)}, u32[]{:S(2)}) collective-permute-start(f32[4,8,128]{2,1,0:T(8,128)S(1)} %get-tuple-element.51), channel_id=1, source_target_pairs={{4,0},{8,4},{12,8},{16,12},{20,16},{24,20},{28,24},{0,28},{5,1},{9... | collective-permute-start | bytes 49160 | tf_op jit(solution)/shard_map/ppermute | solution.py:564
  23.0 0.0 copy-done.1
  23.0 0.2 reshape.16
  23.2 1.2 %collective-permute-done.3.left_next = f32[4,8,128]{2,1,0:T(8,128)S(1)} collective-permute-done((f32[4,8,128]{2,1,0:T(8,128)S(1)}, f32[4,8,128]{2,1,0:T(8,128)S(1)}, u32[]{:S(2)}, u32[]{:S(2)}) %collective-permute-start.3) | collective-permute-done | bytes 16416 | tf_op jit(solution)/shard_map/ppermute | solution.py:564
  24.5 2.6 %all-to-all-done = f32[32,1,128]{2,1,0:T(1,128)S(1)} async-done(((f32[32,1,128]{2,1,0:T(1,128)}), f32[32,1,128]{2,1,0:T(1,128)S(1)}, u32[]{:S(2)}, u32[]{:S(2)}) %all-to-all-start) | async-done | bytes 16416 | tf_op jit(solution)/shard_map/all_to_all | solution.py:554
  27.1 0.0 copy-done
  27.1 1.3 %final.1 = (f32[4,8,32,128]{3,2,1,0:T(8,128)}, f32[1,4,8,32]{3,2,1,0:T(8,128)}) custom-call(f32[32,128]{1,0:T(8,128)S(1)} %bitcast.12, f32[4,14,32,128]{3,2,1,0:T(8,128)S(1)} %get-tuple-element.46.v0, f32[4,12,32,128]{3,2,1,0:T(8,128)S(1)} %get-tuple-element.47.v1, f32[4,10,32,128]{3,2,1,0:T(8,128)S(1)} %get-tuple-element.48.v2, ...), custom_call_target="tpu_custom_call" | custom-call | tf_op jit(solution)/shard_map/final/pallas_call | solution.py:566
  (1 shorter events, 0.0 us)
Async XLA Ops:
  1.9 9.5 %collective-permute-start.2 = (f32[14,32,128]{2,1,0:T(8,128)S(1)}, f32[14,32,128]{2,1,0:T(8,128)S(1)}, u32[]{:S(2)}, u32[]{:S(2)}) collective-permute-start(f32[14,32,128]{2,1,0:T(8,128)S(1)} %get-tuple-element.28.side_a), channel_id=1, source_target_pairs={{1,2},{2,1},{5,6},{6,5},{9,10},{10,9},{13,14},{14,13},{17,18},{18,... | collective-permute-start | bytes 688136 | tf_op jit(solution)/shard_map/ppermute | solution.py:508
  2.6 11.3 %collective-permute-start = (f32[14,32,128]{2,1,0:T(8,128)S(1)}, f32[14,32,128]{2,1,0:T(8,128)S(1)}, u32[]{:S(2)}, u32[]{:S(2)}) collective-permute-start(f32[14,32,128]{2,1,0:T(8,128)S(1)} %get-tuple-element.27.side_b), channel_id=1, source_target_pairs={{0,1},{2,3},{1,0},{3,2},{4,5},{6,7},{5,4},{7,6},{8,9},{10,11},{9,8... | collective-permute-start | bytes 688136 | tf_op jit(solution)/shard_map/ppermute | solution.py:509
  8.5 4.0 %collective-permute-start.1 = (s32[8]{0:T(128)}, s32[8]{0:T(128)S(1)}, u32[]{:S(2)}, u32[]{:S(2)}) collective-permute-start(s32[8]{0:T(128)} %corners_hbm.1), channel_id=1, source_target_pairs={{0,4},{4,8},{8,12},{12,16},{16,20},{20,24},{24,28},{28,0},{1,5},{5... | collective-permute-start | bytes 104 | tf_op jit(solution)/shard_map/ppermute | solution.py:510
  13.8 9.2 %copy-start.1 = (f32[8,256]{1,0:T(8,128)S(1)}, f32[8,256]{1,0:T(8,128)}, u32[]{:S(2)}) copy-start(f32[8,256]{1,0:T(8,128)} %param.9) | copy-start | bytes 24580
  15.5 11.6 %copy-start = (s32[8]{0:T(128)S(1)}, s32[8]{0:T(128)}, u32[]{:S(2)}) copy-start(s32[8]{0:T(128)} %corners_hbm.1) | copy-start | bytes 100
  15.5 11.6 %all-to-all-start = ((f32[32,1,128]{2,1,0:T(1,128)}), f32[32,1,128]{2,1,0:T(1,128)S(1)}, u32[]{:S(2)}, u32[]{:S(2)}) async-start(f32[32,1,128]{2,1,0:T(1,128)} %bitcast.3), calls=%async_computation | async-start | bytes 32768 | tf_op jit(solution)/shard_map/all_to_all | solution.py:554
  20.6 3.9 %collective-permute-start.3 = (f32[4,8,128]{2,1,0:T(8,128)S(1)}, f32[4,8,128]{2,1,0:T(8,128)S(1)}, u32[]{:S(2)}, u32[]{:S(2)}) collective-permute-start(f32[4,8,128]{2,1,0:T(8,128)S(1)} %get-tuple-element.51), channel_id=1, source_target_pairs={{4,0},{8,4},{12,8},{16,12},{20,16},{24,20},{28,24},{0,28},{5,1},{9... | collective-permute-start | bytes 49160 | tf_op jit(solution)/shard_map/ppermute | solution.py:564

commit v6 on v5

--- a/solution.py
+++ b/solution.py
@@ -38,27 +38,24 @@
     return lax.shift_right_logical(index, size.bit_length() - 1), index & (size - 1)
 
 
-def pack_kernel(body, mats, table, a_out, b_out, middle_out, mats_out, table_out, sems, rest):
+def pack_kernel(body, mats, a_out, b_out, kinds, sems):
     comp, depth = body.shape[0], body.shape[1]
     odd = lax.rem(lax.axis_index("in") + 1, 2)
-    sides = ((a_out, odd), (b_out, 1 - odd))
     copies = []
-    for slot, (out, low) in enumerate(sides):
+    for slot, (out, low) in enumerate(((a_out, odd), (b_out, 1 - odd))):
         first = (1 - low) * (depth - ITERS)
         for c in range(comp):
             copies.append(pltpu.make_async_copy(
                 body.at[c, pl.ds(first, ITERS)], out.at[pl.ds(ITERS * c, ITERS)], sems.at[slot, c]))
-    copies.append(pltpu.make_async_copy(mats, mats_out, rest.at[0]))
-    copies.append(pltpu.make_async_copy(body.at[:, pl.ds(ITERS, depth - 2 * ITERS)], middle_out, rest.at[1]))
-    copies.append(pltpu.make_async_copy(table, table_out, rest.at[2]))
+        first = (1 - low) * (depth - MAT_DEPTH)
+        copies.append(pltpu.make_async_copy(
+            mats.at[pl.ds(first, MAT_DEPTH)], kinds.at[slot], sems.at[slot, comp]))
     for copy in copies:
         copy.start()
     for copy in copies:
         copy.wait()
-    for out, low in sides:
-        first = (1 - low) * (depth - MAT_DEPTH)
-        for t in range(MAT_DEPTH):
-            out[ITERS * comp + t] = mats_out[first + t].astype(jnp.float32)
+    for slot, out in enumerate((a_out, b_out)):
+        out[pl.ds(ITERS * comp, MAT_DEPTH)] = kinds[slot].astype(jnp.float32)
 
 
 class Slab:
@@ -156,9 +153,17 @@
     return first, second, third
 
 
-def interior_kernel(side_a, side_b, middle, mats, table, v0, v1, v2, v3, gains, gram, tab):
-    comp, _, py, px = middle.shape
-    depth = mats.shape[0]
+def interior_kernel(side_a, side_b, body_hbm, mats_hbm, table_hbm, v0, v1, v2, v3, gains, gram, tab,
+                    middle, mats, table, sems):
+    comp, depth, py, px = body_hbm.shape
+    fetch = (
+        pltpu.make_async_copy(table_hbm, table, sems.at[0]),
+        pltpu.make_async_copy(mats_hbm, mats, sems.at[1]),
+        pltpu.make_async_copy(body_hbm.at[:, pl.ds(ITERS, depth - 2 * ITERS)], middle, sems.at[2]),
+    )
+    for copy in fetch:
+        copy.start()
+    fetch[0].wait()
     odd = lax.rem(lax.axis_index("in") + 1, 2) == 1
     kinds = table.shape[1]
     entries = comp * comp
@@ -174,6 +179,9 @@
     for c in range(comp):
         for at in (ITERS - 1, ITERS + depth):
             slab.store(v0, [zero] * slab.parts, c, at)
+
+    for copy in fetch[1:]:
+        copy.wait()
 
     def place(values, z, g00):
         for c in range(comp):
@@ -487,19 +495,18 @@
     def hbm(x):
         return pltpu.with_memory_space_constraint(x, pltpu.HBM)
 
-    send_a, send_b, middle, mats, table = pl.pallas_call(
+    send_a, send_b = pl.pallas_call(
         pack_kernel,
-        out_shape=(
-            halo, halo, shape((comp, depth - 2 * ITERS, py, px), f32), shape(materials.shape, jnp.int32), shape(table.shape, f32)),
-        in_specs=[HBM] * 3,
-        out_specs=(VMEM,) * 5,
+        out_shape=(halo, halo),
+        in_specs=[HBM] * 2,
+        out_specs=(VMEM,) * 2,
         scratch_shapes=[
-            pltpu.SemaphoreType.DMA((2, comp)),
-            pltpu.SemaphoreType.DMA((3,)),
+            pltpu.VMEM((2, MAT_DEPTH, py, px), jnp.int32),
+            pltpu.SemaphoreType.DMA((2, comp + 1)),
         ],
         compiler_params=params(4),
         name="pack",
-    )(hbm(body_load), hbm(materials), hbm(table))
+    )(hbm(body_load), hbm(materials))
 
     def swaps(start):
         pairs = [(i, i + 1) for i in range(start, n_in - 1, 2)]
@@ -520,11 +527,17 @@
     *inner, tab = pl.pallas_call(
         interior_kernel,
         out_shape=(*fields, shape((kinds * comp * comp + 24, px), f32)),
-        in_specs=[VMEM] * 5,
+        in_specs=[VMEM] * 2 + [HBM] * 3,
         out_specs=(VMEM,) * 7,
+        scratch_shapes=[
+            pltpu.VMEM((comp, depth - 2 * ITERS, py, px), f32),
+            pltpu.VMEM(materials.shape, jnp.int32),
+            pltpu.VMEM(table.shape, f32),
+            pltpu.SemaphoreType.DMA((3,)),
+        ],
         compiler_params=params(4),
         name="interior",
-    )(send_a, send_b, middle, mats, table)
+    )(send_a, send_b, hbm(body_load), hbm(materials), hbm(table))
 
     inner = pl.pallas_call(
         functools.partial(near_kernel, kinds),

time: 28.6 us -> 28.5 us (level)
  waiting for transfers between devices: 5.45 us -> 4.82 us
  Pallas kernels: 8.54 us -> 8.98 us
    pallas_call x1, Pallas kernels: 2.92 us -> 3.57 us  [on_device(): pl.pallas_call(interior_kernel, out_shape=(*fields, shape((kinds * comp *...]
    ppermute x1, waiting for transfers between devices: 1.3 us -> 0.96 us  [on_device(): halo_b = lax.ppermute(send_b, 'in', swaps(0))]
    ppermute x1, waiting for transfers between devices: 0.3 us -> 0.01 us  [on_device(): lax.ppermute(corner_index, 'sub', [(i, (i + 1) % n_sub) for i in range(n_...]
  transfers between devices with their start and end apart: 5 -> 5, of which waited for: 4 -> 3; matrix products, arithmetic and copies ran while one was open for 1% -> 1% of each run, Pallas kernels for 15% -> 17%
where the time goes in v6:
time: 28.5 us; the launch traced here: 28.2 us
  starting transfers between devices  13.5 us (47%)
  Pallas kernels  8.98 us (32%)
  waiting for transfers between devices  4.82 us (17%)
  between operations  0.73 us (3%)
    ppermute x1, starting transfers between devices, on_device(): halo_b = lax.ppermute(send_b, 'in', swaps(0))  5.93 us
    all_to_all x1, starting transfers between devices, on_device(): messages = lax.all_to_all(message, ('sub', 'in'), 0, 0, tiled=True)  4.42 us
    pallas_call x1, Pallas kernels, on_device(): pl.pallas_call(interior_kernel, out_shape=(*fields, shape((kinds * comp *...  3.57 us
    all_to_all x1, waiting for transfers between devices, on_device(): messages = lax.all_to_all(message, ('sub', 'in'), 0, 0, tiled=True)  2.63 us
    ppermute x1, starting transfers between devices, on_device(): lax.ppermute(left, 'sub', [((i + 1) % n_sub, i) for i in range(n_sub)])  2.44 us
    pallas_call x1, Pallas kernels, on_device(): pl.pallas_call(functools.partial(far_kernel, kinds), out_shape=(*fields[:...  1.66 us
    pallas_call x1, Pallas kernels, on_device(): pl.pallas_call(functools.partial(final_kernel, kinds), out_shape=(shape(b...  1.31 us
    ppermute x1, waiting for transfers between devices, on_device(): lax.ppermute(left, 'sub', [((i + 1) % n_sub, i) for i in range(n_sub)])  1.22 us
  transfers between devices with their start and end apart: 5, of which 3 were waited for; matrix products, arithmetic and copies ran while one was open for 1% of the time, Pallas kernels for 17%

profile of v6, /device:TPU:0, one launch (start us, length us, event | category | flops | bytes accessed | tf_op | source)
XLA Modules:
  0.0 28.2 jit_solution(11013622659838483551)
XLA Ops:
  0.6 1.1 %pack.1 = (f32[14,32,128]{2,1,0:T(8,128)S(1)}, f32[14,32,128]{2,1,0:T(8,128)S(1)}) custom-call(f32[4,8,32,128]{3,2,1,0:T(8,128)} %body_hbm.1, s32[8,32,128]{2,1,0:T(8,128)} %mats_hbm.1), custom_call_target="tpu_custom_call" | custom-call | tf_op jit(solution)/shard_map/pack/pallas_call | solution.py:498
  1.7 0.7 %collective-permute-start.2 = (f32[14,32,128]{2,1,0:T(8,128)S(1)}, f32[14,32,128]{2,1,0:T(8,128)S(1)}, u32[]{:S(2)}, u32[]{:S(2)}) collective-permute-start(f32[14,32,128]{2,1,0:T(8,128)S(1)} %get-tuple-element.25.side_a), channel_id=1, source_target_pairs={{1,2},{2,1},{5,6},{6,5},{9,10},{10,9},{13,14},{14,13},{17,18},{18,... | collective-permute-start | bytes 688136 | tf_op jit(solution)/shard_map/ppermute | solution.py:515
  2.4 5.9 %collective-permute-start = (f32[14,32,128]{2,1,0:T(8,128)S(1)}, f32[14,32,128]{2,1,0:T(8,128)S(1)}, u32[]{:S(2)}, u32[]{:S(2)}) collective-permute-start(f32[14,32,128]{2,1,0:T(8,128)S(1)} %get-tuple-element.24.side_b), channel_id=1, source_target_pairs={{0,1},{2,3},{1,0},{3,2},{4,5},{6,7},{5,4},{7,6},{8,9},{10,11},{9,8... | collective-permute-start | bytes 688136 | tf_op jit(solution)/shard_map/ppermute | solution.py:516
  8.3 0.0 collective-permute-start.1
  8.3 3.6 %interior.1 = (f32[4,14,32,128]{3,2,1,0:T(8,128)S(1)}, f32[4,12,32,128]{3,2,1,0:T(8,128)S(1)}, f32[4,10,32,128]{3,2,1,0:T(8,128)S(1)}, f32[4,8,32,128]{3,2,1,0:T...) custom-call(f32[14,32,128]{2,1,0:T(8,128)S(1)} %get-tuple-element.25.side_a, ...), custom_call_target="tpu_custom_call" | custom-call | tf_op jit(solution)/shard_map/interior/pallas_call | solution.py:527
  11.9 0.0 collective-permute-done.2.halo
  11.9 0.8 %near.1 = (f32[4,14,32,128]{3,2,1,0:T(8,128)S(1)}, f32[4,12,32,128]{3,2,1,0:T(8,128)S(1)}, f32[4,10,32,128]{3,2,1,0:T(8,128)S(1)}, f32[4,8,32,128]{3,2,1,0:T(8,1...) custom-call(f32[14,32,128]{2,1,0:T(8,128)S(1)} %collective-permute-d, ...), custom_call_target="tpu_custom_call", output_to_operand_aliasing={{0}: (2, {}), {1}: (3, {}), {2}: (4, {}), {3}: (5, {}), {4}... | custom-call | tf_op jit(solution)/shard_map/near/pallas_call | solution.py:542
  12.7 0.0 collective-permute-done.1.before_hbm
  12.7 1.0 %collective-permute-done.halo = f32[14,32,128]{2,1,0:T(8,128)S(1)} collective-permute-done((f32[14,32,128]{2,1,0:T(8,128)S(1)}, f32[14,32,128]{2,1,0:T(8,128)S(1)}, u32[]{:S(2)}, u32[]{:S(2)}) %collective-permute-start) | collective-permute-done | bytes 229408 | tf_op jit(solution)/shard_map/ppermute | solution.py:516
  13.7 0.0 copy-start.1
  13.7 1.7 %far.1 = (f32[4,14,32,128]{3,2,1,0:T(8,128)S(1)}, f32[4,12,32,128]{3,2,1,0:T(8,128)S(1)}, f32[4,10,32,128]{3,2,1,0:T(8,128)S(1)}, f32[4,8,32,128]{3,2,1,0:T(8,12...) custom-call(f32[14,32,128]{2,1,0:T(8,128)S(1)} %collective-permute-d, ...), custom_call_target="tpu_custom_call", output_to_operand_aliasing={{0}: (4, {}), {1}: (5, {}), {2}: (6, {}), {3}: (7, {}), {4}... | custom-call | tf_op jit(solution)/shard_map/far/pallas_call | solution.py:552
  15.3 0.0 copy-start
  15.3 4.4 %all-to-all-start = ((f32[32,1,128]{2,1,0:T(1,128)}), f32[32,1,128]{2,1,0:T(1,128)S(1)}, u32[]{:S(2)}, u32[]{:S(2)}) async-start(f32[32,1,128]{2,1,0:T(1,128)} %bitcast.3), calls=%async_computation | async-start | bytes 32768 | tf_op jit(solution)/shard_map/all_to_all | solution.py:567
  19.8 0.6 %faces.1 = (f32[4,8,128]{2,1,0:T(8,128)S(1)}, f32[4,8,128]{2,1,0:T(8,128)S(1)}) custom-call(f32[4,14,32,128]{3,2,1,0:T(8,128)S(1)} %get-tuple-element.40.v0, f32[4,12,32,128]{3,2,1,0:T(8,128)S(1)} %get-tuple-element.41.v1, f32[4,10,32,128]{3,2,1,0:T(8,128)S(1)} %get-tuple-element.42.v2, f32[4,8,32,128]{3,2,1,0:T(8,128)S(1)} %get-tuple-element.43.v3), custom_call_target="tpu_custom_call" | custom-call | tf_op jit(solution)/shard_map/faces/pallas_call | solution.py:569
  20.4 2.4 %collective-permute-start.3 = (f32[4,8,128]{2,1,0:T(8,128)S(1)}, f32[4,8,128]{2,1,0:T(8,128)S(1)}, u32[]{:S(2)}, u32[]{:S(2)}) collective-permute-start(f32[4,8,128]{2,1,0:T(8,128)S(1)} %get-tuple-element.45), channel_id=1, source_target_pairs={{4,0},{8,4},{12,8},{16,12},{20,16},{24,20},{28,24},{0,28},{5,1},{9... | collective-permute-start | bytes 49160 | tf_op jit(solution)/shard_map/ppermute | solution.py:577
  22.8 0.0 copy-done.1
  22.8 0.2 reshape.16
  23.0 1.2 %collective-permute-done.3.left_next = f32[4,8,128]{2,1,0:T(8,128)S(1)} collective-permute-done((f32[4,8,128]{2,1,0:T(8,128)S(1)}, f32[4,8,128]{2,1,0:T(8,128)S(1)}, u32[]{:S(2)}, u32[]{:S(2)}) %collective-permute-start.3) | collective-permute-done | bytes 16416 | tf_op jit(solution)/shard_map/ppermute | solution.py:577
  24.3 2.6 %all-to-all-done = f32[32,1,128]{2,1,0:T(1,128)S(1)} async-done(((f32[32,1,128]{2,1,0:T(1,128)}), f32[32,1,128]{2,1,0:T(1,128)S(1)}, u32[]{:S(2)}, u32[]{:S(2)}) %all-to-all-start) | async-done | bytes 16416 | tf_op jit(solution)/shard_map/all_to_all | solution.py:567
  26.9 0.0 copy-done
  26.9 1.3 %final.1 = (f32[4,8,32,128]{3,2,1,0:T(8,128)}, f32[1,4,8,32]{3,2,1,0:T(8,128)}) custom-call(f32[32,128]{1,0:T(8,128)S(1)} %bitcast.12, f32[4,14,32,128]{3,2,1,0:T(8,128)S(1)} %get-tuple-element.40.v0, f32[4,12,32,128]{3,2,1,0:T(8,128)S(1)} %get-tuple-element.41.v1, f32[4,10,32,128]{3,2,1,0:T(8,128)S(1)} %get-tuple-element.42.v2, ...), custom_call_target="tpu_custom_call" | custom-call | tf_op jit(solution)/shard_map/final/pallas_call | solution.py:579
  (1 shorter events, 0.0 us)
Async XLA Ops:
  1.7 10.2 %collective-permute-start.2 = (f32[14,32,128]{2,1,0:T(8,128)S(1)}, f32[14,32,128]{2,1,0:T(8,128)S(1)}, u32[]{:S(2)}, u32[]{:S(2)}) collective-permute-start(f32[14,32,128]{2,1,0:T(8,128)S(1)} %get-tuple-element.25.side_a), channel_id=1, source_target_pairs={{1,2},{2,1},{5,6},{6,5},{9,10},{10,9},{13,14},{14,13},{17,18},{18,... | collective-permute-start | bytes 688136 | tf_op jit(solution)/shard_map/ppermute | solution.py:515
  2.4 11.3 %collective-permute-start = (f32[14,32,128]{2,1,0:T(8,128)S(1)}, f32[14,32,128]{2,1,0:T(8,128)S(1)}, u32[]{:S(2)}, u32[]{:S(2)}) collective-permute-start(f32[14,32,128]{2,1,0:T(8,128)S(1)} %get-tuple-element.24.side_b), channel_id=1, source_target_pairs={{0,1},{2,3},{1,0},{3,2},{4,5},{6,7},{5,4},{7,6},{8,9},{10,11},{9,8... | collective-permute-start | bytes 688136 | tf_op jit(solution)/shard_map/ppermute | solution.py:516
  8.3 4.4 %collective-permute-start.1 = (s32[8]{0:T(128)}, s32[8]{0:T(128)S(1)}, u32[]{:S(2)}, u32[]{:S(2)}) collective-permute-start(s32[8]{0:T(128)} %corners_hbm.1), channel_id=1, source_target_pairs={{0,4},{4,8},{8,12},{12,16},{16,20},{20,24},{24,28},{28,0},{1,5},{5... | collective-permute-start | bytes 104 | tf_op jit(solution)/shard_map/ppermute | solution.py:517
  13.7 9.2 %copy-start.1 = (f32[8,256]{1,0:T(8,128)S(1)}, f32[8,256]{1,0:T(8,128)}, u32[]{:S(2)}) copy-start(f32[8,256]{1,0:T(8,128)} %param.9) | copy-start | bytes 24580
  15.3 11.6 %copy-start = (s32[8]{0:T(128)S(1)}, s32[8]{0:T(128)}, u32[]{:S(2)}) copy-start(s32[8]{0:T(128)} %corners_hbm.1) | copy-start | bytes 100
  15.3 11.6 %all-to-all-start = ((f32[32,1,128]{2,1,0:T(1,128)}), f32[32,1,128]{2,1,0:T(1,128)S(1)}, u32[]{:S(2)}, u32[]{:S(2)}) async-start(f32[32,1,128]{2,1,0:T(1,128)} %bitcast.3), calls=%async_computation | async-start | bytes 32768 | tf_op jit(solution)/shard_map/all_to_all | solution.py:567
  20.4 3.9 %collective-permute-start.3 = (f32[4,8,128]{2,1,0:T(8,128)S(1)}, f32[4,8,128]{2,1,0:T(8,128)S(1)}, u32[]{:S(2)}, u32[]{:S(2)}) collective-permute-start(f32[4,8,128]{2,1,0:T(8,128)S(1)} %get-tuple-element.45), channel_id=1, source_target_pairs={{4,0},{8,4},{12,8},{16,12},{20,16},{24,20},{28,24},{0,28},{5,1},{9... | collective-permute-start | bytes 49160 | tf_op jit(solution)/shard_map/ppermute | solution.py:577

commit v7 on v6

--- a/solution.py
+++ b/solution.py
@@ -265,7 +265,8 @@
         for c, _, w in slab.applied(v0, z + 3, gains, z + 2, inverse, alive):
             slab.store(v1, w, c, z + 2)
         return carry
-    lax.fori_loop(0, 2, first_halo, 0)
+    for i in range(2):
+        first_halo(i, 0)
 
     z0, z1, z2, out = layer(0), layer(1), layer(2), layer(-1)
 
@@ -295,7 +296,8 @@
     for c, _, w in slab.applied(v1, out + 2, gains, out + 2, inverse, alive):
         slab.store(v2, w, c, out + 1)
     g02, g12, g22 = second(z0, (g02, g12, g22))
-    g03, g13, g23 = lax.fori_loop(0, 2, lambda i, sums: third(layer(i), sums), (g03, g13, g23))
+    for i in range(2):
+        g03, g13, g23 = third(layer(i), (g03, g13, g23))
     return g00, g01, g02, g03, g11, g12, g13, g22, g23
 
 

time: 28.5 us -> 28.1 us (0.986)
  starting transfers between devices: 13.5 us -> 13.1 us
    all_to_all x1, starting transfers between devices: 4.42 us -> 4.1 us  [on_device(): messages = lax.all_to_all(message, ('sub', 'in'), 0, 0, tiled=True)]
where the time goes in v7:
time: 28.1 us; the launch traced here: 27.8 us
  starting transfers between devices  13.1 us (47%)
  Pallas kernels  8.73 us (31%)
  waiting for transfers between devices  5.02 us (18%)
  between operations  0.73 us (3%)
    ppermute x1, starting transfers between devices, on_device(): halo_b = lax.ppermute(send_b, 'in', swaps(0))  5.93 us
    all_to_all x1, starting transfers between devices, on_device(): messages = lax.all_to_all(message, ('sub', 'in'), 0, 0, tiled=True)  4.1 us
    pallas_call x1, Pallas kernels, on_device(): pl.pallas_call(interior_kernel, out_shape=(*fields, shape((kinds * comp *...  3.57 us
    all_to_all x1, waiting for transfers between devices, on_device(): messages = lax.all_to_all(message, ('sub', 'in'), 0, 0, tiled=True)  2.63 us
    ppermute x1, starting transfers between devices, on_device(): lax.ppermute(left, 'sub', [((i + 1) % n_sub, i) for i in range(n_sub)])  2.44 us
    pallas_call x1, Pallas kernels, on_device(): pl.pallas_call(functools.partial(far_kernel, kinds), out_shape=(*fields[:...  1.6 us
    pallas_call x1, Pallas kernels, on_device(): pl.pallas_call(functools.partial(final_kernel, kinds), out_shape=(shape(b...  1.31 us
    ppermute x1, waiting for transfers between devices, on_device(): lax.ppermute(left, 'sub', [((i + 1) % n_sub, i) for i in range(n_sub)])  1.22 us
  transfers between devices with their start and end apart: 5, of which 3 were waited for; matrix products, arithmetic and copies ran while one was open for 1% of the time, Pallas kernels for 17%

profile of v7, /device:TPU:0, one launch (start us, length us, event | category | flops | bytes accessed | tf_op | source)
XLA Modules:
  0.0 27.8 jit_solution(7771974555938891371)
XLA Ops:
  0.6 1.1 %pack.1 = (f32[14,32,128]{2,1,0:T(8,128)S(1)}, f32[14,32,128]{2,1,0:T(8,128)S(1)}) custom-call(f32[4,8,32,128]{3,2,1,0:T(8,128)} %body_hbm.1, s32[8,32,128]{2,1,0:T(8,128)} %mats_hbm.1), custom_call_target="tpu_custom_call" | custom-call | tf_op jit(solution)/shard_map/pack/pallas_call | solution.py:500
  1.7 0.7 %collective-permute-start.2 = (f32[14,32,128]{2,1,0:T(8,128)S(1)}, f32[14,32,128]{2,1,0:T(8,128)S(1)}, u32[]{:S(2)}, u32[]{:S(2)}) collective-permute-start(f32[14,32,128]{2,1,0:T(8,128)S(1)} %get-tuple-element.25.side_a), channel_id=1, source_target_pairs={{1,2},{2,1},{5,6},{6,5},{9,10},{10,9},{13,14},{14,13},{17,18},{18,... | collective-permute-start | bytes 688136 | tf_op jit(solution)/shard_map/ppermute | solution.py:517
  2.4 5.9 %collective-permute-start = (f32[14,32,128]{2,1,0:T(8,128)S(1)}, f32[14,32,128]{2,1,0:T(8,128)S(1)}, u32[]{:S(2)}, u32[]{:S(2)}) collective-permute-start(f32[14,32,128]{2,1,0:T(8,128)S(1)} %get-tuple-element.24.side_b), channel_id=1, source_target_pairs={{0,1},{2,3},{1,0},{3,2},{4,5},{6,7},{5,4},{7,6},{8,9},{10,11},{9,8... | collective-permute-start | bytes 688136 | tf_op jit(solution)/shard_map/ppermute | solution.py:518
  8.3 0.0 collective-permute-start.1
  8.3 3.6 %interior.1 = (f32[4,14,32,128]{3,2,1,0:T(8,128)S(1)}, f32[4,12,32,128]{3,2,1,0:T(8,128)S(1)}, f32[4,10,32,128]{3,2,1,0:T(8,128)S(1)}, f32[4,8,32,128]{3,2,1,0:T...) custom-call(f32[14,32,128]{2,1,0:T(8,128)S(1)} %get-tuple-element.25.side_a, ...), custom_call_target="tpu_custom_call" | custom-call | tf_op jit(solution)/shard_map/interior/pallas_call | solution.py:529
  11.9 0.0 collective-permute-done.2.halo
  11.9 0.6 %near.1 = (f32[4,14,32,128]{3,2,1,0:T(8,128)S(1)}, f32[4,12,32,128]{3,2,1,0:T(8,128)S(1)}, f32[4,10,32,128]{3,2,1,0:T(8,128)S(1)}, f32[4,8,32,128]{3,2,1,0:T(8,1...) custom-call(f32[14,32,128]{2,1,0:T(8,128)S(1)} %collective-permute-d, ...), custom_call_target="tpu_custom_call", output_to_operand_aliasing={{0}: (2, {}), {1}: (3, {}), {2}: (4, {}), {3}: (5, {}), {4}... | custom-call | tf_op jit(solution)/shard_map/near/pallas_call | solution.py:544
  12.5 0.0 collective-permute-done.1.before_hbm
  12.5 1.2 %collective-permute-done.halo = f32[14,32,128]{2,1,0:T(8,128)S(1)} collective-permute-done((f32[14,32,128]{2,1,0:T(8,128)S(1)}, f32[14,32,128]{2,1,0:T(8,128)S(1)}, u32[]{:S(2)}, u32[]{:S(2)}) %collective-permute-start) | collective-permute-done | bytes 229408 | tf_op jit(solution)/shard_map/ppermute | solution.py:518
  13.7 0.0 copy-start.1
  13.7 1.6 %far.1 = (f32[4,14,32,128]{3,2,1,0:T(8,128)S(1)}, f32[4,12,32,128]{3,2,1,0:T(8,128)S(1)}, f32[4,10,32,128]{3,2,1,0:T(8,128)S(1)}, f32[4,8,32,128]{3,2,1,0:T(8,12...) custom-call(f32[14,32,128]{2,1,0:T(8,128)S(1)} %collective-permute-d, ...), custom_call_target="tpu_custom_call", output_to_operand_aliasing={{0}: (4, {}), {1}: (5, {}), {2}: (6, {}), {3}: (7, {}), {4}... | custom-call | tf_op jit(solution)/shard_map/far/pallas_call | solution.py:554
  15.3 0.0 copy-start
  15.3 4.1 %all-to-all-start = ((f32[32,1,128]{2,1,0:T(1,128)}), f32[32,1,128]{2,1,0:T(1,128)S(1)}, u32[]{:S(2)}, u32[]{:S(2)}) async-start(f32[32,1,128]{2,1,0:T(1,128)} %bitcast.3), calls=%async_computation | async-start | bytes 32768 | tf_op jit(solution)/shard_map/all_to_all | solution.py:569
  19.4 0.6 %faces.1 = (f32[4,8,128]{2,1,0:T(8,128)S(1)}, f32[4,8,128]{2,1,0:T(8,128)S(1)}) custom-call(f32[4,14,32,128]{3,2,1,0:T(8,128)S(1)} %get-tuple-element.40.v0, f32[4,12,32,128]{3,2,1,0:T(8,128)S(1)} %get-tuple-element.41.v1, f32[4,10,32,128]{3,2,1,0:T(8,128)S(1)} %get-tuple-element.42.v2, f32[4,8,32,128]{3,2,1,0:T(8,128)S(1)} %get-tuple-element.43.v3), custom_call_target="tpu_custom_call" | custom-call | tf_op jit(solution)/shard_map/faces/pallas_call | solution.py:571
  20.0 2.4 %collective-permute-start.3 = (f32[4,8,128]{2,1,0:T(8,128)S(1)}, f32[4,8,128]{2,1,0:T(8,128)S(1)}, u32[]{:S(2)}, u32[]{:S(2)}) collective-permute-start(f32[4,8,128]{2,1,0:T(8,128)S(1)} %get-tuple-element.45), channel_id=1, source_target_pairs={{4,0},{8,4},{12,8},{16,12},{20,16},{24,20},{28,24},{0,28},{5,1},{9... | collective-permute-start | bytes 49160 | tf_op jit(solution)/shard_map/ppermute | solution.py:579
  22.4 0.0 copy-done.1
  22.4 0.2 reshape.16
  22.7 1.2 %collective-permute-done.3.left_next = f32[4,8,128]{2,1,0:T(8,128)S(1)} collective-permute-done((f32[4,8,128]{2,1,0:T(8,128)S(1)}, f32[4,8,128]{2,1,0:T(8,128)S(1)}, u32[]{:S(2)}, u32[]{:S(2)}) %collective-permute-start.3) | collective-permute-done | bytes 16416 | tf_op jit(solution)/shard_map/ppermute | solution.py:579
  23.9 2.6 %all-to-all-done = f32[32,1,128]{2,1,0:T(1,128)S(1)} async-done(((f32[32,1,128]{2,1,0:T(1,128)}), f32[32,1,128]{2,1,0:T(1,128)S(1)}, u32[]{:S(2)}, u32[]{:S(2)}) %all-to-all-start) | async-done | bytes 16416 | tf_op jit(solution)/shard_map/all_to_all | solution.py:569
  26.5 0.0 copy-done
  26.5 1.3 %final.1 = (f32[4,8,32,128]{3,2,1,0:T(8,128)}, f32[1,4,8,32]{3,2,1,0:T(8,128)}) custom-call(f32[32,128]{1,0:T(8,128)S(1)} %bitcast.12, f32[4,14,32,128]{3,2,1,0:T(8,128)S(1)} %get-tuple-element.40.v0, f32[4,12,32,128]{3,2,1,0:T(8,128)S(1)} %get-tuple-element.41.v1, f32[4,10,32,128]{3,2,1,0:T(8,128)S(1)} %get-tuple-element.42.v2, ...), custom_call_target="tpu_custom_call" | custom-call | tf_op jit(solution)/shard_map/final/pallas_call | solution.py:581
  (1 shorter events, 0.0 us)
Async XLA Ops:
  1.7 10.2 %collective-permute-start.2 = (f32[14,32,128]{2,1,0:T(8,128)S(1)}, f32[14,32,128]{2,1,0:T(8,128)S(1)}, u32[]{:S(2)}, u32[]{:S(2)}) collective-permute-start(f32[14,32,128]{2,1,0:T(8,128)S(1)} %get-tuple-element.25.side_a), channel_id=1, source_target_pairs={{1,2},{2,1},{5,6},{6,5},{9,10},{10,9},{13,14},{14,13},{17,18},{18,... | collective-permute-start | bytes 688136 | tf_op jit(solution)/shard_map/ppermute | solution.py:517
  2.4 11.3 %collective-permute-start = (f32[14,32,128]{2,1,0:T(8,128)S(1)}, f32[14,32,128]{2,1,0:T(8,128)S(1)}, u32[]{:S(2)}, u32[]{:S(2)}) collective-permute-start(f32[14,32,128]{2,1,0:T(8,128)S(1)} %get-tuple-element.24.side_b), channel_id=1, source_target_pairs={{0,1},{2,3},{1,0},{3,2},{4,5},{6,7},{5,4},{7,6},{8,9},{10,11},{9,8... | collective-permute-start | bytes 688136 | tf_op jit(solution)/shard_map/ppermute | solution.py:518
  8.3 4.2 %collective-permute-start.1 = (s32[8]{0:T(128)}, s32[8]{0:T(128)S(1)}, u32[]{:S(2)}, u32[]{:S(2)}) collective-permute-start(s32[8]{0:T(128)} %corners_hbm.1), channel_id=1, source_target_pairs={{0,4},{4,8},{8,12},{12,16},{16,20},{20,24},{24,28},{28,0},{1,5},{5... | collective-permute-start | bytes 104 | tf_op jit(solution)/shard_map/ppermute | solution.py:519
  13.7 8.8 %copy-start.1 = (f32[8,256]{1,0:T(8,128)S(1)}, f32[8,256]{1,0:T(8,128)}, u32[]{:S(2)}) copy-start(f32[8,256]{1,0:T(8,128)} %param.9) | copy-start | bytes 24580
  15.3 11.2 %copy-start = (s32[8]{0:T(128)S(1)}, s32[8]{0:T(128)}, u32[]{:S(2)}) copy-start(s32[8]{0:T(128)} %corners_hbm.1) | copy-start | bytes 100
  15.3 11.2 %all-to-all-start = ((f32[32,1,128]{2,1,0:T(1,128)}), f32[32,1,128]{2,1,0:T(1,128)S(1)}, u32[]{:S(2)}, u32[]{:S(2)}) async-start(f32[32,1,128]{2,1,0:T(1,128)} %bitcast.3), calls=%async_computation | async-start | bytes 32768 | tf_op jit(solution)/shard_map/all_to_all | solution.py:569
  20.0 3.9 %collective-permute-start.3 = (f32[4,8,128]{2,1,0:T(8,128)S(1)}, f32[4,8,128]{2,1,0:T(8,128)S(1)}, u32[]{:S(2)}, u32[]{:S(2)}) collective-permute-start(f32[4,8,128]{2,1,0:T(8,128)S(1)} %get-tuple-element.45), channel_id=1, source_target_pairs={{4,0},{8,4},{12,8},{16,12},{20,16},{24,20},{28,24},{0,28},{5,1},{9... | collective-permute-start | bytes 49160 | tf_op jit(solution)/shard_map/ppermute | solution.py:579

commit v8 on v7

--- a/solution.py
+++ b/solution.py
@@ -222,11 +222,14 @@
         return carry
 
     first, second, third = levels(slab, v0, v1, v2, v3, gains, inverse)
-    lax.fori_loop(0, 2, partial, 0)
+    for i in range(2):
+        partial(i, 0)
     g01, g11 = lax.fori_loop(1, depth - 1, first, (zero,) * 2)
-    lax.fori_loop(0, 2, partial_second, 0)
+    for i in range(2):
+        partial_second(i, 0)
     g02, g12, g22 = lax.fori_loop(2, depth - 2, second, (zero,) * 3)
-    lax.fori_loop(0, 2, partial_third, 0)
+    for i in range(2):
+        partial_third(i, 0)
     g03, g13, g23 = lax.fori_loop(3, depth - 3, third, (zero,) * 3)
     for g, value in enumerate((g00, g01, g02, g03, g11, g12, g13, g22, g23)):
         gram[g] = value

time: 28.1 us -> 28.1 us (level)
  transfers between devices with their start and end apart: 5 -> 5, of which waited for: 3 -> 4; matrix products, arithmetic and copies ran while one was open for 1% -> 1% of each run, Pallas kernels for 17% -> 16%
where the time goes in v8:
time: 28.1 us; the launch traced here: 27.8 us
  starting transfers between devices  13.1 us (47%)
  Pallas kernels  8.51 us (30%)
  waiting for transfers between devices  5.25 us (19%)
  between operations  0.72 us (3%)
    ppermute x1, starting transfers between devices, on_device(): halo_b = lax.ppermute(send_b, 'in', swaps(0))  5.93 us
    all_to_all x1, starting transfers between devices, on_device(): messages = lax.all_to_all(message, ('sub', 'in'), 0, 0, tiled=True)  4.1 us
    pallas_call x1, Pallas kernels, on_device(): pl.pallas_call(interior_kernel, out_shape=(*fields, shape((kinds * comp *...  3.35 us
    all_to_all x1, waiting for transfers between devices, on_device(): messages = lax.all_to_all(message, ('sub', 'in'), 0, 0, tiled=True)  2.63 us
    ppermute x1, starting transfers between devices, on_device(): lax.ppermute(left, 'sub', [((i + 1) % n_sub, i) for i in range(n_sub)])  2.44 us
    pallas_call x1, Pallas kernels, on_device(): pl.pallas_call(functools.partial(far_kernel, kinds), out_shape=(*fields[:...  1.6 us
    pallas_call x1, Pallas kernels, on_device(): pl.pallas_call(functools.partial(final_kernel, kinds), out_shape=(shape(b...  1.31 us
    ppermute x1, waiting for transfers between devices, on_device(): halo_b = lax.ppermute(send_b, 'in', swaps(0))  1.3 us
  transfers between devices with their start and end apart: 5, of which 4 were waited for; matrix products, arithmetic and copies ran while one was open for 1% of the time, Pallas kernels for 16%

profile of v8, /device:TPU:0, one launch (start us, length us, event | category | flops | bytes accessed | tf_op | source)
XLA Modules:
  0.0 27.8 jit_solution(3837766560105355225)
XLA Ops:
  0.6 1.1 %pack.1 = (f32[14,32,128]{2,1,0:T(8,128)S(1)}, f32[14,32,128]{2,1,0:T(8,128)S(1)}) custom-call(f32[4,8,32,128]{3,2,1,0:T(8,128)} %body_hbm.1, s32[8,32,128]{2,1,0:T(8,128)} %mats_hbm.1), custom_call_target="tpu_custom_call" | custom-call | tf_op jit(solution)/shard_map/pack/pallas_call | solution.py:503
  1.7 0.7 %collective-permute-start.2 = (f32[14,32,128]{2,1,0:T(8,128)S(1)}, f32[14,32,128]{2,1,0:T(8,128)S(1)}, u32[]{:S(2)}, u32[]{:S(2)}) collective-permute-start(f32[14,32,128]{2,1,0:T(8,128)S(1)} %get-tuple-element.25.side_a), channel_id=1, source_target_pairs={{1,2},{2,1},{5,6},{6,5},{9,10},{10,9},{13,14},{14,13},{17,18},{18,... | collective-permute-start | bytes 688136 | tf_op jit(solution)/shard_map/ppermute | solution.py:520
  2.4 5.9 %collective-permute-start = (f32[14,32,128]{2,1,0:T(8,128)S(1)}, f32[14,32,128]{2,1,0:T(8,128)S(1)}, u32[]{:S(2)}, u32[]{:S(2)}) collective-permute-start(f32[14,32,128]{2,1,0:T(8,128)S(1)} %get-tuple-element.24.side_b), channel_id=1, source_target_pairs={{0,1},{2,3},{1,0},{3,2},{4,5},{6,7},{5,4},{7,6},{8,9},{10,11},{9,8... | collective-permute-start | bytes 688136 | tf_op jit(solution)/shard_map/ppermute | solution.py:521
  8.3 0.0 collective-permute-start.1
  8.3 3.3 %interior.1 = (f32[4,14,32,128]{3,2,1,0:T(8,128)S(1)}, f32[4,12,32,128]{3,2,1,0:T(8,128)S(1)}, f32[4,10,32,128]{3,2,1,0:T(8,128)S(1)}, f32[4,8,32,128]{3,2,1,0:T...) custom-call(f32[14,32,128]{2,1,0:T(8,128)S(1)} %get-tuple-element.25.side_a, ...), custom_call_target="tpu_custom_call" | custom-call | tf_op jit(solution)/shard_map/interior/pallas_call | solution.py:532
  11.7 0.0 collective-permute-done.2.halo
  11.7 0.6 %near.1 = (f32[4,14,32,128]{3,2,1,0:T(8,128)S(1)}, f32[4,12,32,128]{3,2,1,0:T(8,128)S(1)}, f32[4,10,32,128]{3,2,1,0:T(8,128)S(1)}, f32[4,8,32,128]{3,2,1,0:T(8,1...) custom-call(f32[14,32,128]{2,1,0:T(8,128)S(1)} %collective-permute-d, ...), custom_call_target="tpu_custom_call", output_to_operand_aliasing={{0}: (2, {}), {1}: (3, {}), {2}: (4, {}), {3}: (5, {}), {4}... | custom-call | tf_op jit(solution)/shard_map/near/pallas_call | solution.py:547
  12.3 0.1 collective-permute-done.1.before_hbm
  12.4 1.3 %collective-permute-done.halo = f32[14,32,128]{2,1,0:T(8,128)S(1)} collective-permute-done((f32[14,32,128]{2,1,0:T(8,128)S(1)}, f32[14,32,128]{2,1,0:T(8,128)S(1)}, u32[]{:S(2)}, u32[]{:S(2)}) %collective-permute-start) | collective-permute-done | bytes 229408 | tf_op jit(solution)/shard_map/ppermute | solution.py:521
  13.7 0.0 copy-start.1
  13.7 1.6 %far.1 = (f32[4,14,32,128]{3,2,1,0:T(8,128)S(1)}, f32[4,12,32,128]{3,2,1,0:T(8,128)S(1)}, f32[4,10,32,128]{3,2,1,0:T(8,128)S(1)}, f32[4,8,32,128]{3,2,1,0:T(8,12...) custom-call(f32[14,32,128]{2,1,0:T(8,128)S(1)} %collective-permute-d, ...), custom_call_target="tpu_custom_call", output_to_operand_aliasing={{0}: (4, {}), {1}: (5, {}), {2}: (6, {}), {3}: (7, {}), {4}... | custom-call | tf_op jit(solution)/shard_map/far/pallas_call | solution.py:557
  15.3 0.0 copy-start
  15.3 4.1 %all-to-all-start = ((f32[32,1,128]{2,1,0:T(1,128)}), f32[32,1,128]{2,1,0:T(1,128)S(1)}, u32[]{:S(2)}, u32[]{:S(2)}) async-start(f32[32,1,128]{2,1,0:T(1,128)} %bitcast.3), calls=%async_computation | async-start | bytes 32768 | tf_op jit(solution)/shard_map/all_to_all | solution.py:572
  19.4 0.6 %faces.1 = (f32[4,8,128]{2,1,0:T(8,128)S(1)}, f32[4,8,128]{2,1,0:T(8,128)S(1)}) custom-call(f32[4,14,32,128]{3,2,1,0:T(8,128)S(1)} %get-tuple-element.40.v0, f32[4,12,32,128]{3,2,1,0:T(8,128)S(1)} %get-tuple-element.41.v1, f32[4,10,32,128]{3,2,1,0:T(8,128)S(1)} %get-tuple-element.42.v2, f32[4,8,32,128]{3,2,1,0:T(8,128)S(1)} %get-tuple-element.43.v3), custom_call_target="tpu_custom_call" | custom-call | tf_op jit(solution)/shard_map/faces/pallas_call | solution.py:574
  20.0 2.4 %collective-permute-start.3 = (f32[4,8,128]{2,1,0:T(8,128)S(1)}, f32[4,8,128]{2,1,0:T(8,128)S(1)}, u32[]{:S(2)}, u32[]{:S(2)}) collective-permute-start(f32[4,8,128]{2,1,0:T(8,128)S(1)} %get-tuple-element.45), channel_id=1, source_target_pairs={{4,0},{8,4},{12,8},{16,12},{20,16},{24,20},{28,24},{0,28},{5,1},{9... | collective-permute-start | bytes 49160 | tf_op jit(solution)/shard_map/ppermute | solution.py:582
  22.4 0.0 copy-done.1
  22.4 0.2 reshape.16
  22.7 1.2 %collective-permute-done.3.left_next = f32[4,8,128]{2,1,0:T(8,128)S(1)} collective-permute-done((f32[4,8,128]{2,1,0:T(8,128)S(1)}, f32[4,8,128]{2,1,0:T(8,128)S(1)}, u32[]{:S(2)}, u32[]{:S(2)}) %collective-permute-start.3) | collective-permute-done | bytes 16416 | tf_op jit(solution)/shard_map/ppermute | solution.py:582
  23.9 2.6 %all-to-all-done = f32[32,1,128]{2,1,0:T(1,128)S(1)} async-done(((f32[32,1,128]{2,1,0:T(1,128)}), f32[32,1,128]{2,1,0:T(1,128)S(1)}, u32[]{:S(2)}, u32[]{:S(2)}) %all-to-all-start) | async-done | bytes 16416 | tf_op jit(solution)/shard_map/all_to_all | solution.py:572
  26.5 0.0 copy-done
  26.5 1.3 %final.1 = (f32[4,8,32,128]{3,2,1,0:T(8,128)}, f32[1,4,8,32]{3,2,1,0:T(8,128)}) custom-call(f32[32,128]{1,0:T(8,128)S(1)} %bitcast.12, f32[4,14,32,128]{3,2,1,0:T(8,128)S(1)} %get-tuple-element.40.v0, f32[4,12,32,128]{3,2,1,0:T(8,128)S(1)} %get-tuple-element.41.v1, f32[4,10,32,128]{3,2,1,0:T(8,128)S(1)} %get-tuple-element.42.v2, ...), custom_call_target="tpu_custom_call" | custom-call | tf_op jit(solution)/shard_map/final/pallas_call | solution.py:584
  (1 shorter events, 0.0 us)
Async XLA Ops:
  1.7 10.0 %collective-permute-start.2 = (f32[14,32,128]{2,1,0:T(8,128)S(1)}, f32[14,32,128]{2,1,0:T(8,128)S(1)}, u32[]{:S(2)}, u32[]{:S(2)}) collective-permute-start(f32[14,32,128]{2,1,0:T(8,128)S(1)} %get-tuple-element.25.side_a), channel_id=1, source_target_pairs={{1,2},{2,1},{5,6},{6,5},{9,10},{10,9},{13,14},{14,13},{17,18},{18,... | collective-permute-start | bytes 688136 | tf_op jit(solution)/shard_map/ppermute | solution.py:520
  2.4 11.3 %collective-permute-start = (f32[14,32,128]{2,1,0:T(8,128)S(1)}, f32[14,32,128]{2,1,0:T(8,128)S(1)}, u32[]{:S(2)}, u32[]{:S(2)}) collective-permute-start(f32[14,32,128]{2,1,0:T(8,128)S(1)} %get-tuple-element.24.side_b), channel_id=1, source_target_pairs={{0,1},{2,3},{1,0},{3,2},{4,5},{6,7},{5,4},{7,6},{8,9},{10,11},{9,8... | collective-permute-start | bytes 688136 | tf_op jit(solution)/shard_map/ppermute | solution.py:521
  8.3 4.0 %collective-permute-start.1 = (s32[8]{0:T(128)}, s32[8]{0:T(128)S(1)}, u32[]{:S(2)}, u32[]{:S(2)}) collective-permute-start(s32[8]{0:T(128)} %corners_hbm.1), channel_id=1, source_target_pairs={{0,4},{4,8},{8,12},{12,16},{16,20},{20,24},{24,28},{28,0},{1,5},{5... | collective-permute-start | bytes 104 | tf_op jit(solution)/shard_map/ppermute | solution.py:522
  13.7 8.8 %copy-start.1 = (f32[8,256]{1,0:T(8,128)S(1)}, f32[8,256]{1,0:T(8,128)}, u32[]{:S(2)}) copy-start(f32[8,256]{1,0:T(8,128)} %param.9) | copy-start | bytes 24580
  15.3 11.2 %copy-start = (s32[8]{0:T(128)S(1)}, s32[8]{0:T(128)}, u32[]{:S(2)}) copy-start(s32[8]{0:T(128)} %corners_hbm.1) | copy-start | bytes 100
  15.3 11.2 %all-to-all-start = ((f32[32,1,128]{2,1,0:T(1,128)}), f32[32,1,128]{2,1,0:T(1,128)S(1)}, u32[]{:S(2)}, u32[]{:S(2)}) async-start(f32[32,1,128]{2,1,0:T(1,128)} %bitcast.3), calls=%async_computation | async-start | bytes 32768 | tf_op jit(solution)/shard_map/all_to_all | solution.py:572
  20.0 3.9 %collective-permute-start.3 = (f32[4,8,128]{2,1,0:T(8,128)S(1)}, f32[4,8,128]{2,1,0:T(8,128)S(1)}, u32[]{:S(2)}, u32[]{:S(2)}) collective-permute-start(f32[4,8,128]{2,1,0:T(8,128)S(1)} %get-tuple-element.45), channel_id=1, source_target_pairs={{4,0},{8,4},{12,8},{16,12},{20,16},{24,20},{28,24},{0,28},{5,1},{9... | collective-permute-start | bytes 49160 | tf_op jit(solution)/shard_map/ppermute | solution.py:582
